TPU v7x, 32 devices: a whole 2x2x4 slice. The times are simulated.
32 devices in a mesh: pipe: 4 (over y, x), expert: 8 (over z, core).
Axes of the slice: x: 2, y: 2, z: 4, core: 2. Of those that a mesh axis runs over, the one named last changes fastest.
Arguments:
- tokens_in: bfloat16 [4, 2048, 2048], P('pipe', 'expert'), may hold values from -6 to 6
- out_grad: bfloat16 [4, 2048, 2048], P('pipe', 'expert'), may hold values from -6 to 6
- route_weight: float32 [4, 2048, 8], P('pipe', 'expert'), may hold values from 0.05 to 1
- expert_ids: int32 [4, 2048, 8], P('pipe', 'expert'), may hold values from 0 to 127, as said below
- slot_pos: int32 [4, 2048, 8], P('pipe', 'expert'), may hold values from 0 to 19, as said below
- dropped: int32 [4, 2048, 8], P('pipe', 'expert'), may hold values from 0 to 1, as said below
- gate_weight: bfloat16 [4, 8, 2048, 384], P('pipe', 'expert'), may hold values from -0.125 to 0.125
- up_weight: bfloat16 [4, 8, 2048, 384], P('pipe', 'expert'), may hold values from -0.125 to 0.125
- down_weight: bfloat16 [4, 8, 384, 2048], P('pipe', 'expert'), may hold values from -0.3125 to 0.3125
Outputs:
- upstream: bfloat16 [4, 2048, 2048], P('pipe', 'expert')
- grad_gate: bfloat16 [4, 8, 2048, 384], P('pipe', 'expert')
- grad_up: bfloat16 [4, 8, 2048, 384], P('pipe', 'expert')
- grad_down: bfloat16 [4, 8, 384, 2048], P('pipe', 'expert')
Inputs may be any that keep to these rules, and one draw needn't show every extreme that they name: `expert_ids`: each token names 8 different experts. A route's slot_pos counts the earlier routes (by token, then rank) to the same expert among the 256 tokens of its source block, capped at 19; in every layer some expert of the window gets 20 or more routes from every block. dropped is 1 exactly where that count reaches 20.
All inputs are finite; a program needn't handle non-finite values.
Results may differ from a plain program's by a relative error of at most 0.0058.
Values may be sent and summed in bfloat16 or wider, within the bound.
No kernel may reach another device: no remote copies, remote signals or barrier semaphores. Data moves between devices by JAX's collectives and lax.ppermute only.
A program may use at most 64 MiB of HBM per device.

v0:
```python
import jax
import jax.numpy as jnp
from jax import lax
from jax.sharding import PartitionSpec as P

CAP = 20


def from_behind(value, axis, by):
    length = lax.axis_size(axis)
    pairs = [(i, i + by) for i in range(length) if 0 <= i + by < length]
    return lax.ppermute(value, axis, pairs)


def expert_rows(expert_in, expert_grad, w_gate, w_up, w_down):
    gate_pre = jnp.dot(expert_in, w_gate, preferred_element_type=jnp.float32)
    up_pre = jnp.dot(expert_in, w_up, preferred_element_type=jnp.float32)
    sigma = jax.nn.sigmoid(gate_pre)
    active = gate_pre * sigma
    hidden = (active * up_pre).astype(jnp.bfloat16)
    hidden_grad = lax.dot_general(
        expert_grad, w_down, (((1,), (1,)), ((), ())), preferred_element_type=jnp.float32
    )
    gate_grad = (hidden_grad * up_pre * sigma * (1.0 + gate_pre * (1.0 - sigma))).astype(
        jnp.bfloat16
    )
    up_grad = (hidden_grad * active).astype(jnp.bfloat16)
    row_grad = lax.dot_general(
        gate_grad, w_gate, (((1,), (1,)), ((), ())), preferred_element_type=jnp.float32
    )
    row_grad = row_grad + lax.dot_general(
        up_grad, w_up, (((1,), (1,)), ((), ())), preferred_element_type=jnp.float32
    )
    return (row_grad.astype(jnp.bfloat16), hidden, gate_grad, up_grad)


def weight_grads(expert_in, expert_grad, hidden, gate_grad, up_grad):
    contract = (((0,), (0,)), ((), ()))
    grad_gate = lax.dot_general(
        expert_in, gate_grad, contract, preferred_element_type=jnp.float32
    ).astype(jnp.bfloat16)
    grad_up = lax.dot_general(
        expert_in, up_grad, contract, preferred_element_type=jnp.float32
    ).astype(jnp.bfloat16)
    grad_down = lax.dot_general(
        hidden, expert_grad, contract, preferred_element_type=jnp.float32
    ).astype(jnp.bfloat16)
    return (grad_gate, grad_up, grad_down)


def per_device(
    tokens_in,
    out_grad,
    route_weight,
    expert_ids,
    slot_pos,
    dropped,
    gate_weight,
    up_weight,
    down_weight,
):
    inputs = tokens_in[0]
    grads = out_grad[0]
    weights = route_weight[0]
    w_gate = gate_weight[0, 0]
    w_up = up_weight[0, 0]
    w_down = down_weight[0, 0]
    width = inputs.shape[1]
    n_expert = lax.axis_size("expert")
    rows = n_expert * CAP
    live = (expert_ids[0] < n_expert) & (dropped[0] == 0)
    target = jnp.where(live, expert_ids[0] * CAP + slot_pos[0], -1)
    placed = jnp.transpose(target)[:, None, :] == jnp.arange(rows)[None, :, None]
    picker = jnp.any(placed, axis=0).astype(jnp.bfloat16)
    slot_weight = jnp.sum(jnp.where(placed, jnp.transpose(weights)[:, None, :], 0.0), axis=(0, 2))
    send_in = jnp.dot(picker, inputs, preferred_element_type=jnp.float32).astype(jnp.bfloat16)
    grad_rows = jnp.dot(picker, grads, preferred_element_type=jnp.float32)
    send_grad = (slot_weight[:, None] * grad_rows).astype(jnp.bfloat16)
    send_in = send_in.reshape(n_expert, CAP, width)
    send_grad = send_grad.reshape(n_expert, CAP, width)
    got_in, got_grad = (
        lax.all_to_all(send_in, "expert", split_axis=0, concat_axis=0, tiled=True),
        lax.all_to_all(send_grad, "expert", split_axis=0, concat_axis=0, tiled=True),
    )
    flat_in = got_in.reshape(rows, width)
    flat_grad = got_grad.reshape(rows, width)
    row_grad, hidden, gate_grad, up_grad = expert_rows(flat_in, flat_grad, w_gate, w_up, w_down)
    returned = lax.all_to_all(
        row_grad.reshape(n_expert, CAP, width), "expert", split_axis=0, concat_axis=0, tiled=True
    )
    grad_gate, grad_up, grad_down = weight_grads(flat_in, flat_grad, hidden, gate_grad, up_grad)
    summed = lax.dot_general(
        picker,
        returned.reshape(rows, width),
        (((0,), (0,)), ((), ())),
        preferred_element_type=jnp.float32,
    )
    section_grad = (grads.astype(jnp.float32) + summed).astype(jnp.bfloat16)
    upstream = from_behind(section_grad, "pipe", -1)
    return (upstream[None], grad_gate[None, None], grad_up[None, None], grad_down[None, None])


def solution(mesh):
    return jax.shard_map(
        per_device,
        mesh=mesh,
        in_specs=(
            P("pipe", "expert", None),
            P("pipe", "expert", None),
            P("pipe", "expert", None),
            P("pipe", "expert", None),
            P("pipe", "expert", None),
            P("pipe", "expert", None),
            P("pipe", "expert", None, None),
            P("pipe", "expert", None, None),
            P("pipe", "expert", None, None),
        ),
        out_specs=(
            P("pipe", "expert", None),
            P("pipe", "expert", None, None),
            P("pipe", "expert", None, None),
            P("pipe", "expert", None, None),
        ),
        check_vma=False,
    )
```

profile of v0, /device:TPU:0, one launch (start us, length us, event | category | flops | bytes accessed | tf_op | source)
XLA Modules:
  0.0 122.6 jit_solution(16417157709058932164)
XLA Ops:
  0.6 0.9 select_bitcast_fusion
  1.7 1.6 %convolution_convert_fusion.3 = bf16[160,2048]{1,0:T(8,128)(2,1)S(1)} fusion(pred[160,256]{1,0:T(8,128)(4,1)S(1)} %fusion.15, bf16[1,256,2048]{2,1,0:T(8,128)(2,1)} %param.9), kind=kOutput, calls=%fused_computation.12 | convolution fusion | flops 168099840 | bytes 1744896 | tf_op jit(solution)/shard_map/dot_general | solution.py:76
  3.3 1.0 reshape.41
  4.3 6.3 %all-to-all-start.1 = ((bf16[8,20,2048]{2,1,0:T(8,128)(2,1)}), bf16[8,20,2048]{2,1,0:T(8,128)(2,1)}, u32[]{:S(2)}, u32[]{:S(2)}) async-start(bf16[8,20,2048]{2,1,0:T(8,128)(2,1)} %reshape.41), calls=%async_computation.1 | async-start | bytes 1572864 | tf_op jit(solution)/shard_map/all_to_all | solution.py:82
  11.2 1.0 reshape.39
  12.2 19.5 %all-to-all-done.1 = bf16[8,20,2048]{2,1,0:T(8,128)(2,1)} async-done(((bf16[8,20,2048]{2,1,0:T(8,128)(2,1)}), bf16[8,20,2048]{2,1,0:T(8,128)(2,1)}, u32[]{:S(2)}, u32[]{:S(2)}) %all-to-all-start.1) | async-done | bytes 655392 | tf_op jit(solution)/shard_map/all_to_all | solution.py:82
  31.7 4.2 %all-to-all-start = ((bf16[8,20,2048]{2,1,0:T(8,128)(2,1)}), bf16[8,20,2048]{2,1,0:T(8,128)(2,1)}, u32[]{:S(2)}, u32[]{:S(2)}) async-start(bf16[8,20,2048]{2,1,0:T(8,128)(2,1)} %reshape.39), calls=%async_computation | async-start | bytes 1572864 | tf_op jit(solution)/shard_map/all_to_all | solution.py:83
  35.9 1.3 %reshape.42 = bf16[160,2048]{1,0:T(8,128)(2,1)S(1)} reshape(bf16[8,20,2048]{2,1,0:T(8,128)(2,1)} %all-to-all-done.1) | data formatting | bytes 1310720 | tf_op jit(solution)/shard_map/reshape | solution.py:85
  37.7 0.9 copy-done.1
  38.6 1.2 %fusion.11 = f32[160,384]{1,0:T(8,128)} fusion(bf16[160,2048]{1,0:T(8,128)(2,1)S(1)} %reshape.42, bf16[1,1,2048,384]{3,2,1,0:T(8,128)(2,1)S(1)} %copy-done.1), kind=kOutput, calls=%fused_computation.18 | convolution fusion | flops 251658240 | bytes 2473984 | tf_op jit(solution)/shard_map/dot_general | solution.py:17
  39.8 17.1 %all-to-all-done = bf16[8,20,2048]{2,1,0:T(8,128)(2,1)} async-done(((bf16[8,20,2048]{2,1,0:T(8,128)(2,1)}), bf16[8,20,2048]{2,1,0:T(8,128)(2,1)}, u32[]{:S(2)}, u32[]{:S(2)}) %all-to-all-start) | async-done | bytes 655392 | tf_op jit(solution)/shard_map/all_to_all | solution.py:83
  56.9 2.0 %reshape.40 = bf16[160,2048]{1,0:T(8,128)(2,1)} reshape(bf16[8,20,2048]{2,1,0:T(8,128)(2,1)} %all-to-all-done) | data formatting | bytes 1310720 | tf_op jit(solution)/shard_map/reshape | solution.py:86
  58.9 2.3 %multiply_convert_fusion.1 = (bf16[160,384]{1,0:T(8,128)(2,1)S(1)}, bf16[160,384]{1,0:T(8,128)(2,1)S(1)}) fusion(f32[160,384]{1,0:T(8,128)S(1)} %fusion.8, f32[160,384]{1,0:T(8,128)} %fusion.11, bf16[160,2048]{1,0:T(8,128)(2,1)} %reshape.40, bf16[1,1,384,2048]{3,2,1,0:T(8,128)(2,1)} %param.17), kind=kOutput, calls=%fused_computation.28 | convolution fusion | flops 252456960 | bytes 2965504 | tf_op jit(solution)/shard_map/dot_general | solution.py:21
  62.7 1.5 %fusion.5 = bf16[160,2048]{1,0:T(8,128)(2,1)} fusion(f32[160,2048]{1,0:T(8,128)S(1)} %fusion.6, bf16[160,384]{1,0:T(8,128)(2,1)S(1)} %get-tuple-element.4, bf16[1,1,2048,384]{3,2,1,0:T(8,128)(2,1)S(1)} %copy-done.2), kind=kOutput, calls=%fused_computation.11 | convolution fusion | flops 252313600 | bytes 3661824 | tf_op jit(solution)/shard_map/dot_general | solution.py:31
  64.2 2.0 %reshape.43 = bf16[8,20,2048]{2,1,0:T(8,128)(2,1)} reshape(bf16[160,2048]{1,0:T(8,128)(2,1)} %fusion.5) | data formatting | bytes 1310720 | tf_op jit(solution)/shard_map/reshape | solution.py:89
  66.2 25.2 %all_to_all.15 = bf16[8,20,2048]{2,1,0:T(8,128)(2,1)} all-to-all(bf16[8,20,2048]{2,1,0:T(8,128)(2,1)} %reshape.43), channel_id=1, replica_groups=mesh['pipe'=4,'expert'=8] {'expert'}, dimensions={0} | all-to-all | bytes 1310720 | tf_op jit(solution)/shard_map/all_to_all | solution.py:88
  91.4 2.0 %reshape.44 = bf16[160,2048]{1,0:T(8,128)(2,1)} reshape(bf16[8,20,2048]{2,1,0:T(8,128)(2,1)} %all_to_all.15) | data formatting | bytes 1310720 | tf_op jit(solution)/shard_map/reshape | solution.py:94
  93.4 1.6 %fusion.3 = bf16[256,2048]{1,0:T(8,128)(2,1)S(1)} fusion(pred[160,256]{1,0:T(8,128)(4,1)} %copy-done.6, bf16[160,2048]{1,0:T(8,128)(2,1)} %reshape.44, bf16[1,256,2048]{2,1,0:T(8,128)(2,1)S(1)} %copy-done.3), kind=kOutput, calls=%fused_computation.7 | convolution fusion | flops 169345024 | bytes 2793472 | tf_op jit(solution)/shard_map/dot_general | solution.py:92
  95.0 1.4 %collective-permute-start = (bf16[256,2048]{1,0:T(8,128)(2,1)S(1)}, bf16[256,2048]{1,0:T(8,128)(2,1)S(1)}, u32[]{:S(2)}, u32[]{:S(2)}) collective-permute-start(bf16[256,2048]{1,0:T(8,128)(2,1)S(1)} %fusion.3), channel_id=1, source_target_pairs={{8,0},{16,8},{24,16},{9,1},{17,9},{25,17},{10,2},{18,10},{26,18},{... | collective-permute-start | bytes 3145736 | tf_op jit(solution)/shard_map/ppermute | solution.py:12
  96.5 1.9 %fusion.1 = bf16[1,1,2048,384]{3,2,1,0:T(8,128)(2,1)} fusion(bf16[160,2048]{1,0:T(8,128)(2,1)S(1)} %reshape.42, bf16[160,384]{1,0:T(8,128)(2,1)S(1)} %copy-done.10), kind=kOutput, calls=%fused_computation.5 | convolution fusion | flops 252444672 | bytes 2351104 | tf_op jit(solution)/shard_map/dot_general | solution.py:42
  98.4 1.9 %fusion = bf16[1,1,2048,384]{3,2,1,0:T(8,128)(2,1)} fusion(bf16[160,2048]{1,0:T(8,128)(2,1)S(1)} %reshape.42, bf16[160,384]{1,0:T(8,128)(2,1)S(1)} %copy-done.8), kind=kOutput, calls=%fused_computation.4 | convolution fusion | flops 252444672 | bytes 2351104 | tf_op jit(solution)/shard_map/dot_general | solution.py:39
  100.3 1.8 %fusion.2 = bf16[1,1,384,2048]{3,2,1,0:T(8,128)(2,1)} fusion(bf16[160,2048]{1,0:T(8,128)(2,1)S(1)} %copy-done.4, f32[160,384]{1,0:T(8,128)S(1)} %copy-done.5, f32[160,384]{1,0:T(8,128)S(1)} %fusion.8), kind=kOutput, calls=%fused_computation.6 | convolution fusion | flops 252813312 | bytes 2719744 | tf_op jit(solution)/shard_map/dot_general | solution.py:45
  102.0 19.6 %collective-permute-done = bf16[256,2048]{1,0:T(8,128)(2,1)S(1)} collective-permute-done((bf16[256,2048]{1,0:T(8,128)(2,1)S(1)}, bf16[256,2048]{1,0:T(8,128)(2,1)S(1)}, u32[]{:S(2)}, u32[]{:S(2)}) %collective-permute-start) | collective-permute-done | bytes 1048608 | tf_op jit(solution)/shard_map/ppermute | solution.py:12
  121.6 1.0 copy.14
  (28 shorter events, 2.8 us)
Async XLA Ops:
  0.6 36.6 %copy-start = (bf16[1,1,2048,384]{3,2,1,0:T(8,128)(2,1)S(1)}, bf16[1,1,2048,384]{3,2,1,0:T(8,128)(2,1)}, u32[]{:S(2)}) copy-start(bf16[1,1,2048,384]{3,2,1,0:T(8,128)(2,1)} %param.15) | copy-start | bytes 4718596
  1.7 9.2 %copy-start.6 = (pred[160,256]{1,0:T(8,128)(4,1)}, pred[160,256]{1,0:T(8,128)(4,1)S(1)}, u32[]{:S(2)}) copy-start(pred[160,256]{1,0:T(8,128)(4,1)S(1)} %fusion.15) | copy-start | bytes 122884
  3.3 7.4 %copy-start.11 = (f32[1,256,8]{1,2,0:T(8,128)S(1)}, f32[1,256,8]{1,2,0:T(8,128)}, u32[]{:S(2)}) copy-start(f32[1,256,8]{1,2,0:T(8,128)} %param.11) | copy-start | bytes 24580
  3.3 7.6 %copy-start.3 = (bf16[1,256,2048]{2,1,0:T(8,128)(2,1)S(1)}, bf16[1,256,2048]{2,1,0:T(8,128)(2,1)}, u32[]{:S(2)}) copy-start(bf16[1,256,2048]{2,1,0:T(8,128)(2,1)} %param.10) | copy-start | bytes 3145732
  4.3 27.4 %all-to-all-start.1 = ((bf16[8,20,2048]{2,1,0:T(8,128)(2,1)}), bf16[8,20,2048]{2,1,0:T(8,128)(2,1)}, u32[]{:S(2)}, u32[]{:S(2)}) async-start(bf16[8,20,2048]{2,1,0:T(8,128)(2,1)} %reshape.41), calls=%async_computation.1 | async-start | bytes 1572864 | tf_op jit(solution)/shard_map/all_to_all | solution.py:82
  31.7 25.2 %all-to-all-start = ((bf16[8,20,2048]{2,1,0:T(8,128)(2,1)}), bf16[8,20,2048]{2,1,0:T(8,128)(2,1)}, u32[]{:S(2)}, u32[]{:S(2)}) async-start(bf16[8,20,2048]{2,1,0:T(8,128)(2,1)} %reshape.39), calls=%async_computation | async-start | bytes 1572864 | tf_op jit(solution)/shard_map/all_to_all | solution.py:83
  37.2 1.4 %copy-start.1 = (bf16[1,1,2048,384]{3,2,1,0:T(8,128)(2,1)S(1)}, bf16[1,1,2048,384]{3,2,1,0:T(8,128)(2,1)}, u32[]{:S(2)}) copy-start(bf16[1,1,2048,384]{3,2,1,0:T(8,128)(2,1)} %param.16) | copy-start | bytes 4718596
  61.2 0.7 copy-start.7
  61.2 1.3 %copy-start.9 = (bf16[160,384]{1,0:T(8,128)(2,1)}, bf16[160,384]{1,0:T(8,128)(2,1)S(1)}, u32[]{:S(2)}) copy-start(bf16[160,384]{1,0:T(8,128)(2,1)S(1)} %get-tuple-element.4) | copy-start | bytes 368644
  61.2 1.5 %copy-start.2 = (bf16[1,1,2048,384]{3,2,1,0:T(8,128)(2,1)S(1)}, bf16[1,1,2048,384]{3,2,1,0:T(8,128)(2,1)}, u32[]{:S(2)}) copy-start(bf16[1,1,2048,384]{3,2,1,0:T(8,128)(2,1)} %param.16) | copy-start | bytes 4718596
  93.4 3.1 %copy-start.10 = (bf16[160,384]{1,0:T(8,128)(2,1)S(1)}, bf16[160,384]{1,0:T(8,128)(2,1)}, u32[]{:S(2)}) copy-start(bf16[160,384]{1,0:T(8,128)(2,1)} %copy-done.9) | copy-start | bytes 368644
  95.0 3.4 %copy-start.8 = (bf16[160,384]{1,0:T(8,128)(2,1)S(1)}, bf16[160,384]{1,0:T(8,128)(2,1)}, u32[]{:S(2)}) copy-start(bf16[160,384]{1,0:T(8,128)(2,1)} %copy-done.7) | copy-start | bytes 368644
  95.0 26.6 %collective-permute-start = (bf16[256,2048]{1,0:T(8,128)(2,1)S(1)}, bf16[256,2048]{1,0:T(8,128)(2,1)S(1)}, u32[]{:S(2)}, u32[]{:S(2)}) collective-permute-start(bf16[256,2048]{1,0:T(8,128)(2,1)S(1)} %fusion.3), channel_id=1, source_target_pairs={{8,0},{16,8},{24,16},{9,1},{17,9},{25,17},{10,2},{18,10},{26,18},{... | collective-permute-start | bytes 3145736 | tf_op jit(solution)/shard_map/ppermute | solution.py:12
  98.4 1.9 %copy-start.4 = (bf16[160,2048]{1,0:T(8,128)(2,1)S(1)}, bf16[160,2048]{1,0:T(8,128)(2,1)}, u32[]{:S(2)}) copy-start(bf16[160,2048]{1,0:T(8,128)(2,1)} %reshape.40) | copy-start | bytes 1966084
  98.4 1.9 %copy-start.5 = (f32[160,384]{1,0:T(8,128)S(1)}, f32[160,384]{1,0:T(8,128)}, u32[]{:S(2)}) copy-start(f32[160,384]{1,0:T(8,128)} %fusion.11) | copy-start | bytes 737284
where the time goes:
time: 123 us
  waiting for transfers between devices  56.1 us (46%)
  blocking collectives  25.2 us (20%)
  matrix products  15.3 us (12%)
  local copies, waits for them, and re-layouts  12 us (10%)
  starting transfers between devices  12 us (10%)
  other arithmetic  1.23 us (1%)
    all_to_all x1, blocking collectives, per_device(): lax.all_to_all(row_grad.reshape(n_expert, CAP, width), 'expert', split_ax...  25.2 us
    ppermute x1, waiting for transfers between devices, from_behind(): return lax.ppermute(value, axis, pairs)  19.6 us
    all_to_all x1, waiting for transfers between devices, per_device(): lax.all_to_all(send_in, 'expert', split_axis=0, concat_axis=0, tiled=True)  19.5 us
    all_to_all x1, waiting for transfers between devices, per_device(): lax.all_to_all(send_grad, 'expert', split_axis=0, concat_axis=0, tiled=True)  17.1 us
    all_to_all x1, starting transfers between devices, per_device(): lax.all_to_all(send_in, 'expert', split_axis=0, concat_axis=0, tiled=True)  6.32 us
    all_to_all x1, starting transfers between devices, per_device(): lax.all_to_all(send_grad, 'expert', split_axis=0, concat_axis=0, tiled=True)  4.21 us
    unnamed x25, local copies, waits for them, and re-layouts  2.74 us
  transfers between devices with their start and end apart: 3, of which 3 were waited for; matrix products, arithmetic and copies ran while one was open for 8% of the time, Pallas kernels for 0%

commit v1 on v0

v1 whole, which is shorter than its diff:
```python
import functools

import jax
import jax.numpy as jnp
from jax import lax
from jax.experimental import pallas as pl
from jax.experimental.pallas import tpu as pltpu
from jax.sharding import PartitionSpec as P

CAP = 20
PAIR = 2 * CAP
F32 = jnp.float32
BF16 = jnp.bfloat16


def vmem(count):
    return [pl.BlockSpec(memory_space=pltpu.VMEM)] * count


def is_first(shape):
    return lax.rem(lax.broadcasted_iota(jnp.int32, shape, 0), PAIR) < CAP


def match_rows(keys, first_row, rows):
    tokens = keys.shape[1]
    row = lax.broadcasted_iota(jnp.int32, (rows, tokens), 0)
    slot = first_row + row - jnp.where(lax.rem(row, PAIR) < CAP, 0, CAP)
    return [keys[k : k + 1, :] == slot for k in range(keys.shape[0])]


def gather_kernel(keys_ref, weight_ref, in_ref, grad_ref, *outs):
    keys = keys_ref[...]
    weight = weight_ref[...]
    rows = PAIR * len(outs)
    tokens = keys.shape[1]
    own = jnp.zeros((rows, tokens), F32)
    scaled = jnp.zeros((rows, tokens), F32)
    for k, hit in enumerate(match_rows(keys, 0, rows)):
        own = jnp.where(hit, 1.0, own)
        scaled = jnp.where(hit, weight[k : k + 1, :], scaled)
    first = is_first((rows, tokens))
    pick_in = jnp.where(first, own, 0.0).astype(BF16)
    pick_grad = jnp.where(first, 0.0, own).astype(BF16)
    row_weight = jnp.sum(scaled, axis=1, keepdims=True)
    got = jnp.dot(pick_in, in_ref[...], preferred_element_type=F32)
    got = got + row_weight * jnp.dot(pick_grad, grad_ref[...], preferred_element_type=F32)
    got = got.astype(BF16)
    for k, out in enumerate(outs):
        out[...] = got[k * PAIR : (k + 1) * PAIR, :]


def gather(keys, weight, inputs, grads, count):
    width = inputs.shape[1]
    return pl.pallas_call(
        gather_kernel,
        out_shape=[jax.ShapeDtypeStruct((PAIR, width), BF16)] * count,
        in_specs=vmem(4),
        out_specs=vmem(count),
        name="gather",
    )(keys, weight, inputs, grads)


def nt(a, b):
    return lax.dot_general(a, b, (((1,), (1,)), ((), ())), preferred_element_type=F32)


def tn(a, b):
    return lax.dot_general(a, b, (((0,), (0,)), ((), ())), preferred_element_type=F32)


def expert_kernel(count, *refs):
    payloads = refs[:count]
    w_gate, w_up, w_down = refs[count : count + 3]
    returns = refs[count + 3 : 2 * count + 3]
    gate_out, up_out, hidden_out = refs[2 * count + 3 :]
    rows = count * PAIR
    half = w_gate.shape[0] // 2
    both = jnp.concatenate([p[...] for p in payloads], axis=0)
    gate_pre = jnp.dot(both, w_gate[...], preferred_element_type=F32)
    up_pre = jnp.dot(both, w_up[...], preferred_element_type=F32)
    hidden_grad = pltpu.roll(nt(both, w_down[...]), rows - CAP, 0)
    first = is_first(gate_pre.shape)
    sigma = jax.nn.sigmoid(gate_pre)
    active = gate_pre * sigma
    hidden = jnp.where(first, active * up_pre, 0.0)
    gate_grad = hidden_grad * up_pre * sigma * (1.0 + gate_pre * (1.0 - sigma))
    gate_grad = jnp.where(first, gate_grad, 0.0)
    up_grad = jnp.where(first, hidden_grad * active, 0.0)
    gate_out[...] = gate_grad.astype(BF16)
    up_out[...] = up_grad.astype(BF16)
    hidden_out[...] = pltpu.roll(hidden, CAP, 0).astype(BF16)
    gate_two = (gate_grad + pltpu.roll(gate_grad, CAP, 0)).astype(BF16)
    up_two = (up_grad + pltpu.roll(up_grad, CAP, 0)).astype(BF16)
    left = nt(gate_two, w_gate[:half, :]) + nt(up_two, w_up[:half, :])
    right = nt(gate_two, w_gate[half:, :]) + nt(up_two, w_up[half:, :])
    row_grad = jnp.where(is_first(left.shape), left, right).astype(BF16)
    for k, out in enumerate(returns):
        out[...] = row_grad[k * PAIR : (k + 1) * PAIR, :]


def expert_chunk(payloads, w_gate, w_up, w_down):
    count = len(payloads)
    width, hidden = w_gate.shape
    out = pl.pallas_call(
        functools.partial(expert_kernel, count),
        out_shape=[jax.ShapeDtypeStruct((PAIR, width // 2), BF16)] * count
        + [jax.ShapeDtypeStruct((PAIR * count, hidden), BF16)] * 3,
        in_specs=vmem(count + 3),
        out_specs=vmem(count + 3),
        name="expert",
    )(*payloads, w_gate, w_up, w_down)
    return out[:count], out[count:]


def weight_kernel(count, chunks, *refs):
    payloads = refs[:count]
    small = refs[count : count + 3 * chunks]
    grad_gate, grad_up, grad_down = refs[count + 3 * chunks :]
    both = jnp.concatenate([p[...] for p in payloads], axis=0)
    gate = jnp.concatenate([r[...] for r in small[0::3]], axis=0)
    up = jnp.concatenate([r[...] for r in small[1::3]], axis=0)
    hidden = jnp.concatenate([r[...] for r in small[2::3]], axis=0)
    grad_gate[...] = tn(both, gate).astype(BF16)
    grad_up[...] = tn(both, up).astype(BF16)
    grad_down[...] = tn(hidden, both).astype(BF16)


def weight_grads(payloads, small, width, hidden):
    count = len(payloads)
    chunks = len(small)
    flat = [a for part in small for a in part]
    return pl.pallas_call(
        functools.partial(weight_kernel, count, chunks),
        out_shape=[
            jax.ShapeDtypeStruct((width, hidden), BF16),
            jax.ShapeDtypeStruct((width, hidden), BF16),
            jax.ShapeDtypeStruct((hidden, width), BF16),
        ],
        in_specs=vmem(count + 3 * chunks),
        out_specs=vmem(3),
        name="weight_grads",
    )(*payloads, *flat)


def combine_kernel(keys_ref, grad_ref, *refs):
    returned, out = refs[:-1], refs[-1]
    keys = keys_ref[...]
    rows = PAIR * len(returned)
    tokens = keys.shape[1]
    half = grad_ref.shape[1] // 2
    own = jnp.zeros((rows, tokens), F32)
    for hit in match_rows(keys, 0, rows):
        own = jnp.where(hit, 1.0, own)
    first = is_first((rows, tokens))
    back = jnp.concatenate([r[...] for r in returned], axis=0)
    for side in range(2):
        pick = jnp.where(first, own, 0.0) if side == 0 else jnp.where(first, 0.0, own)
        cols = slice(side * half, (side + 1) * half)
        total = grad_ref[:, cols].astype(F32) + tn(pick.astype(BF16), back)
        out[:, cols] = total.astype(BF16)


def combine(keys, grads, returned):
    return pl.pallas_call(
        combine_kernel,
        out_shape=jax.ShapeDtypeStruct(grads.shape, BF16),
        in_specs=vmem(2 + len(returned)),
        out_specs=pl.BlockSpec(memory_space=pltpu.VMEM),
        name="combine",
    )(keys, grads, *returned)


def per_device(
    tokens_in,
    out_grad,
    route_weight,
    expert_ids,
    slot_pos,
    dropped,
    gate_weight,
    up_weight,
    down_weight,
):
    inputs = tokens_in[0]
    grads = out_grad[0]
    w_gate = gate_weight[0, 0]
    w_up = up_weight[0, 0]
    w_down = down_weight[0, 0]
    width, hidden = w_gate.shape
    n_expert = lax.axis_size("expert")
    n_pipe = lax.axis_size("pipe")
    me = lax.axis_index("expert")
    both_axes = ("pipe", "expert")

    def to_partner(value, k):
        return lax.ppermute(value, "expert", [(i, i ^ k) for i in range(n_expert)])

    def to_before(value, k):
        pairs = [
            (p * n_expert + i, (p - 1) * n_expert + (i ^ k))
            for p in range(1, n_pipe)
            for i in range(n_expert)
        ]
        return lax.ppermute(value, both_axes, pairs)

    live = (expert_ids[0] < n_expert) & (dropped[0] == 0)
    key = jnp.where(live, (expert_ids[0] ^ me) * PAIR + slot_pos[0], -1)
    keys = jnp.transpose(key)
    weight = jnp.transpose(route_weight[0])
    sent = gather(keys, weight, inputs, grads, n_expert)

    near = list(range(n_expert // 2))
    far_a = list(range(n_expert // 2, 3 * n_expert // 4))
    far_b = list(range(3 * n_expert // 4, n_expert))
    got = {}
    for k in far_a + far_b + near[::-1]:
        got[k] = to_partner(sent[k], k) if k else sent[k]
    next_grads = to_before(grads, 0)
    next_keys = to_before(keys, 0)

    returned = {}
    order, small = [], []
    for chunk in (far_a, near, far_b):
        back, parts = expert_chunk([got[k] for k in chunk], w_gate, w_up, w_down)
        for k, value in zip(chunk, back):
            returned[k] = to_before(value, k)
        order += chunk
        small.append(parts)
    grad_gate, grad_up, grad_down = weight_grads([got[k] for k in order], small, width, hidden)
    upstream = combine(next_keys, next_grads, [returned[k] for k in range(n_expert)])
    return (upstream[None], grad_gate[None, None], grad_up[None, None], grad_down[None, None])


def solution(mesh):
    return jax.shard_map(
        per_device,
        mesh=mesh,
        in_specs=(
            P("pipe", "expert", None),
            P("pipe", "expert", None),
            P("pipe", "expert", None),
            P("pipe", "expert", None),
            P("pipe", "expert", None),
            P("pipe", "expert", None),
            P("pipe", "expert", None, None),
            P("pipe", "expert", None, None),
            P("pipe", "expert", None, None),
        ),
        out_specs=(
            P("pipe", "expert", None),
            P("pipe", "expert", None, None),
            P("pipe", "expert", None, None),
            P("pipe", "expert", None, None),
        ),
        check_vma=False,
    )
```

time: 123 us -> 100 us (0.81)
  the two profiles are of different devices: /device:TPU:0 before, /device:TPU:13 now
where the time goes in v1:
time: 100 us; the launch traced here: 99.5 us
  starting transfers between devices  37.9 us (38%)
  Pallas kernels  29.4 us (29%)
  waiting for transfers between devices  28.3 us (28%)
  local copies, waits for them, and re-layouts  1.63 us (2%)
  other arithmetic  1.33 us (1%)
    ppermute x10, starting transfers between devices, to_before(): return lax.ppermute(value, both_axes, pairs)  29.4 us
    ppermute x10, waiting for transfers between devices, to_before(): return lax.ppermute(value, both_axes, pairs)  18.7 us
    pallas_call x3, Pallas kernels, expert_chunk(): pl.pallas_call(functools.partial(expert_kernel, count), out_shape=[jax.Sh...  16.8 us
    ppermute x7, waiting for transfers between devices, to_partner(): return lax.ppermute(value, 'expert', [(i, i ^ k) for i in range(n_expert)])  9.6 us
    ppermute x7, starting transfers between devices, to_partner(): return lax.ppermute(value, 'expert', [(i, i ^ k) for i in range(n_expert)])  8.48 us
    pallas_call x1, Pallas kernels, weight_grads(): pl.pallas_call(functools.partial(weight_kernel, count, chunks), out_shape...  5.66 us
    pallas_call x1, Pallas kernels, gather(): pl.pallas_call(gather_kernel, out_shape=[jax.ShapeDtypeStruct((PAIR, widt...  3.71 us
    pallas_call x1, Pallas kernels, combine(): pl.pallas_call(combine_kernel, out_shape=jax.ShapeDtypeStruct(grads.shape...  3.29 us
  transfers between devices with their start and end apart: 17, of which 5 were waited for; matrix products, arithmetic and copies ran while one was open for 1% of the time, Pallas kernels for 26%

profile of v1, /device:TPU:13, one launch (start us, length us, event | category | flops | bytes accessed | tf_op | source)
XLA Modules:
  0.0 99.5 jit_solution(8958372921958608407)
XLA Ops:
  0.6 3.1 %collective-permute-start.1 = (bf16[256,2048]{1,0:T(8,128)(2,1)}, bf16[256,2048]{1,0:T(8,128)(2,1)S(1)}, u32[]{:S(2)}, u32[]{:S(2)}) collective-permute-start(bf16[256,2048]{1,0:T(8,128)(2,1)} %bitcast.26), channel_id=1, source_target_pairs={{8,0},{9,1},{10,2},{11,3},{12,4},{13,5},{14,6},{15,7},{16,8},{17,9... | collective-permute-start | bytes 3145736 | tf_op jit(solution)/shard_map/ppermute | solution.py:204
  3.7 1.3 %select_bitcast_fusion.keys_ref = s32[8,256]{1,0:T(8,128)} fusion(s32[1,256,8]{1,2,0:T(8,128)} %param.13, s32[1,256,8]{1,2,0:T(8,128)} %param.12, s32[1,256,8]{1,2,0:T(8,128)} %param.14, s32[]{:T(128)S(6)} %axis_index.12), kind=kLoop, calls=%fused_computation | loop fusion | flops 14336 | bytes 32772 | tf_op jit(solution)/shard_map/transpose | solution.py:208
  5.0 3.7 %gather.1 = (bf16[40,2048]{1,0:T(8,128)(2,1)}, bf16[40,2048]{1,0:T(8,128)(2,1)}, bf16[40,2048]{1,0:T(8,128)(2,1)}, bf16[40,2048]{1,0:T(8,128)(2,1)}, bf16[40,204...) custom-call(s32[8,256]{1,0:T(8,128)} %select_bitcast_fusion.keys_ref, ...), custom_call_target="tpu_custom_call" | custom-call | tf_op jit(solution)/shard_map/gather/pallas_call | solution.py:54
  9.9 1.5 %collective-permute-start.4 = (bf16[40,2048]{1,0:T(8,128)(2,1)}, bf16[40,2048]{1,0:T(8,128)(2,1)S(1)}, u32[]{:S(2)}, u32[]{:S(2)}) collective-permute-start(bf16[40,2048]{1,0:T(8,128)(2,1)} %get-tuple-element.35), channel_id=1, source_target_pairs={{0,3},{1,2},{2,1},{3,0},{4,7},{5,6},{6,5},{7,4},{8,11},{9,10},{10,... | collective-permute-start | bytes 491528 | tf_op jit(solution)/shard_map/ppermute | solution.py:196
  11.4 2.2 %collective-permute-start = (s32[8,256]{1,0:T(8,128)S(1)}, s32[8,256]{1,0:T(8,128)S(1)}, u32[]{:S(2)}, u32[]{:S(2)}) collective-permute-start(s32[8,256]{1,0:T(8,128)S(1)} %copy-done.16), channel_id=1, source_target_pairs={{8,0},{9,1},{10,2},{11,3},{12,4},{13,5},{14,6},{15,7},{16,8},{17,9... | collective-permute-start | bytes 24584 | tf_op jit(solution)/shard_map/ppermute | solution.py:204
  13.5 13.4 %collective-permute-done.keys_ref = s32[8,256]{1,0:T(8,128)S(1)} collective-permute-done((s32[8,256]{1,0:T(8,128)S(1)}, s32[8,256]{1,0:T(8,128)S(1)}, u32[]{:S(2)}, u32[]{:S(2)}) %collective-permute-start) | collective-permute-done | bytes 8224 | tf_op jit(solution)/shard_map/ppermute | solution.py:204
  26.9 3.7 %collective-permute-start.10 = (bf16[40,2048]{1,0:T(8,128)(2,1)}, bf16[40,2048]{1,0:T(8,128)(2,1)S(1)}, u32[]{:S(2)}, u32[]{:S(2)}) collective-permute-start(bf16[40,2048]{1,0:T(8,128)(2,1)} %get-tuple-element.41), channel_id=1, source_target_pairs={{0,5},{1,4},{2,7},{3,6},{4,1},{5,0},{6,3},{7,2},{8,13},{9,12},{10,... | collective-permute-start | bytes 491528 | tf_op jit(solution)/shard_map/ppermute | solution.py:196
  30.8 1.3 %collective-permute-start.13 = (bf16[40,2048]{1,0:T(8,128)(2,1)}, bf16[40,2048]{1,0:T(8,128)(2,1)S(1)}, u32[]{:S(2)}, u32[]{:S(2)}) collective-permute-start(bf16[40,2048]{1,0:T(8,128)(2,1)} %get-tuple-element.44), channel_id=1, source_target_pairs={{0,6},{1,7},{2,4},{3,5},{4,2},{5,3},{6,0},{7,1},{8,14},{9,15},{10,... | collective-permute-start | bytes 491528 | tf_op jit(solution)/shard_map/ppermute | solution.py:196
  32.8 5.9 %expert.3 = (bf16[40,1024]{1,0:T(8,128)(2,1)}, bf16[40,1024]{1,0:T(8,128)(2,1)}, bf16[40,1024]{1,0:T(8,128)(2,1)}, bf16[40,1024]{1,0:T(8,128)(2,1)}, bf16[160,38...) custom-call(bf16[40,2048]{1,0:T(8,128)(2,1)} %get-tuple-element.32.refs_0_.refs_2_, ...), custom_call_target="tpu_custom_call" | custom-call | tf_op jit(solution)/shard_map/expert/pallas_call | solution.py:104
  38.8 9.4 %collective-permute-done.10.refs_1_ = bf16[40,2048]{1,0:T(8,128)(2,1)S(1)} collective-permute-done((bf16[40,2048]{1,0:T(8,128)(2,1)}, bf16[40,2048]{1,0:T(8,128)(2,1)S(1)}, u32[]{:S(2)}, u32[]{:S(2)}) %collective-permute-start.10) | collective-permute-done | bytes 163872 | tf_op jit(solution)/shard_map/ppermute | solution.py:196
  48.2 3.9 %collective-permute-start.5 = (bf16[40,1024]{1,0:T(8,128)(2,1)}, bf16[40,1024]{1,0:T(8,128)(2,1)S(1)}, u32[]{:S(2)}, u32[]{:S(2)}) collective-permute-start(bf16[40,1024]{1,0:T(8,128)(2,1)} %get-tuple-element.36), channel_id=1, source_target_pairs={{8,0},{9,1},{10,2},{11,3},{12,4},{13,5},{14,6},{15,7},{16,8},{17,9... | collective-permute-start | bytes 245768 | tf_op jit(solution)/shard_map/ppermute | solution.py:204
  52.1 3.6 %collective-permute-start.6 = (bf16[40,1024]{1,0:T(8,128)(2,1)}, bf16[40,1024]{1,0:T(8,128)(2,1)S(1)}, u32[]{:S(2)}, u32[]{:S(2)}) collective-permute-start(bf16[40,1024]{1,0:T(8,128)(2,1)} %get-tuple-element.37), channel_id=1, source_target_pairs={{8,1},{9,0},{10,3},{11,2},{12,5},{13,4},{14,7},{15,6},{16,9},{17,8... | collective-permute-start | bytes 245768 | tf_op jit(solution)/shard_map/ppermute | solution.py:204
  55.8 3.1 %collective-permute-start.7 = (bf16[40,1024]{1,0:T(8,128)(2,1)}, bf16[40,1024]{1,0:T(8,128)(2,1)S(1)}, u32[]{:S(2)}, u32[]{:S(2)}) collective-permute-start(bf16[40,1024]{1,0:T(8,128)(2,1)} %get-tuple-element.38), channel_id=1, source_target_pairs={{8,2},{9,3},{10,0},{11,1},{12,6},{13,7},{14,4},{15,5},{16,10},{17,... | collective-permute-start | bytes 245768 | tf_op jit(solution)/shard_map/ppermute | solution.py:204
  59.0 3.6 %collective-permute-start.8 = (bf16[40,1024]{1,0:T(8,128)(2,1)}, bf16[40,1024]{1,0:T(8,128)(2,1)S(1)}, u32[]{:S(2)}, u32[]{:S(2)}) collective-permute-start(bf16[40,1024]{1,0:T(8,128)(2,1)} %get-tuple-element.39), channel_id=1, source_target_pairs={{8,3},{9,2},{10,1},{11,0},{12,7},{13,6},{14,5},{15,4},{16,11},{17,... | collective-permute-start | bytes 245768 | tf_op jit(solution)/shard_map/ppermute | solution.py:204
  62.7 5.4 %expert.4 = (bf16[40,1024]{1,0:T(8,128)(2,1)}, bf16[40,1024]{1,0:T(8,128)(2,1)}, bf16[80,384]{1,0:T(8,128)(2,1)}, bf16[80,384]{1,0:T(8,128)(2,1)}, bf16[80,384]{1,0:T(8,128)(2,1)}) custom-call(bf16[40,2048]{1,0:T(8,128)(2,1)} %copy-done.2, bf16[40,2048]{1,0:T(8,128)(2,1)} %copy-done.1, bf16[2048,384]{1,0:T(8,128)(2,1)} %bitcast.17, ...), custom_call_target="tpu_custom_call" | custom-call | tf_op jit(solution)/shard_map/expert/pallas_call | solution.py:104
  68.1 5.4 %expert.5 = (bf16[40,1024]{1,0:T(8,128)(2,1)}, bf16[40,1024]{1,0:T(8,128)(2,1)}, bf16[80,384]{1,0:T(8,128)(2,1)}, bf16[80,384]{1,0:T(8,128)(2,1)}, bf16[80,384]{1,0:T(8,128)(2,1)}) custom-call(bf16[40,2048]{1,0:T(8,128)(2,1)} %copy-done.3, bf16[40,2048]{1,0:T(8,128)(2,1)} %copy-done.4, bf16[2048,384]{1,0:T(8,128)(2,1)} %bitcast.18, ...), custom_call_target="tpu_custom_call" | custom-call | tf_op jit(solution)/shard_map/expert/pallas_call | solution.py:104
  73.5 4.2 %collective-permute-start.11 = (bf16[40,1024]{1,0:T(8,128)(2,1)S(1)}, bf16[40,1024]{1,0:T(8,128)(2,1)S(1)}, u32[]{:S(2)}, u32[]{:S(2)}) collective-permute-start(bf16[40,1024]{1,0:T(8,128)(2,1)S(1)} %copy-done.19), channel_id=1, source_target_pairs={{8,4},{9,5},{10,6},{11,7},{12,0},{13,1},{14,2},{15,3},{16,12},{17,... | collective-permute-start | bytes 245768 | tf_op jit(solution)/shard_map/ppermute | solution.py:204
  77.8 1.9 %collective-permute-start.12 = (bf16[40,1024]{1,0:T(8,128)(2,1)S(1)}, bf16[40,1024]{1,0:T(8,128)(2,1)S(1)}, u32[]{:S(2)}, u32[]{:S(2)}) collective-permute-start(bf16[40,1024]{1,0:T(8,128)(2,1)S(1)} %copy-done.18), channel_id=1, source_target_pairs={{8,5},{9,4},{10,7},{11,6},{12,1},{13,0},{14,3},{15,2},{16,13},{17,... | collective-permute-start | bytes 245768 | tf_op jit(solution)/shard_map/ppermute | solution.py:204
  79.7 1.9 %collective-permute-start.15 = (bf16[40,1024]{1,0:T(8,128)(2,1)}, bf16[40,1024]{1,0:T(8,128)(2,1)S(1)}, u32[]{:S(2)}, u32[]{:S(2)}) collective-permute-start(bf16[40,1024]{1,0:T(8,128)(2,1)} %get-tuple-element.46), channel_id=1, source_target_pairs={{8,6},{9,7},{10,4},{11,5},{12,2},{13,3},{14,0},{15,1},{16,14},{17,... | collective-permute-start | bytes 245768 | tf_op jit(solution)/shard_map/ppermute | solution.py:204
  81.7 1.9 %collective-permute-start.16 = (bf16[40,1024]{1,0:T(8,128)(2,1)}, bf16[40,1024]{1,0:T(8,128)(2,1)S(1)}, u32[]{:S(2)}, u32[]{:S(2)}) collective-permute-start(bf16[40,1024]{1,0:T(8,128)(2,1)} %get-tuple-element.47), channel_id=1, source_target_pairs={{8,7},{9,6},{10,5},{11,4},{12,3},{13,2},{14,1},{15,0},{16,15},{17,... | collective-permute-start | bytes 245768 | tf_op jit(solution)/shard_map/ppermute | solution.py:204
  83.6 5.7 %weight_grads.1 = (bf16[2048,384]{1,0:T(8,128)(2,1)}, bf16[2048,384]{1,0:T(8,128)(2,1)}, bf16[384,2048]{1,0:T(8,128)(2,1)}) custom-call(bf16[40,2048]{1,0:T(8,128)(2,1)} %copy-done.2, bf16[40,2048]{1,0:T(8,128)(2,1)} %copy-done.1, bf16[40,2048]{1,0:T(8,128)(2,1)} %get-tuple-element.32.refs_0_.refs_2_, bf16[40,2048]{1,0:T(8,128)(2,1)} %copy-done.5, ...), custom_call_target="tpu_custom_call" | custom-call | tf_op jit(solution)/shard_map/weight_grads/pallas_call | solution.py:132
  89.3 3.6 %collective-permute-done.15.refs_6_ = bf16[40,1024]{1,0:T(8,128)(2,1)S(1)} collective-permute-done((bf16[40,1024]{1,0:T(8,128)(2,1)}, bf16[40,1024]{1,0:T(8,128)(2,1)S(1)}, u32[]{:S(2)}, u32[]{:S(2)}) %collective-permute-start.15) | collective-permute-done | bytes 81952 | tf_op jit(solution)/shard_map/ppermute | solution.py:204
  92.9 1.8 %collective-permute-done.16.refs_7_ = bf16[40,1024]{1,0:T(8,128)(2,1)S(1)} collective-permute-done((bf16[40,1024]{1,0:T(8,128)(2,1)}, bf16[40,1024]{1,0:T(8,128)(2,1)S(1)}, u32[]{:S(2)}, u32[]{:S(2)}) %collective-permute-start.16) | collective-permute-done | bytes 81952 | tf_op jit(solution)/shard_map/ppermute | solution.py:204
  96.2 3.3 %combine.1 = bf16[256,2048]{1,0:T(8,128)(2,1)} custom-call(s32[8,256]{1,0:T(8,128)} %copy-done.17, bf16[256,2048]{1,0:T(8,128)(2,1)} %copy-done, bf16[40,1024]{1,0:T(8,128)(2,1)} %copy-done.8, bf16[40,1024]{1,0:T(8,128)(2,1)} %copy-done.9, bf16[40,1024]{1,0:T(8,128)(2,1)} %copy-done.10, bf16[40,1024]{1,0:T(8,128)(2,1)} %copy-done.11, ...), custom_call_target="tpu_custom_call" | custom-call | tf_op jit(solution)/shard_map/combine/pallas_call | solution.py:164
  (57 shorter events, 3.8 us)
Async XLA Ops:
  0.6 94.0 %collective-permute-start.1 = (bf16[256,2048]{1,0:T(8,128)(2,1)}, bf16[256,2048]{1,0:T(8,128)(2,1)S(1)}, u32[]{:S(2)}, u32[]{:S(2)}) collective-permute-start(bf16[256,2048]{1,0:T(8,128)(2,1)} %bitcast.26), channel_id=1, source_target_pairs={{8,0},{9,1},{10,2},{11,3},{12,4},{13,5},{14,6},{15,7},{16,8},{17,9... | collective-permute-start | bytes 3145736 | tf_op jit(solution)/shard_map/ppermute | solution.py:204
  8.7 21.9 %collective-permute-start.2 = (bf16[40,2048]{1,0:T(8,128)(2,1)}, bf16[40,2048]{1,0:T(8,128)(2,1)S(1)}, u32[]{:S(2)}, u32[]{:S(2)}) collective-permute-start(bf16[40,2048]{1,0:T(8,128)(2,1)} %get-tuple-element.33), channel_id=1, source_target_pairs={{0,1},{1,0},{2,3},{3,2},{4,5},{5,4},{6,7},{7,6},{8,9},{9,8},{10,11... | collective-permute-start | bytes 491528 | tf_op jit(solution)/shard_map/ppermute | solution.py:196
  9.7 21.0 %collective-permute-start.3 = (bf16[40,2048]{1,0:T(8,128)(2,1)}, bf16[40,2048]{1,0:T(8,128)(2,1)S(1)}, u32[]{:S(2)}, u32[]{:S(2)}) collective-permute-start(bf16[40,2048]{1,0:T(8,128)(2,1)} %get-tuple-element.34), channel_id=1, source_target_pairs={{0,2},{1,3},{2,0},{3,1},{4,6},{5,7},{6,4},{7,5},{8,10},{9,11},{10,... | collective-permute-start | bytes 491528 | tf_op jit(solution)/shard_map/ppermute | solution.py:196
  9.9 22.2 %collective-permute-start.4 = (bf16[40,2048]{1,0:T(8,128)(2,1)}, bf16[40,2048]{1,0:T(8,128)(2,1)S(1)}, u32[]{:S(2)}, u32[]{:S(2)}) collective-permute-start(bf16[40,2048]{1,0:T(8,128)(2,1)} %get-tuple-element.35), channel_id=1, source_target_pairs={{0,3},{1,2},{2,1},{3,0},{4,7},{5,6},{6,5},{7,4},{8,11},{9,10},{10,... | collective-permute-start | bytes 491528 | tf_op jit(solution)/shard_map/ppermute | solution.py:196
  11.4 15.6 %collective-permute-start = (s32[8,256]{1,0:T(8,128)S(1)}, s32[8,256]{1,0:T(8,128)S(1)}, u32[]{:S(2)}, u32[]{:S(2)}) collective-permute-start(s32[8,256]{1,0:T(8,128)S(1)} %copy-done.16), channel_id=1, source_target_pairs={{8,0},{9,1},{10,2},{11,3},{12,4},{13,5},{14,6},{15,7},{16,8},{17,9... | collective-permute-start | bytes 24584 | tf_op jit(solution)/shard_map/ppermute | solution.py:204
  26.9 11.8 %copy-start.17 = (s32[8,256]{1,0:T(8,128)}, s32[8,256]{1,0:T(8,128)S(1)}, u32[]{:S(2)}) copy-start(s32[8,256]{1,0:T(8,128)S(1)} %collective-permute-done.keys_ref) | copy-start | bytes 24580
  26.9 21.2 %collective-permute-start.10 = (bf16[40,2048]{1,0:T(8,128)(2,1)}, bf16[40,2048]{1,0:T(8,128)(2,1)S(1)}, u32[]{:S(2)}, u32[]{:S(2)}) collective-permute-start(bf16[40,2048]{1,0:T(8,128)(2,1)} %get-tuple-element.41), channel_id=1, source_target_pairs={{0,5},{1,4},{2,7},{3,6},{4,1},{5,0},{6,3},{7,2},{8,13},{9,12},{10,... | collective-permute-start | bytes 491528 | tf_op jit(solution)/shard_map/ppermute | solution.py:196
  30.7 21.4 %collective-permute-start.9 = (bf16[40,2048]{1,0:T(8,128)(2,1)}, bf16[40,2048]{1,0:T(8,128)(2,1)S(1)}, u32[]{:S(2)}, u32[]{:S(2)}) collective-permute-start(bf16[40,2048]{1,0:T(8,128)(2,1)} %get-tuple-element.40), channel_id=1, source_target_pairs={{0,4},{1,5},{2,6},{3,7},{4,0},{5,1},{6,2},{7,3},{8,12},{9,13},{10,... | collective-permute-start | bytes 491528 | tf_op jit(solution)/shard_map/ppermute | solution.py:196
  30.8 25.0 %collective-permute-start.13 = (bf16[40,2048]{1,0:T(8,128)(2,1)}, bf16[40,2048]{1,0:T(8,128)(2,1)S(1)}, u32[]{:S(2)}, u32[]{:S(2)}) collective-permute-start(bf16[40,2048]{1,0:T(8,128)(2,1)} %get-tuple-element.44), channel_id=1, source_target_pairs={{0,6},{1,7},{2,4},{3,5},{4,2},{5,3},{6,0},{7,1},{8,14},{9,15},{10,... | collective-permute-start | bytes 491528 | tf_op jit(solution)/shard_map/ppermute | solution.py:196
  32.1 27.0 %collective-permute-start.14 = (bf16[40,2048]{1,0:T(8,128)(2,1)}, bf16[40,2048]{1,0:T(8,128)(2,1)S(1)}, u32[]{:S(2)}, u32[]{:S(2)}) collective-permute-start(bf16[40,2048]{1,0:T(8,128)(2,1)} %get-tuple-element.45), channel_id=1, source_target_pairs={{0,7},{1,6},{2,5},{3,4},{4,3},{5,2},{6,1},{7,0},{8,15},{9,14},{10,... | collective-permute-start | bytes 491528 | tf_op jit(solution)/shard_map/ppermute | solution.py:196
  48.2 14.5 %copy-start.1 = (bf16[40,2048]{1,0:T(8,128)(2,1)}, bf16[40,2048]{1,0:T(8,128)(2,1)S(1)}, u32[]{:S(2)}) copy-start(bf16[40,2048]{1,0:T(8,128)(2,1)S(1)} %collective-permute-done.10.refs_1_) | copy-start | bytes 491524
  48.2 25.3 %collective-permute-start.5 = (bf16[40,1024]{1,0:T(8,128)(2,1)}, bf16[40,1024]{1,0:T(8,128)(2,1)S(1)}, u32[]{:S(2)}, u32[]{:S(2)}) collective-permute-start(bf16[40,1024]{1,0:T(8,128)(2,1)} %get-tuple-element.36), channel_id=1, source_target_pairs={{8,0},{9,1},{10,2},{11,3},{12,4},{13,5},{14,6},{15,7},{16,8},{17,9... | collective-permute-start | bytes 245768 | tf_op jit(solution)/shard_map/ppermute | solution.py:204
  52.1 25.6 %collective-permute-start.6 = (bf16[40,1024]{1,0:T(8,128)(2,1)}, bf16[40,1024]{1,0:T(8,128)(2,1)S(1)}, u32[]{:S(2)}, u32[]{:S(2)}) collective-permute-start(bf16[40,1024]{1,0:T(8,128)(2,1)} %get-tuple-element.37), channel_id=1, source_target_pairs={{8,1},{9,0},{10,3},{11,2},{12,5},{13,4},{14,7},{15,6},{16,9},{17,8... | collective-permute-start | bytes 245768 | tf_op jit(solution)/shard_map/ppermute | solution.py:204
  55.8 12.3 %copy-start.3 = (bf16[40,2048]{1,0:T(8,128)(2,1)}, bf16[40,2048]{1,0:T(8,128)(2,1)S(1)}, u32[]{:S(2)}) copy-start(bf16[40,2048]{1,0:T(8,128)(2,1)S(1)} %collective-permute-done.13.refs_0_.refs_6_) | copy-start | bytes 491524
  55.8 23.9 %collective-permute-start.7 = (bf16[40,1024]{1,0:T(8,128)(2,1)}, bf16[40,1024]{1,0:T(8,128)(2,1)S(1)}, u32[]{:S(2)}, u32[]{:S(2)}) collective-permute-start(bf16[40,1024]{1,0:T(8,128)(2,1)} %get-tuple-element.38), channel_id=1, source_target_pairs={{8,2},{9,3},{10,0},{11,1},{12,6},{13,7},{14,4},{15,5},{16,10},{17,... | collective-permute-start | bytes 245768 | tf_op jit(solution)/shard_map/ppermute | solution.py:204
  59.0 22.6 %collective-permute-start.8 = (bf16[40,1024]{1,0:T(8,128)(2,1)}, bf16[40,1024]{1,0:T(8,128)(2,1)S(1)}, u32[]{:S(2)}, u32[]{:S(2)}) collective-permute-start(bf16[40,1024]{1,0:T(8,128)(2,1)} %get-tuple-element.39), channel_id=1, source_target_pairs={{8,3},{9,2},{10,1},{11,0},{12,7},{13,6},{14,5},{15,4},{16,11},{17,... | collective-permute-start | bytes 245768 | tf_op jit(solution)/shard_map/ppermute | solution.py:204
  73.5 21.1 %copy-start.8 = (bf16[40,1024]{1,0:T(8,128)(2,1)}, bf16[40,1024]{1,0:T(8,128)(2,1)S(1)}, u32[]{:S(2)}) copy-start(bf16[40,1024]{1,0:T(8,128)(2,1)S(1)} %collective-permute-done.5.refs_0_) | copy-start | bytes 245764
  73.5 15.7 %collective-permute-start.11 = (bf16[40,1024]{1,0:T(8,128)(2,1)S(1)}, bf16[40,1024]{1,0:T(8,128)(2,1)S(1)}, u32[]{:S(2)}, u32[]{:S(2)}) collective-permute-start(bf16[40,1024]{1,0:T(8,128)(2,1)S(1)} %copy-done.19), channel_id=1, source_target_pairs={{8,4},{9,5},{10,6},{11,7},{12,0},{13,1},{14,2},{15,3},{16,12},{17,... | collective-permute-start | bytes 245768 | tf_op jit(solution)/shard_map/ppermute | solution.py:204
  77.8 16.9 %copy-start.9 = (bf16[40,1024]{1,0:T(8,128)(2,1)}, bf16[40,1024]{1,0:T(8,128)(2,1)S(1)}, u32[]{:S(2)}) copy-start(bf16[40,1024]{1,0:T(8,128)(2,1)S(1)} %collective-permute-done.6.refs_1_) | copy-start | bytes 245764
  77.8 11.5 %collective-permute-start.12 = (bf16[40,1024]{1,0:T(8,128)(2,1)S(1)}, bf16[40,1024]{1,0:T(8,128)(2,1)S(1)}, u32[]{:S(2)}, u32[]{:S(2)}) collective-permute-start(bf16[40,1024]{1,0:T(8,128)(2,1)S(1)} %copy-done.18), channel_id=1, source_target_pairs={{8,5},{9,4},{10,7},{11,6},{12,1},{13,0},{14,3},{15,2},{16,13},{17,... | collective-permute-start | bytes 245768 | tf_op jit(solution)/shard_map/ppermute | solution.py:204
  79.7 14.9 %copy-start.10 = (bf16[40,1024]{1,0:T(8,128)(2,1)}, bf16[40,1024]{1,0:T(8,128)(2,1)S(1)}, u32[]{:S(2)}) copy-start(bf16[40,1024]{1,0:T(8,128)(2,1)S(1)} %collective-permute-done.7.refs_2_) | copy-start | bytes 245764
  79.7 13.1 %collective-permute-start.15 = (bf16[40,1024]{1,0:T(8,128)(2,1)}, bf16[40,1024]{1,0:T(8,128)(2,1)S(1)}, u32[]{:S(2)}, u32[]{:S(2)}) collective-permute-start(bf16[40,1024]{1,0:T(8,128)(2,1)} %get-tuple-element.46), channel_id=1, source_target_pairs={{8,6},{9,7},{10,4},{11,5},{12,2},{13,3},{14,0},{15,1},{16,14},{17,... | collective-permute-start | bytes 245768 | tf_op jit(solution)/shard_map/ppermute | solution.py:204
  81.7 13.0 %copy-start.11 = (bf16[40,1024]{1,0:T(8,128)(2,1)}, bf16[40,1024]{1,0:T(8,128)(2,1)S(1)}, u32[]{:S(2)}) copy-start(bf16[40,1024]{1,0:T(8,128)(2,1)S(1)} %collective-permute-done.8.refs_3_) | copy-start | bytes 245764
  81.7 12.9 %collective-permute-start.16 = (bf16[40,1024]{1,0:T(8,128)(2,1)}, bf16[40,1024]{1,0:T(8,128)(2,1)S(1)}, u32[]{:S(2)}, u32[]{:S(2)}) collective-permute-start(bf16[40,1024]{1,0:T(8,128)(2,1)} %get-tuple-element.47), channel_id=1, source_target_pairs={{8,7},{9,6},{10,5},{11,4},{12,3},{13,2},{14,1},{15,0},{16,15},{17,... | collective-permute-start | bytes 245768 | tf_op jit(solution)/shard_map/ppermute | solution.py:204
  (13 other events, 60.2 us)

commit v2 on v1

--- a/solution.py
+++ b/solution.py
@@ -11,6 +11,7 @@
 PAIR = 2 * CAP
 F32 = jnp.float32
 BF16 = jnp.bfloat16
+SHORT = pl.CostEstimate(flops=1, transcendentals=0, bytes_accessed=1)
 
 
 def vmem(count):
@@ -31,7 +32,7 @@
 def gather_kernel(keys_ref, weight_ref, in_ref, grad_ref, *outs):
     keys = keys_ref[...]
     weight = weight_ref[...]
-    rows = PAIR * len(outs)
+    rows = sum(out.shape[0] for out in outs)
     tokens = keys.shape[1]
     own = jnp.zeros((rows, tokens), F32)
     scaled = jnp.zeros((rows, tokens), F32)
@@ -45,19 +46,26 @@
     got = jnp.dot(pick_in, in_ref[...], preferred_element_type=F32)
     got = got + row_weight * jnp.dot(pick_grad, grad_ref[...], preferred_element_type=F32)
     got = got.astype(BF16)
-    for k, out in enumerate(outs):
-        out[...] = got[k * PAIR : (k + 1) * PAIR, :]
-
-
-def gather(keys, weight, inputs, grads, count):
+    start = 0
+    for out in outs:
+        out[...] = got[start : start + out.shape[0], :]
+        start += out.shape[0]
+
+
+def gather(keys, weight, inputs, grads, chips, apart):
     width = inputs.shape[1]
-    return pl.pallas_call(
+    sizes = [n for c in range(chips) for n in ([PAIR, PAIR] if c in apart else [2 * PAIR])]
+    outs = pl.pallas_call(
         gather_kernel,
-        out_shape=[jax.ShapeDtypeStruct((PAIR, width), BF16)] * count,
+        out_shape=[jax.ShapeDtypeStruct((n, width), BF16) for n in sizes],
         in_specs=vmem(4),
-        out_specs=vmem(count),
+        out_specs=vmem(len(sizes)),
         name="gather",
+        compiler_params=pltpu.CompilerParams(vmem_limit_bytes=16 << 20),
+        cost_estimate=SHORT,
     )(keys, weight, inputs, grads)
+    outs = list(outs)
+    return [[outs.pop(0), outs.pop(0)] if c in apart else outs.pop(0) for c in range(chips)]
 
 
 def nt(a, b):
@@ -68,14 +76,26 @@
     return lax.dot_general(a, b, (((0,), (0,)), ((), ())), preferred_element_type=F32)
 
 
-def expert_kernel(count, *refs):
+def joined(pieces):
+    return jnp.concatenate(
+        [
+            p[PAIR : 2 * PAIR, :] if i % 2 and p.shape[0] > PAIR else p[:PAIR, :]
+            for i, p in enumerate(pieces)
+        ],
+        axis=0,
+    )
+
+
+def expert_kernel(count, with_keys, *refs):
+    if with_keys:
+        keys_ref, refs = refs[0], refs[1:]
     payloads = refs[:count]
     w_gate, w_up, w_down = refs[count : count + 3]
-    returns = refs[count + 3 : 2 * count + 3]
-    gate_out, up_out, hidden_out = refs[2 * count + 3 :]
+    returns = refs[count + 3 : -3]
+    gate_out, up_out, hidden_out = refs[-3:]
     rows = count * PAIR
     half = w_gate.shape[0] // 2
-    both = jnp.concatenate([p[...] for p in payloads], axis=0)
+    both = joined(payloads)
     gate_pre = jnp.dot(both, w_gate[...], preferred_element_type=F32)
     up_pre = jnp.dot(both, w_up[...], preferred_element_type=F32)
     hidden_grad = pltpu.roll(nt(both, w_down[...]), rows - CAP, 0)
@@ -94,29 +114,43 @@
     left = nt(gate_two, w_gate[:half, :]) + nt(up_two, w_up[:half, :])
     right = nt(gate_two, w_gate[half:, :]) + nt(up_two, w_up[half:, :])
     row_grad = jnp.where(is_first(left.shape), left, right).astype(BF16)
+    step = rows // len(returns)
     for k, out in enumerate(returns):
-        out[...] = row_grad[k * PAIR : (k + 1) * PAIR, :]
-
-
-def expert_chunk(payloads, w_gate, w_up, w_down):
-    count = len(payloads)
+        out[:step, :] = row_grad[k * step : (k + 1) * step, :]
+    if with_keys:
+        ranks, tokens = keys_ref.shape
+        keys = keys_ref[...].astype(F32)
+        block = jnp.floor((keys + 0.5) / PAIR)
+        returns[0][2 * PAIR :, :tokens] = block.astype(BF16)
+        returns[0][2 * PAIR :, tokens : 2 * tokens] = (keys - PAIR * block).astype(BF16)
+        returns[0][2 * PAIR :, 2 * tokens :] = jnp.zeros((ranks, half - 2 * tokens), BF16)
+
+
+def expert_chunk(pieces, w_gate, w_up, w_down, keys=None, single=False):
+    count = len(pieces)
     width, hidden = w_gate.shape
+    extra = [] if keys is None else [keys]
+    rows = [PAIR] * count if single else [2 * PAIR] * (count // 2)
+    if extra:
+        rows[0] += keys.shape[0]
     out = pl.pallas_call(
-        functools.partial(expert_kernel, count),
-        out_shape=[jax.ShapeDtypeStruct((PAIR, width // 2), BF16)] * count
+        functools.partial(expert_kernel, count, bool(extra)),
+        out_shape=[jax.ShapeDtypeStruct((r, width // 2), BF16) for r in rows]
         + [jax.ShapeDtypeStruct((PAIR * count, hidden), BF16)] * 3,
-        in_specs=vmem(count + 3),
-        out_specs=vmem(count + 3),
+        in_specs=vmem(len(extra) + count + 3),
+        out_specs=vmem(len(rows) + 3),
         name="expert",
-    )(*payloads, w_gate, w_up, w_down)
-    return out[:count], out[count:]
+        compiler_params=pltpu.CompilerParams(vmem_limit_bytes=20 << 20),
+        cost_estimate=SHORT,
+    )(*extra, *pieces, w_gate, w_up, w_down)
+    return out[: len(rows)], out[len(rows) :]
 
 
 def weight_kernel(count, chunks, *refs):
     payloads = refs[:count]
     small = refs[count : count + 3 * chunks]
     grad_gate, grad_up, grad_down = refs[count + 3 * chunks :]
-    both = jnp.concatenate([p[...] for p in payloads], axis=0)
+    both = joined(payloads)
     gate = jnp.concatenate([r[...] for r in small[0::3]], axis=0)
     up = jnp.concatenate([r[...] for r in small[1::3]], axis=0)
     hidden = jnp.concatenate([r[...] for r in small[2::3]], axis=0)
@@ -139,20 +173,24 @@
         in_specs=vmem(count + 3 * chunks),
         out_specs=vmem(3),
         name="weight_grads",
+        compiler_params=pltpu.CompilerParams(vmem_limit_bytes=24 << 20),
+        cost_estimate=SHORT,
     )(*payloads, *flat)
 
 
-def combine_kernel(keys_ref, grad_ref, *refs):
+def combine_kernel(ranks, grad_ref, *refs):
     returned, out = refs[:-1], refs[-1]
-    keys = keys_ref[...]
     rows = PAIR * len(returned)
-    tokens = keys.shape[1]
+    tokens = grad_ref.shape[0]
+    block = returned[0][2 * PAIR : 2 * PAIR + ranks, :tokens].astype(F32)
+    slot = returned[0][2 * PAIR : 2 * PAIR + ranks, tokens : 2 * tokens].astype(F32)
+    keys = (PAIR * block + slot).astype(jnp.int32)
     half = grad_ref.shape[1] // 2
     own = jnp.zeros((rows, tokens), F32)
     for hit in match_rows(keys, 0, rows):
         own = jnp.where(hit, 1.0, own)
     first = is_first((rows, tokens))
-    back = jnp.concatenate([r[...] for r in returned], axis=0)
+    back = joined(returned)
     for side in range(2):
         pick = jnp.where(first, own, 0.0) if side == 0 else jnp.where(first, 0.0, own)
         cols = slice(side * half, (side + 1) * half)
@@ -160,14 +198,16 @@
         out[:, cols] = total.astype(BF16)
 
 
-def combine(keys, grads, returned):
+def combine(ranks, grads, returned):
     return pl.pallas_call(
-        combine_kernel,
+        functools.partial(combine_kernel, ranks),
         out_shape=jax.ShapeDtypeStruct(grads.shape, BF16),
-        in_specs=vmem(2 + len(returned)),
+        in_specs=vmem(1 + len(returned)),
         out_specs=pl.BlockSpec(memory_space=pltpu.VMEM),
         name="combine",
-    )(keys, grads, *returned)
+        compiler_params=pltpu.CompilerParams(vmem_limit_bytes=16 << 20),
+        cost_estimate=SHORT,
+    )(grads, *returned)
 
 
 def per_device(
@@ -207,27 +247,56 @@
     key = jnp.where(live, (expert_ids[0] ^ me) * PAIR + slot_pos[0], -1)
     keys = jnp.transpose(key)
     weight = jnp.transpose(route_weight[0])
-    sent = gather(keys, weight, inputs, grads, n_expert)
-
-    near = list(range(n_expert // 2))
-    far_a = list(range(n_expert // 2, 3 * n_expert // 4))
-    far_b = list(range(3 * n_expert // 4, n_expert))
-    got = {}
-    for k in far_a + far_b + near[::-1]:
-        got[k] = to_partner(sent[k], k) if k else sent[k]
-    next_grads = to_before(grads, 0)
-    next_keys = to_before(keys, 0)
-
-    returned = {}
-    order, small = [], []
-    for chunk in (far_a, near, far_b):
-        back, parts = expert_chunk([got[k] for k in chunk], w_gate, w_up, w_down)
-        for k, value in zip(chunk, back):
-            returned[k] = to_before(value, k)
-        order += chunk
+    chips = n_expert // 2
+    near = list(range(1, chips // 2))
+    early = list(range(chips // 2, 3 * chips // 4))
+    late = list(range(3 * chips // 4, chips))
+    sent = gather(keys, weight, inputs, grads, chips, [])
+    behind, _ = lax.optimization_barrier((grads, sent[0]))
+    next_grads = to_before(behind, 0)
+
+    got, small, order, arrived, returned = {}, [], [], {}, {}
+
+    def after(values, event):
+        return lax.optimization_barrier((values, event))[0]
+
+    def process(chunk, event=None, **options):
+        pieces = [piece for c in chunk for piece in got[c]]
+        if event is not None:
+            pieces = after(pieces, event)
+        back, parts = expert_chunk(pieces, w_gate, w_up, w_down, **options)
+        order.extend(pieces)
         small.append(parts)
-    grad_gate, grad_up, grad_down = weight_grads([got[k] for k in order], small, width, hidden)
-    upstream = combine(next_keys, next_grads, [returned[k] for k in range(n_expert)])
+        return back, parts
+
+    def forward(values, event):
+        values = after(values, event)
+        return [[value, to_partner(value, 1)] for value in values]
+
+    for c in early + near:
+        arrived[c] = to_partner(sent[c], 2 * c)
+    got[0] = [sent[0], to_partner(sent[0], 1)]
+    back, own = process([0], keys=keys)
+    returned[0] = to_before(back[0], 0)
+    for c, value in zip(late, after([sent[c] for c in late], own)):
+        arrived[c] = to_partner(value, 2 * c)
+    got.update(zip(early + near, forward([arrived[c] for c in early + near], own)))
+    parts = own
+    for chunk in (early, near):
+        if chunk:
+            back, parts = process(chunk, parts)
+            for c, value in zip(chunk, back):
+                returned[c] = to_before(value, 2 * c)
+    got.update(zip(late, forward([arrived[c] for c in late], parts)))
+    back, parts = process(late, single=True)
+    for i, c in enumerate(late):
+        returned[c] = [to_before(back[2 * i + j], 2 * c + j) for j in range(2)]
+    grad_gate, grad_up, grad_down = weight_grads(order, small, width, hidden)
+    both = [0] + early + near
+    returned.update(zip(both, forward([returned[c] for c in both], grad_gate)))
+    upstream = combine(
+        keys.shape[0], next_grads, [piece for c in range(chips) for piece in returned[c]]
+    )
     return (upstream[None], grad_gate[None, None], grad_up[None, None], grad_down[None, None])
 
 

time: 100 us -> 76.8 us (0.77)
  the two profiles are of different devices: /device:TPU:13 before, /device:TPU:5 now
where the time goes in v2:
time: 76.8 us; the launch traced here: 76.4 us
  starting transfers between devices  32.5 us (42%)
  waiting for transfers between devices  20.2 us (26%)
  Pallas kernels  17.3 us (23%)
  local copies, waits for them, and re-layouts  4.74 us (6%)
  other arithmetic  0.85 us (1%)
  between operations  0.79 us (1%)
    ppermute x6, starting transfers between devices, to_before(): return lax.ppermute(value, both_axes, pairs)  21.2 us
    ppermute x6, waiting for transfers between devices, to_before(): return lax.ppermute(value, both_axes, pairs)  11.5 us
    ppermute x10, starting transfers between devices, to_partner(): return lax.ppermute(value, 'expert', [(i, i ^ k) for i in range(n_expert)])  11.3 us
    pallas_call x4, Pallas kernels, expert_chunk(): pl.pallas_call(functools.partial(expert_kernel, count, bool(extra)), out_...  8.93 us
    ppermute x10, waiting for transfers between devices, to_partner(): return lax.ppermute(value, 'expert', [(i, i ^ k) for i in range(n_expert)])  8.66 us
    unnamed x10, local copies, waits for them, and re-layouts  4.74 us
    pallas_call x1, Pallas kernels, weight_grads(): pl.pallas_call(functools.partial(weight_kernel, count, chunks), out_shape...  4.14 us
    pallas_call x1, Pallas kernels, gather(): pl.pallas_call(gather_kernel, out_shape=[jax.ShapeDtypeStruct((n, width),...  2.37 us
  transfers between devices with their start and end apart: 16, of which 5 were waited for; matrix products, arithmetic and copies ran while one was open for 0% of the time, Pallas kernels for 17%

profile of v2, /device:TPU:5, one launch (start us, length us, event | category | flops | bytes accessed | tf_op | source)
XLA Modules:
  0.0 76.4 jit_solution(15811995350362854396)
XLA Ops:
  3.4 2.4 %gather.1 = (bf16[80,2048]{1,0:T(8,128)(2,1)S(1)}, bf16[80,2048]{1,0:T(8,128)(2,1)S(1)}, bf16[80,2048]{1,0:T(8,128)(2,1)S(1)}, bf16[80,2048]{1,0:T(8,128)(2,1)S(1)}) custom-call(s32[8,256]{1,0:T(8,128)S(1)} %select_bitcast_fusion.keys_ref.refs_0_, f32[8,256]{1,0:T(8,128)S(1)} %bitcast.29, bf16[256,2048]{1,0:T(8,128)(2,1)S(1)} %bitcast.28, ...), custom_call_target="tpu_custom_call" | custom-call | flops 1 | bytes 1 | tf_op jit(solution)/shard_map/gather/pallas_call | solution.py:58
  6.5 2.3 %collective-permute-start.3 = (bf16[80,2048]{1,0:T(8,128)(2,1)S(1)}, bf16[80,2048]{1,0:T(8,128)(2,1)S(1)}, u32[]{:S(2)}, u32[]{:S(2)}) collective-permute-start(bf16[80,2048]{1,0:T(8,128)(2,1)S(1)} %get-tuple-element.43), channel_id=1, source_target_pairs={{0,4},{1,5},{2,6},{3,7},{4,0},{5,1},{6,2},{7,3},{8,12},{9,13},{10,... | collective-permute-start | bytes 983048 | tf_op jit(solution)/shard_map/ppermute | solution.py:236
  8.9 1.3 %collective-permute-start.4 = (bf16[80,2048]{1,0:T(8,128)(2,1)S(1)}, bf16[80,2048]{1,0:T(8,128)(2,1)S(1)}, u32[]{:S(2)}, u32[]{:S(2)}) collective-permute-start(bf16[80,2048]{1,0:T(8,128)(2,1)S(1)} %get-tuple-element.44), channel_id=1, source_target_pairs={{0,2},{1,3},{2,0},{3,1},{4,6},{5,7},{6,4},{7,5},{8,10},{9,11},{10,... | collective-permute-start | bytes 983048 | tf_op jit(solution)/shard_map/ppermute | solution.py:236
  10.2 3.1 %collective-permute-start = (bf16[256,2048]{1,0:T(8,128)(2,1)}, bf16[256,2048]{1,0:T(8,128)(2,1)S(1)}, u32[]{:S(2)}, u32[]{:S(2)}) collective-permute-start(bf16[256,2048]{1,0:T(8,128)(2,1)} %bitcast.grad_ref), channel_id=1, source_target_pairs={{8,0},{9,1},{10,2},{11,3},{12,4},{13,5},{14,6},{15,7},{16,8},{17,9... | collective-permute-start | bytes 3145736 | tf_op jit(solution)/shard_map/ppermute | solution.py:244
  13.3 1.4 %copy-done.1 = bf16[1,1,2048,384]{3,2,1,0:T(8,128)(2,1)S(1)} copy-done((bf16[1,1,2048,384]{3,2,1,0:T(8,128)(2,1)S(1)}, bf16[1,1,2048,384]{3,2,1,0:T(8,128)(2,1)}, u32[]{:S(2)}) %copy-start.1) | copy-done | bytes 1572888
  14.7 1.4 %copy-done.2 = bf16[1,1,384,2048]{3,2,1,0:T(8,128)(2,1)S(1)} copy-done((bf16[1,1,384,2048]{3,2,1,0:T(8,128)(2,1)S(1)}, bf16[1,1,384,2048]{3,2,1,0:T(8,128)(2,1)}, u32[]{:S(2)}) %copy-start.2) | copy-done | bytes 1572888
  16.1 2.2 %expert.4 = (bf16[88,1024]{1,0:T(8,128)(2,1)S(1)}, bf16[80,384]{1,0:T(8,128)(2,1)S(1)}, bf16[80,384]{1,0:T(8,128)(2,1)S(1)}, bf16[80,384]{1,0:T(8,128)(2,1)S(1)}) custom-call(s32[8,256]{1,0:T(8,128)S(1)} %select_bitcast_fusion.keys_ref.refs_0_, bf16[80,2048]{1,0:T(8,128)(2,1)S(1)} %get-tuple-element.40.refs_1_.refs_0_, ...), custom_call_target="tpu_custom_call" | custom-call | flops 1 | bytes 1 | tf_op jit(solution)/shard_map/expert/pallas_call | solution.py:136
  18.3 5.5 %collective-permute-done.3.refs_0_.refs_2_ = bf16[80,2048]{1,0:T(8,128)(2,1)S(1)} collective-permute-done((bf16[80,2048]{1,0:T(8,128)(2,1)S(1)}, bf16[80,2048]{1,0:T(8,128)(2,1)S(1)}, u32[]{:S(2)}, u32[]{:S(2)}) %collective-permute-start.3) | collective-permute-done | bytes 327712 | tf_op jit(solution)/shard_map/ppermute | solution.py:236
  24.9 3.0 %collective-permute-start.9 = (bf16[80,2048]{1,0:T(8,128)(2,1)S(1)}, bf16[80,2048]{1,0:T(8,128)(2,1)S(1)}, u32[]{:S(2)}, u32[]{:S(2)}) collective-permute-start(bf16[80,2048]{1,0:T(8,128)(2,1)S(1)} %get-tuple-element.60), channel_id=1, source_target_pairs={{0,6},{1,7},{2,4},{3,5},{4,2},{5,3},{6,0},{7,1},{8,14},{9,15},{10,... | collective-permute-start | bytes 983048 | tf_op jit(solution)/shard_map/ppermute | solution.py:236
  27.9 2.2 %expert.5 = (bf16[80,1024]{1,0:T(8,128)(2,1)S(1)}, bf16[80,384]{1,0:T(8,128)(2,1)S(1)}, bf16[80,384]{1,0:T(8,128)(2,1)S(1)}, bf16[80,384]{1,0:T(8,128)(2,1)S(1)}) custom-call(bf16[80,2048]{1,0:T(8,128)(2,1)S(1)} %collective-permute-done.3.refs_0_.refs_2_, bf16[80,2048]{1,0:T(8,128)(2,1)S(1)} %collective-permute-done.5.refs_1_.refs_3_, ...), custom_call_target="tpu_custom_call" | custom-call | flops 1 | bytes 1 | tf_op jit(solution)/shard_map/expert/pallas_call | solution.py:136
  30.1 2.2 %expert.6 = (bf16[80,1024]{1,0:T(8,128)(2,1)S(1)}, bf16[80,384]{1,0:T(8,128)(2,1)S(1)}, bf16[80,384]{1,0:T(8,128)(2,1)S(1)}, bf16[80,384]{1,0:T(8,128)(2,1)S(1)}) custom-call(bf16[80,2048]{1,0:T(8,128)(2,1)S(1)} %collective-permute-done.4.refs_0_.refs_4_, bf16[80,2048]{1,0:T(8,128)(2,1)S(1)} %collective-permute-done.7.refs_1_.refs_5_, ...), custom_call_target="tpu_custom_call" | custom-call | flops 1 | bytes 1 | tf_op jit(solution)/shard_map/expert/pallas_call | solution.py:136
  32.4 3.1 %collective-permute-done.9.refs_0_.refs_6_ = bf16[80,2048]{1,0:T(8,128)(2,1)S(1)} collective-permute-done((bf16[80,2048]{1,0:T(8,128)(2,1)S(1)}, bf16[80,2048]{1,0:T(8,128)(2,1)S(1)}, u32[]{:S(2)}, u32[]{:S(2)}) %collective-permute-start.9) | collective-permute-done | bytes 327712 | tf_op jit(solution)/shard_map/ppermute | solution.py:236
  35.5 1.4 %collective-permute-start.10 = (bf16[80,2048]{1,0:T(8,128)(2,1)S(1)}, bf16[80,2048]{1,0:T(8,128)(2,1)S(1)}, u32[]{:S(2)}, u32[]{:S(2)}) collective-permute-start(bf16[80,2048]{1,0:T(8,128)(2,1)S(1)} %collective-permute-done.9.refs_0_.refs_6_), channel_id=1, source_target_pairs={{0,1},{1,0},{2,3},{3,2},{4,5},{5,4},{6,7},{7,6},{8,9},{9,8},{10,11... | collective-permute-start | bytes 983048 | tf_op jit(solution)/shard_map/ppermute | solution.py:236
  36.9 3.1 %collective-permute-start.2 = (bf16[88,1024]{1,0:T(8,128)(2,1)S(1)}, bf16[88,1024]{1,0:T(8,128)(2,1)S(1)}, u32[]{:S(2)}, u32[]{:S(2)}) collective-permute-start(bf16[88,1024]{1,0:T(8,128)(2,1)S(1)} %get-tuple-element.42), channel_id=1, source_target_pairs={{8,0},{9,1},{10,2},{11,3},{12,4},{13,5},{14,6},{15,7},{16,8},{17,9... | collective-permute-start | bytes 540680 | tf_op jit(solution)/shard_map/ppermute | solution.py:244
  40.0 8.2 %collective-permute-start.8 = (bf16[80,1024]{1,0:T(8,128)(2,1)S(1)}, bf16[80,1024]{1,0:T(8,128)(2,1)S(1)}, u32[]{:S(2)}, u32[]{:S(2)}) collective-permute-start(bf16[80,1024]{1,0:T(8,128)(2,1)S(1)} %get-tuple-element.58), channel_id=1, source_target_pairs={{8,2},{9,3},{10,0},{11,1},{12,6},{13,7},{14,4},{15,5},{16,10},{17,... | collective-permute-start | bytes 491528 | tf_op jit(solution)/shard_map/ppermute | solution.py:244
  48.2 1.9 %collective-permute-start.6 = (bf16[80,1024]{1,0:T(8,128)(2,1)S(1)}, bf16[80,1024]{1,0:T(8,128)(2,1)S(1)}, u32[]{:S(2)}, u32[]{:S(2)}) collective-permute-start(bf16[80,1024]{1,0:T(8,128)(2,1)S(1)} %get-tuple-element.51), channel_id=1, source_target_pairs={{8,4},{9,5},{10,6},{11,7},{12,0},{13,1},{14,2},{15,3},{16,12},{17,... | collective-permute-start | bytes 491528 | tf_op jit(solution)/shard_map/ppermute | solution.py:244
  50.1 2.2 %expert.7 = (bf16[40,1024]{1,0:T(8,128)(2,1)S(1)}, bf16[40,1024]{1,0:T(8,128)(2,1)S(1)}, bf16[80,384]{1,0:T(8,128)(2,1)S(1)}, bf16[80,384]{1,0:T(8,128)(2,1)S(1)}, bf16[80,384]{1,0:T(8,128)(2,1)S(1)}) custom-call(bf16[80,2048]{1,0:T(8,128)(2,1)S(1)} %collective-permute-done.9.refs_0_.refs_6_, bf16[80,2048]{1,0:T(8,128)(2,1)S(1)} %collective-permute-done.10.refs_1_.refs_7_, ...), custom_call_target="tpu_custom_call" | custom-call | flops 1 | bytes 1 | tf_op jit(solution)/shard_map/expert/pallas_call | solution.py:136
  52.3 4.1 %weight_grads.1 = (bf16[2048,384]{1,0:T(8,128)(2,1)}, bf16[2048,384]{1,0:T(8,128)(2,1)}, bf16[384,2048]{1,0:T(8,128)(2,1)}) custom-call(bf16[80,2048]{1,0:T(8,128)(2,1)S(1)} %get-tuple-element.40.refs_1_.refs_0_, bf16[80,2048]{1,0:T(8,128)(2,1)S(1)} %collective-permute-done.1.refs_2_.refs_1_, bf16[80,2048]{1,0:T(8,128)(2,1)S(1)} %collective-permute-done.3.refs_0_.refs_2_, ...), custom_call_target="tpu_custom_call" | custom-call | flops 1 | bytes 1 | tf_op jit(solution)/shard_map/weight_grads/pallas_call | solution.py:166
  56.5 4.5 %collective-permute-done.6.refs_4_ = bf16[80,1024]{1,0:T(8,128)(2,1)S(1)} collective-permute-done((bf16[80,1024]{1,0:T(8,128)(2,1)S(1)}, bf16[80,1024]{1,0:T(8,128)(2,1)S(1)}, u32[]{:S(2)}, u32[]{:S(2)}) %collective-permute-start.6) | collective-permute-done | bytes 163872 | tf_op jit(solution)/shard_map/ppermute | solution.py:244
  62.4 3.1 %collective-permute-start.14 = (bf16[40,1024]{1,0:T(8,128)(2,1)S(1)}, bf16[40,1024]{1,0:T(8,128)(2,1)S(1)}, u32[]{:S(2)}, u32[]{:S(2)}) collective-permute-start(bf16[40,1024]{1,0:T(8,128)(2,1)S(1)} %get-tuple-element.72), channel_id=1, source_target_pairs={{8,6},{9,7},{10,4},{11,5},{12,2},{13,3},{14,0},{15,1},{16,14},{17,... | collective-permute-start | bytes 245768 | tf_op jit(solution)/shard_map/ppermute | solution.py:244
  65.5 1.9 %collective-permute-start.15 = (bf16[40,1024]{1,0:T(8,128)(2,1)S(1)}, bf16[40,1024]{1,0:T(8,128)(2,1)S(1)}, u32[]{:S(2)}, u32[]{:S(2)}) collective-permute-start(bf16[40,1024]{1,0:T(8,128)(2,1)S(1)} %get-tuple-element.73), channel_id=1, source_target_pairs={{8,7},{9,6},{10,5},{11,4},{12,3},{13,2},{14,1},{15,0},{16,15},{17,... | collective-permute-start | bytes 245768 | tf_op jit(solution)/shard_map/ppermute | solution.py:244
  67.4 3.6 %collective-permute-done.14.refs_6_ = bf16[40,1024]{1,0:T(8,128)(2,1)S(1)} collective-permute-done((bf16[40,1024]{1,0:T(8,128)(2,1)S(1)}, bf16[40,1024]{1,0:T(8,128)(2,1)S(1)}, u32[]{:S(2)}, u32[]{:S(2)}) %collective-permute-start.14) | collective-permute-done | bytes 81952 | tf_op jit(solution)/shard_map/ppermute | solution.py:244
  71.1 3.4 %collective-permute-done.15.refs_7_ = bf16[40,1024]{1,0:T(8,128)(2,1)S(1)} collective-permute-done((bf16[40,1024]{1,0:T(8,128)(2,1)S(1)}, bf16[40,1024]{1,0:T(8,128)(2,1)S(1)}, u32[]{:S(2)}, u32[]{:S(2)}) %collective-permute-start.15) | collective-permute-done | bytes 81952 | tf_op jit(solution)/shard_map/ppermute | solution.py:244
  74.5 1.9 %combine.1 = bf16[256,2048]{1,0:T(8,128)(2,1)} custom-call(bf16[256,2048]{1,0:T(8,128)(2,1)S(1)} %collective-permute-done.grad_ref, bf16[88,1024]{1,0:T(8,128)(2,1)S(1)} %collective-permute-done.2.refs_0_, bf16[88,1024]{1,0:T(8,128)(2,1)S(1)} %collective-permute-done.11.refs_1_, bf16[80,1024]{1,0:T(8,128)(2,1)S(1)} %collective-permute-done.8.refs_2_, ...), custom_call_target="tpu_custom_call" | custom-call | flops 1 | bytes 1 | tf_op jit(solution)/shard_map/combine/pallas_call | solution.py:202
  (26 shorter events, 6.1 us)
Async XLA Ops:
  0.6 12.6 %copy-start = (bf16[1,1,2048,384]{3,2,1,0:T(8,128)(2,1)S(1)}, bf16[1,1,2048,384]{3,2,1,0:T(8,128)(2,1)}, u32[]{:S(2)}) copy-start(bf16[1,1,2048,384]{3,2,1,0:T(8,128)(2,1)} %param.15) | copy-start | bytes 4718596
  1.5 1.2 %copy-start.3 = (bf16[1,256,2048]{2,1,0:T(8,128)(2,1)S(1)}, bf16[1,256,2048]{2,1,0:T(8,128)(2,1)}, u32[]{:S(2)}) copy-start(bf16[1,256,2048]{2,1,0:T(8,128)(2,1)} %param.9) | copy-start | bytes 3145732
  2.7 0.7 copy-start.4
  5.8 7.4 %collective-permute-start.1 = (bf16[80,2048]{1,0:T(8,128)(2,1)S(1)}, bf16[80,2048]{1,0:T(8,128)(2,1)S(1)}, u32[]{:S(2)}, u32[]{:S(2)}) collective-permute-start(bf16[80,2048]{1,0:T(8,128)(2,1)S(1)} %get-tuple-element.40.refs_1_.refs_0_), channel_id=1, source_target_pairs={{0,1},{1,0},{2,3},{3,2},{4,5},{5,4},{6,7},{7,6},{8,9},{9,8},{10,11... | collective-permute-start | bytes 983048 | tf_op jit(solution)/shard_map/ppermute | solution.py:236
  6.5 17.3 %collective-permute-start.3 = (bf16[80,2048]{1,0:T(8,128)(2,1)S(1)}, bf16[80,2048]{1,0:T(8,128)(2,1)S(1)}, u32[]{:S(2)}, u32[]{:S(2)}) collective-permute-start(bf16[80,2048]{1,0:T(8,128)(2,1)S(1)} %get-tuple-element.43), channel_id=1, source_target_pairs={{0,4},{1,5},{2,6},{3,7},{4,0},{5,1},{6,2},{7,3},{8,12},{9,13},{10,... | collective-permute-start | bytes 983048 | tf_op jit(solution)/shard_map/ppermute | solution.py:236
  8.9 14.9 %collective-permute-start.4 = (bf16[80,2048]{1,0:T(8,128)(2,1)S(1)}, bf16[80,2048]{1,0:T(8,128)(2,1)S(1)}, u32[]{:S(2)}, u32[]{:S(2)}) collective-permute-start(bf16[80,2048]{1,0:T(8,128)(2,1)S(1)} %get-tuple-element.44), channel_id=1, source_target_pairs={{0,2},{1,3},{2,0},{3,1},{4,6},{5,7},{6,4},{7,5},{8,10},{9,11},{10,... | collective-permute-start | bytes 983048 | tf_op jit(solution)/shard_map/ppermute | solution.py:236
  10.2 55.4 %collective-permute-start = (bf16[256,2048]{1,0:T(8,128)(2,1)}, bf16[256,2048]{1,0:T(8,128)(2,1)S(1)}, u32[]{:S(2)}, u32[]{:S(2)}) collective-permute-start(bf16[256,2048]{1,0:T(8,128)(2,1)} %bitcast.grad_ref), channel_id=1, source_target_pairs={{8,0},{9,1},{10,2},{11,3},{12,4},{13,5},{14,6},{15,7},{16,8},{17,9... | collective-permute-start | bytes 3145736 | tf_op jit(solution)/shard_map/ppermute | solution.py:244
  13.2 1.4 %copy-start.1 = (bf16[1,1,2048,384]{3,2,1,0:T(8,128)(2,1)S(1)}, bf16[1,1,2048,384]{3,2,1,0:T(8,128)(2,1)}, u32[]{:S(2)}) copy-start(bf16[1,1,2048,384]{3,2,1,0:T(8,128)(2,1)} %param.16) | copy-start | bytes 4718596
  14.7 1.4 %copy-start.2 = (bf16[1,1,384,2048]{3,2,1,0:T(8,128)(2,1)S(1)}, bf16[1,1,384,2048]{3,2,1,0:T(8,128)(2,1)}, u32[]{:S(2)}) copy-start(bf16[1,1,384,2048]{3,2,1,0:T(8,128)(2,1)} %param.17) | copy-start | bytes 4718596
  23.8 4.1 %collective-permute-start.5 = (bf16[80,2048]{1,0:T(8,128)(2,1)S(1)}, bf16[80,2048]{1,0:T(8,128)(2,1)S(1)}, u32[]{:S(2)}, u32[]{:S(2)}) collective-permute-start(bf16[80,2048]{1,0:T(8,128)(2,1)S(1)} %collective-permute-done.3.refs_0_.refs_2_), channel_id=1, source_target_pairs={{0,1},{1,0},{2,3},{3,2},{4,5},{5,4},{6,7},{7,6},{8,9},{9,8},{10,11... | collective-permute-start | bytes 983048 | tf_op jit(solution)/shard_map/ppermute | solution.py:236
  24.9 5.2 %collective-permute-start.7 = (bf16[80,2048]{1,0:T(8,128)(2,1)S(1)}, bf16[80,2048]{1,0:T(8,128)(2,1)S(1)}, u32[]{:S(2)}, u32[]{:S(2)}) collective-permute-start(bf16[80,2048]{1,0:T(8,128)(2,1)S(1)} %collective-permute-done.4.refs_0_.refs_4_), channel_id=1, source_target_pairs={{0,1},{1,0},{2,3},{3,2},{4,5},{5,4},{6,7},{7,6},{8,9},{9,8},{10,11... | collective-permute-start | bytes 983048 | tf_op jit(solution)/shard_map/ppermute | solution.py:236
  24.9 10.6 %collective-permute-start.9 = (bf16[80,2048]{1,0:T(8,128)(2,1)S(1)}, bf16[80,2048]{1,0:T(8,128)(2,1)S(1)}, u32[]{:S(2)}, u32[]{:S(2)}) collective-permute-start(bf16[80,2048]{1,0:T(8,128)(2,1)S(1)} %get-tuple-element.60), channel_id=1, source_target_pairs={{0,6},{1,7},{2,4},{3,5},{4,2},{5,3},{6,0},{7,1},{8,14},{9,15},{10,... | collective-permute-start | bytes 983048 | tf_op jit(solution)/shard_map/ppermute | solution.py:236
  35.5 14.6 %collective-permute-start.10 = (bf16[80,2048]{1,0:T(8,128)(2,1)S(1)}, bf16[80,2048]{1,0:T(8,128)(2,1)S(1)}, u32[]{:S(2)}, u32[]{:S(2)}) collective-permute-start(bf16[80,2048]{1,0:T(8,128)(2,1)S(1)} %collective-permute-done.9.refs_0_.refs_6_), channel_id=1, source_target_pairs={{0,1},{1,0},{2,3},{3,2},{4,5},{5,4},{6,7},{7,6},{8,9},{9,8},{10,11... | collective-permute-start | bytes 983048 | tf_op jit(solution)/shard_map/ppermute | solution.py:236
  36.9 19.5 %collective-permute-start.2 = (bf16[88,1024]{1,0:T(8,128)(2,1)S(1)}, bf16[88,1024]{1,0:T(8,128)(2,1)S(1)}, u32[]{:S(2)}, u32[]{:S(2)}) collective-permute-start(bf16[88,1024]{1,0:T(8,128)(2,1)S(1)} %get-tuple-element.42), channel_id=1, source_target_pairs={{8,0},{9,1},{10,2},{11,3},{12,4},{13,5},{14,6},{15,7},{16,8},{17,9... | collective-permute-start | bytes 540680 | tf_op jit(solution)/shard_map/ppermute | solution.py:244
  40.0 16.5 %collective-permute-start.8 = (bf16[80,1024]{1,0:T(8,128)(2,1)S(1)}, bf16[80,1024]{1,0:T(8,128)(2,1)S(1)}, u32[]{:S(2)}, u32[]{:S(2)}) collective-permute-start(bf16[80,1024]{1,0:T(8,128)(2,1)S(1)} %get-tuple-element.58), channel_id=1, source_target_pairs={{8,2},{9,3},{10,0},{11,1},{12,6},{13,7},{14,4},{15,5},{16,10},{17,... | collective-permute-start | bytes 491528 | tf_op jit(solution)/shard_map/ppermute | solution.py:244
  48.2 12.8 %collective-permute-start.6 = (bf16[80,1024]{1,0:T(8,128)(2,1)S(1)}, bf16[80,1024]{1,0:T(8,128)(2,1)S(1)}, u32[]{:S(2)}, u32[]{:S(2)}) collective-permute-start(bf16[80,1024]{1,0:T(8,128)(2,1)S(1)} %get-tuple-element.51), channel_id=1, source_target_pairs={{8,4},{9,5},{10,6},{11,7},{12,0},{13,1},{14,2},{15,3},{16,12},{17,... | collective-permute-start | bytes 491528 | tf_op jit(solution)/shard_map/ppermute | solution.py:244
  61.0 13.5 %collective-permute-start.11 = (bf16[88,1024]{1,0:T(8,128)(2,1)S(1)}, bf16[88,1024]{1,0:T(8,128)(2,1)S(1)}, u32[]{:S(2)}, u32[]{:S(2)}) collective-permute-start(bf16[88,1024]{1,0:T(8,128)(2,1)S(1)} %collective-permute-done.2.refs_0_), channel_id=1, source_target_pairs={{0,1},{1,0},{2,3},{3,2},{4,5},{5,4},{6,7},{7,6},{8,9},{9,8},{10,11... | collective-permute-start | bytes 540680 | tf_op jit(solution)/shard_map/ppermute | solution.py:236
  61.9 12.6 %collective-permute-start.12 = (bf16[80,1024]{1,0:T(8,128)(2,1)S(1)}, bf16[80,1024]{1,0:T(8,128)(2,1)S(1)}, u32[]{:S(2)}, u32[]{:S(2)}) collective-permute-start(bf16[80,1024]{1,0:T(8,128)(2,1)S(1)} %collective-permute-done.8.refs_2_), channel_id=1, source_target_pairs={{0,1},{1,0},{2,3},{3,2},{4,5},{5,4},{6,7},{7,6},{8,9},{9,8},{10,11... | collective-permute-start | bytes 491528 | tf_op jit(solution)/shard_map/ppermute | solution.py:236
  61.9 12.6 %collective-permute-start.13 = (bf16[80,1024]{1,0:T(8,128)(2,1)S(1)}, bf16[80,1024]{1,0:T(8,128)(2,1)S(1)}, u32[]{:S(2)}, u32[]{:S(2)}) collective-permute-start(bf16[80,1024]{1,0:T(8,128)(2,1)S(1)} %collective-permute-done.6.refs_4_), channel_id=1, source_target_pairs={{0,1},{1,0},{2,3},{3,2},{4,5},{5,4},{6,7},{7,6},{8,9},{9,8},{10,11... | collective-permute-start | bytes 491528 | tf_op jit(solution)/shard_map/ppermute | solution.py:236
  62.4 8.7 %collective-permute-start.14 = (bf16[40,1024]{1,0:T(8,128)(2,1)S(1)}, bf16[40,1024]{1,0:T(8,128)(2,1)S(1)}, u32[]{:S(2)}, u32[]{:S(2)}) collective-permute-start(bf16[40,1024]{1,0:T(8,128)(2,1)S(1)} %get-tuple-element.72), channel_id=1, source_target_pairs={{8,6},{9,7},{10,4},{11,5},{12,2},{13,3},{14,0},{15,1},{16,14},{17,... | collective-permute-start | bytes 245768 | tf_op jit(solution)/shard_map/ppermute | solution.py:244
  65.5 8.9 %collective-permute-start.15 = (bf16[40,1024]{1,0:T(8,128)(2,1)S(1)}, bf16[40,1024]{1,0:T(8,128)(2,1)S(1)}, u32[]{:S(2)}, u32[]{:S(2)}) collective-permute-start(bf16[40,1024]{1,0:T(8,128)(2,1)S(1)} %get-tuple-element.73), channel_id=1, source_target_pairs={{8,7},{9,6},{10,5},{11,4},{12,3},{13,2},{14,1},{15,0},{16,15},{17,... | collective-permute-start | bytes 245768 | tf_op jit(solution)/shard_map/ppermute | solution.py:244

commit v3 on v2

--- a/solution.py
+++ b/solution.py
@@ -76,26 +76,21 @@
     return lax.dot_general(a, b, (((0,), (0,)), ((), ())), preferred_element_type=F32)
 
 
-def joined(pieces):
-    return jnp.concatenate(
-        [
-            p[PAIR : 2 * PAIR, :] if i % 2 and p.shape[0] > PAIR else p[:PAIR, :]
-            for i, p in enumerate(pieces)
-        ],
-        axis=0,
-    )
-
-
-def expert_kernel(count, with_keys, *refs):
+def joined(refs, spans):
+    return jnp.concatenate([r[lo:hi, :] for r, (lo, hi) in zip(refs, spans)], axis=0)
+
+
+def expert_kernel(spans, with_keys, *refs):
+    count = len(spans)
     if with_keys:
         keys_ref, refs = refs[0], refs[1:]
     payloads = refs[:count]
     w_gate, w_up, w_down = refs[count : count + 3]
     returns = refs[count + 3 : -3]
     gate_out, up_out, hidden_out = refs[-3:]
-    rows = count * PAIR
+    rows = sum(hi - lo for lo, hi in spans)
     half = w_gate.shape[0] // 2
-    both = joined(payloads)
+    both = joined(payloads, spans)
     gate_pre = jnp.dot(both, w_gate[...], preferred_element_type=F32)
     up_pre = jnp.dot(both, w_up[...], preferred_element_type=F32)
     hidden_grad = pltpu.roll(nt(both, w_down[...]), rows - CAP, 0)
@@ -121,36 +116,39 @@
         ranks, tokens = keys_ref.shape
         keys = keys_ref[...].astype(F32)
         block = jnp.floor((keys + 0.5) / PAIR)
-        returns[0][2 * PAIR :, :tokens] = block.astype(BF16)
-        returns[0][2 * PAIR :, tokens : 2 * tokens] = (keys - PAIR * block).astype(BF16)
-        returns[0][2 * PAIR :, 2 * tokens :] = jnp.zeros((ranks, half - 2 * tokens), BF16)
-
-
-def expert_chunk(pieces, w_gate, w_up, w_down, keys=None, single=False):
-    count = len(pieces)
+        for out in returns:
+            out[2 * PAIR :, :tokens] = block.astype(BF16)
+            out[2 * PAIR :, tokens : 2 * tokens] = (keys - PAIR * block).astype(BF16)
+            out[2 * PAIR :, 2 * tokens :] = jnp.zeros((ranks, half - 2 * tokens), BF16)
+
+
+def expert_chunk(pieces, w_gate, w_up, w_down, keys=None):
+    arrays, spans = [p[0] for p in pieces], [p[1] for p in pieces]
+    total = sum(hi - lo for lo, hi in spans)
     width, hidden = w_gate.shape
     extra = [] if keys is None else [keys]
-    rows = [PAIR] * count if single else [2 * PAIR] * (count // 2)
+    rows = [2 * PAIR] * (total // (2 * PAIR))
     if extra:
-        rows[0] += keys.shape[0]
+        rows = [r + keys.shape[0] for r in rows]
     out = pl.pallas_call(
-        functools.partial(expert_kernel, count, bool(extra)),
+        functools.partial(expert_kernel, spans, bool(extra)),
         out_shape=[jax.ShapeDtypeStruct((r, width // 2), BF16) for r in rows]
-        + [jax.ShapeDtypeStruct((PAIR * count, hidden), BF16)] * 3,
-        in_specs=vmem(len(extra) + count + 3),
+        + [jax.ShapeDtypeStruct((total, hidden), BF16)] * 3,
+        in_specs=vmem(len(extra) + len(pieces) + 3),
         out_specs=vmem(len(rows) + 3),
         name="expert",
         compiler_params=pltpu.CompilerParams(vmem_limit_bytes=20 << 20),
         cost_estimate=SHORT,
-    )(*extra, *pieces, w_gate, w_up, w_down)
+    )(*extra, *arrays, w_gate, w_up, w_down)
     return out[: len(rows)], out[len(rows) :]
 
 
-def weight_kernel(count, chunks, *refs):
+def weight_kernel(spans, chunks, *refs):
+    count = len(spans)
     payloads = refs[:count]
     small = refs[count : count + 3 * chunks]
     grad_gate, grad_up, grad_down = refs[count + 3 * chunks :]
-    both = joined(payloads)
+    both = joined(payloads, spans)
     gate = jnp.concatenate([r[...] for r in small[0::3]], axis=0)
     up = jnp.concatenate([r[...] for r in small[1::3]], axis=0)
     hidden = jnp.concatenate([r[...] for r in small[2::3]], axis=0)
@@ -159,12 +157,13 @@
     grad_down[...] = tn(hidden, both).astype(BF16)
 
 
-def weight_grads(payloads, small, width, hidden):
-    count = len(payloads)
+def weight_grads(pieces, small, width, hidden):
+    count = len(pieces)
+    payloads, spans = [p[0] for p in pieces], [p[1] for p in pieces]
     chunks = len(small)
     flat = [a for part in small for a in part]
     return pl.pallas_call(
-        functools.partial(weight_kernel, count, chunks),
+        functools.partial(weight_kernel, spans, chunks),
         out_shape=[
             jax.ShapeDtypeStruct((width, hidden), BF16),
             jax.ShapeDtypeStruct((width, hidden), BF16),
@@ -178,9 +177,9 @@
     )(*payloads, *flat)
 
 
-def combine_kernel(ranks, grad_ref, *refs):
+def combine_kernel(spans, ranks, grad_ref, *refs):
     returned, out = refs[:-1], refs[-1]
-    rows = PAIR * len(returned)
+    rows = sum(hi - lo for lo, hi in spans)
     tokens = grad_ref.shape[0]
     block = returned[0][2 * PAIR : 2 * PAIR + ranks, :tokens].astype(F32)
     slot = returned[0][2 * PAIR : 2 * PAIR + ranks, tokens : 2 * tokens].astype(F32)
@@ -190,7 +189,7 @@
     for hit in match_rows(keys, 0, rows):
         own = jnp.where(hit, 1.0, own)
     first = is_first((rows, tokens))
-    back = joined(returned)
+    back = joined(returned, spans)
     for side in range(2):
         pick = jnp.where(first, own, 0.0) if side == 0 else jnp.where(first, 0.0, own)
         cols = slice(side * half, (side + 1) * half)
@@ -198,9 +197,10 @@
         out[:, cols] = total.astype(BF16)
 
 
-def combine(ranks, grads, returned):
+def combine(ranks, grads, pieces):
+    returned, spans = [p[0] for p in pieces], [p[1] for p in pieces]
     return pl.pallas_call(
-        functools.partial(combine_kernel, ranks),
+        functools.partial(combine_kernel, spans, ranks),
         out_shape=jax.ShapeDtypeStruct(grads.shape, BF16),
         in_specs=vmem(1 + len(returned)),
         out_specs=pl.BlockSpec(memory_space=pltpu.VMEM),
@@ -251,52 +251,54 @@
     near = list(range(1, chips // 2))
     early = list(range(chips // 2, 3 * chips // 4))
     late = list(range(3 * chips // 4, chips))
-    sent = gather(keys, weight, inputs, grads, chips, [])
-    behind, _ = lax.optimization_barrier((grads, sent[0]))
-    next_grads = to_before(behind, 0)
-
-    got, small, order, arrived, returned = {}, [], [], {}, {}
+    sent = gather(keys, weight, inputs, grads, chips, [0] + late)
+    mine = (0, PAIR)
 
     def after(values, event):
         return lax.optimization_barrier((values, event))[0]
 
-    def process(chunk, event=None, **options):
-        pieces = [piece for c in chunk for piece in got[c]]
-        if event is not None:
-            pieces = after(pieces, event)
+    def forward(value, *cuts):
+        edges = [PAIR, *cuts, 2 * PAIR]
+        pieces = [(value, mine)]
+        for lo, hi in zip(edges, edges[1:]):
+            pieces.append((to_partner(value[lo:hi], 1), (0, hi - lo)))
+        return pieces
+
+    def gated(pieces, event):
+        values = after([p[0] for p in pieces], event)
+        return [(v, p[1]) for v, p in zip(values, pieces)]
+
+    arrived, order, small, returned = {}, [], [], {}
+
+    def process(chunk, pieces, **options):
         back, parts = expert_chunk(pieces, w_gate, w_up, w_down, **options)
         order.extend(pieces)
         small.append(parts)
-        return back, parts
-
-    def forward(values, event):
-        values = after(values, event)
-        return [[value, to_partner(value, 1)] for value in values]
+        for c, value in zip(chunk, back):
+            returned[c] = to_before(value, 2 * c)
+        return parts
 
     for c in early + near:
         arrived[c] = to_partner(sent[c], 2 * c)
-    got[0] = [sent[0], to_partner(sent[0], 1)]
-    back, own = process([0], keys=keys)
-    returned[0] = to_before(back[0], 0)
-    for c, value in zip(late, after([sent[c] for c in late], own)):
-        arrived[c] = to_partner(value, 2 * c)
-    got.update(zip(early + near, forward([arrived[c] for c in early + near], own)))
-    parts = own
-    for chunk in (early, near):
-        if chunk:
-            back, parts = process(chunk, parts)
-            for c, value in zip(chunk, back):
-                returned[c] = to_before(value, 2 * c)
-    got.update(zip(late, forward([arrived[c] for c in late], parts)))
-    back, parts = process(late, single=True)
-    for i, c in enumerate(late):
-        returned[c] = [to_before(back[2 * i + j], 2 * c + j) for j in range(2)]
+    for c in late:
+        arrived[c] = [(to_partner(v, 2 * c + i), mine) for i, v in enumerate(sent[c])]
+    beside = to_partner(sent[0][1], 1)
+    next_grads = to_before(after(grads, sent[0][0]), 0)
+    pieces = [(sent[0][0], mine), (beside, mine)]
+    for c in near:
+        pieces += forward(arrived[c])
+    parts = process([0] + near, pieces, keys=keys)
+    pieces = [piece for c in early for piece in forward(arrived[c], PAIR + 24)]
+    parts = process(early, gated(pieces, parts))
+    pieces = [piece for c in late for piece in arrived[c]]
+    process(late, gated(pieces, (parts, next_grads)))
+    small[0] = after(small[0], [returned[c] for c in [0] + near])
     grad_gate, grad_up, grad_down = weight_grads(order, small, width, hidden)
-    both = [0] + early + near
-    returned.update(zip(both, forward([returned[c] for c in both], grad_gate)))
-    upstream = combine(
-        keys.shape[0], next_grads, [piece for c in range(chips) for piece in returned[c]]
-    )
+    pieces = []
+    for c in range(chips):
+        value = after(returned[c], grad_gate) if c not in late else returned[c]
+        pieces += forward(value)
+    upstream = combine(keys.shape[0], next_grads, pieces)
     return (upstream[None], grad_gate[None, None], grad_up[None, None], grad_down[None, None])
 
 

time: 76.8 us -> 66 us (0.86)
  the two profiles are of different devices: /device:TPU:5 before, /device:TPU:13 now
where the time goes in v3:
time: 66 us; the launch traced here: 65.7 us
  starting transfers between devices  26.8 us (41%)
  waiting for transfers between devices  16.9 us (26%)
  Pallas kernels  15.5 us (23%)
  local copies, waits for them, and re-layouts  4.79 us (7%)
  other arithmetic  0.85 us (1%)
  between operations  0.82 us (1%)
    ppermute x5, starting transfers between devices, to_before(): return lax.ppermute(value, both_axes, pairs)  14.2 us
    ppermute x12, starting transfers between devices, to_partner(): return lax.ppermute(value, 'expert', [(i, i ^ k) for i in range(n_expert)])  12.6 us
    ppermute x12, waiting for transfers between devices, to_partner(): return lax.ppermute(value, 'expert', [(i, i ^ k) for i in range(n_expert)])  10.1 us
    pallas_call x3, Pallas kernels, expert_chunk(): pl.pallas_call(functools.partial(expert_kernel, spans, bool(extra)), out_...  7.11 us
    ppermute x5, waiting for transfers between devices, to_before(): return lax.ppermute(value, both_axes, pairs)  6.83 us
    unnamed x10, local copies, waits for them, and re-layouts  4.74 us
    pallas_call x1, Pallas kernels, weight_grads(): pl.pallas_call(functools.partial(weight_kernel, spans, chunks), out_shape...  4.15 us
    pallas_call x1, Pallas kernels, gather(): pl.pallas_call(gather_kernel, out_shape=[jax.ShapeDtypeStruct((n, width),...  2.37 us
  transfers between devices with their start and end apart: 17, of which 4 were waited for; matrix products, arithmetic and copies ran while one was open for 0% of the time, Pallas kernels for 17%

profile of v3, /device:TPU:13, one launch (start us, length us, event | category | flops | bytes accessed | tf_op | source)
XLA Modules:
  0.0 65.7 jit_solution(6967916113916031967)
XLA Ops:
  1.5 1.2 %copy-done.3 = bf16[1,256,2048]{2,1,0:T(8,128)(2,1)S(1)} copy-done((bf16[1,256,2048]{2,1,0:T(8,128)(2,1)S(1)}, bf16[1,256,2048]{2,1,0:T(8,128)(2,1)}, u32[]{:S(2)}) %copy-start.3) | copy-done | bytes 1048600
  3.4 2.4 %gather.1 = (bf16[40,2048]{1,0:T(8,128)(2,1)S(1)}, bf16[40,2048]{1,0:T(8,128)(2,1)S(1)}, bf16[80,2048]{1,0:T(8,128)(2,1)S(1)}, bf16[80,2048]{1,0:T(8,128)(2,1)S(...) custom-call(s32[8,256]{1,0:T(8,128)S(1)} %select_bitcast_fusion.keys_ref.refs_0_, f32[8,256]{1,0:T(8,128)S(1)} %bitcast.26, ...), custom_call_target="tpu_custom_call" | custom-call | flops 1 | bytes 1 | tf_op jit(solution)/shard_map/gather/pallas_call | solution.py:58
  5.8 3.1 %collective-permute-start = (bf16[256,2048]{1,0:T(8,128)(2,1)}, bf16[256,2048]{1,0:T(8,128)(2,1)S(1)}, u32[]{:S(2)}, u32[]{:S(2)}) collective-permute-start(bf16[256,2048]{1,0:T(8,128)(2,1)} %bitcast.grad_ref), channel_id=1, source_target_pairs={{8,0},{9,1},{10,2},{11,3},{12,4},{13,5},{14,6},{15,7},{16,8},{17,9... | collective-permute-start | bytes 3145736 | tf_op jit(solution)/shard_map/ppermute | solution.py:244
  9.1 2.3 %collective-permute-start.5 = (bf16[80,2048]{1,0:T(8,128)(2,1)S(1)}, bf16[80,2048]{1,0:T(8,128)(2,1)S(1)}, u32[]{:S(2)}, u32[]{:S(2)}) collective-permute-start(bf16[80,2048]{1,0:T(8,128)(2,1)S(1)} %get-tuple-element.43), channel_id=1, source_target_pairs={{0,4},{1,5},{2,6},{3,7},{4,0},{5,1},{6,2},{7,3},{8,12},{9,13},{10,... | collective-permute-start | bytes 983048 | tf_op jit(solution)/shard_map/ppermute | solution.py:236
  11.4 1.5 %collective-permute-start.1 = (bf16[40,2048]{1,0:T(8,128)(2,1)S(1)}, bf16[40,2048]{1,0:T(8,128)(2,1)S(1)}, u32[]{:S(2)}, u32[]{:S(2)}) collective-permute-start(bf16[40,2048]{1,0:T(8,128)(2,1)S(1)} %get-tuple-element.40), channel_id=1, source_target_pairs={{0,1},{1,0},{2,3},{3,2},{4,5},{5,4},{6,7},{7,6},{8,9},{9,8},{10,11... | collective-permute-start | bytes 491528 | tf_op jit(solution)/shard_map/ppermute | solution.py:236
  12.9 9.1 %collective-permute-done.2.refs_3_.refs_2_ = bf16[80,2048]{1,0:T(8,128)(2,1)S(1)} collective-permute-done((bf16[80,2048]{1,0:T(8,128)(2,1)S(1)}, bf16[80,2048]{1,0:T(8,128)(2,1)S(1)}, u32[]{:S(2)}, u32[]{:S(2)}) %collective-permute-start.2) | collective-permute-done | bytes 327712 | tf_op jit(solution)/shard_map/ppermute | solution.py:236
  22.1 1.9 %collective-permute-start.3 = (bf16[40,2048]{1,0:T(8,128)(2,1)S(1)}, bf16[40,2048]{1,0:T(8,128)(2,1)S(1)}, u32[]{:S(2)}, u32[]{:S(2)}) collective-permute-start(bf16[40,2048]{1,0:T(8,128)(2,1)S(1)} %slice.28), channel_id=1, source_target_pairs={{0,1},{1,0},{2,3},{3,2},{4,5},{5,4},{6,7},{7,6},{8,9},{9,8},{10,11... | collective-permute-start | bytes 491528 | tf_op jit(solution)/shard_map/ppermute | solution.py:236
  24.0 1.3 %collective-permute-start.8 = (bf16[40,2048]{1,0:T(8,128)(2,1)S(1)}, bf16[40,2048]{1,0:T(8,128)(2,1)S(1)}, u32[]{:S(2)}, u32[]{:S(2)}) collective-permute-start(bf16[40,2048]{1,0:T(8,128)(2,1)S(1)} %get-tuple-element.50), channel_id=1, source_target_pairs={{0,6},{1,7},{2,4},{3,5},{4,2},{5,3},{6,0},{7,1},{8,14},{9,15},{10,... | collective-permute-start | bytes 491528 | tf_op jit(solution)/shard_map/ppermute | solution.py:236
  25.3 1.9 %collective-permute-start.9 = (bf16[40,2048]{1,0:T(8,128)(2,1)S(1)}, bf16[40,2048]{1,0:T(8,128)(2,1)S(1)}, u32[]{:S(2)}, u32[]{:S(2)}) collective-permute-start(bf16[40,2048]{1,0:T(8,128)(2,1)S(1)} %get-tuple-element.51), channel_id=1, source_target_pairs={{0,7},{1,6},{2,5},{3,4},{4,3},{5,2},{6,1},{7,0},{8,15},{9,14},{10,... | collective-permute-start | bytes 491528 | tf_op jit(solution)/shard_map/ppermute | solution.py:236
  27.9 1.4 %copy-done.1 = bf16[1,1,2048,384]{3,2,1,0:T(8,128)(2,1)S(1)} copy-done((bf16[1,1,2048,384]{3,2,1,0:T(8,128)(2,1)S(1)}, bf16[1,1,2048,384]{3,2,1,0:T(8,128)(2,1)}, u32[]{:S(2)}) %copy-start.1) | copy-done | bytes 1572888
  29.3 1.4 %copy-done.2 = bf16[1,1,384,2048]{3,2,1,0:T(8,128)(2,1)S(1)} copy-done((bf16[1,1,384,2048]{3,2,1,0:T(8,128)(2,1)S(1)}, bf16[1,1,384,2048]{3,2,1,0:T(8,128)(2,1)}, u32[]{:S(2)}) %copy-start.2) | copy-done | bytes 1572888
  30.7 2.6 %expert.3 = (bf16[88,1024]{1,0:T(8,128)(2,1)S(1)}, bf16[88,1024]{1,0:T(8,128)(2,1)S(1)}, bf16[160,384]{1,0:T(8,128)(2,1)S(1)}, bf16[160,384]{1,0:T(8,128)(2,1)S(1)}, bf16[160,384]{1,0:T(8,128)(2,1)S(1)}) custom-call(s32[8,256]{1,0:T(8,128)S(1)} %select_bitcast_fusion.keys_ref.refs_0_, bf16[40,2048]{1,0:T(8,128)(2,1)S(1)} %get-tuple-element.38.refs_1_.refs_0_, ...), custom_call_target="tpu_custom_call" | custom-call | flops 1 | bytes 1 | tf_op jit(solution)/shard_map/expert/pallas_call | solution.py:133
  33.4 5.3 %collective-permute-start.10 = (bf16[88,1024]{1,0:T(8,128)(2,1)S(1)}, bf16[88,1024]{1,0:T(8,128)(2,1)S(1)}, u32[]{:S(2)}, u32[]{:S(2)}) collective-permute-start(bf16[88,1024]{1,0:T(8,128)(2,1)S(1)} %get-tuple-element.57), channel_id=1, source_target_pairs={{8,2},{9,3},{10,0},{11,1},{12,6},{13,7},{14,4},{15,5},{16,10},{17,... | collective-permute-start | bytes 540680 | tf_op jit(solution)/shard_map/ppermute | solution.py:244
  38.7 1.9 %collective-permute-start.4 = (bf16[88,1024]{1,0:T(8,128)(2,1)S(1)}, bf16[88,1024]{1,0:T(8,128)(2,1)S(1)}, u32[]{:S(2)}, u32[]{:S(2)}) collective-permute-start(bf16[88,1024]{1,0:T(8,128)(2,1)S(1)} %get-tuple-element.42), channel_id=1, source_target_pairs={{8,0},{9,1},{10,2},{11,3},{12,4},{13,5},{14,6},{15,7},{16,8},{17,9... | collective-permute-start | bytes 540680 | tf_op jit(solution)/shard_map/ppermute | solution.py:244
  40.6 2.2 %expert.4 = (bf16[80,1024]{1,0:T(8,128)(2,1)S(1)}, bf16[80,384]{1,0:T(8,128)(2,1)S(1)}, bf16[80,384]{1,0:T(8,128)(2,1)S(1)}, bf16[80,384]{1,0:T(8,128)(2,1)S(1)}) custom-call(bf16[80,2048]{1,0:T(8,128)(2,1)S(1)} %collective-permute-done.5.refs_0_.refs_4_, bf16[24,2048]{1,0:T(8,128)(2,1)S(1)} %collective-permute-done.6.refs_1_.refs_5_, ...), custom_call_target="tpu_custom_call" | custom-call | flops 1 | bytes 1 | tf_op jit(solution)/shard_map/expert/pallas_call | solution.py:133
  42.9 2.0 %collective-permute-start.13 = (bf16[80,1024]{1,0:T(8,128)(2,1)S(1)}, bf16[80,1024]{1,0:T(8,128)(2,1)S(1)}, u32[]{:S(2)}, u32[]{:S(2)}) collective-permute-start(bf16[80,1024]{1,0:T(8,128)(2,1)S(1)} %get-tuple-element.67), channel_id=1, source_target_pairs={{8,4},{9,5},{10,6},{11,7},{12,0},{13,1},{14,2},{15,3},{16,12},{17,... | collective-permute-start | bytes 491528 | tf_op jit(solution)/shard_map/ppermute | solution.py:244
  44.9 2.2 %expert.5 = (bf16[80,1024]{1,0:T(8,128)(2,1)S(1)}, bf16[80,384]{1,0:T(8,128)(2,1)S(1)}, bf16[80,384]{1,0:T(8,128)(2,1)S(1)}, bf16[80,384]{1,0:T(8,128)(2,1)S(1)}) custom-call(bf16[40,2048]{1,0:T(8,128)(2,1)S(1)} %collective-permute-done.8.refs_0_.refs_7_, bf16[40,2048]{1,0:T(8,128)(2,1)S(1)} %collective-permute-done.9.refs_1_.refs_8_, ...), custom_call_target="tpu_custom_call" | custom-call | flops 1 | bytes 1 | tf_op jit(solution)/shard_map/expert/pallas_call | solution.py:133
  47.2 1.9 %collective-permute-start.15 = (bf16[80,1024]{1,0:T(8,128)(2,1)S(1)}, bf16[80,1024]{1,0:T(8,128)(2,1)S(1)}, u32[]{:S(2)}, u32[]{:S(2)}) collective-permute-start(bf16[80,1024]{1,0:T(8,128)(2,1)S(1)} %get-tuple-element.69), channel_id=1, source_target_pairs={{8,6},{9,7},{10,4},{11,5},{12,2},{13,3},{14,0},{15,1},{16,14},{17,... | collective-permute-start | bytes 491528 | tf_op jit(solution)/shard_map/ppermute | solution.py:244
  49.1 4.1 %weight_grads.1 = (bf16[2048,384]{1,0:T(8,128)(2,1)}, bf16[2048,384]{1,0:T(8,128)(2,1)}, bf16[384,2048]{1,0:T(8,128)(2,1)}) custom-call(bf16[40,2048]{1,0:T(8,128)(2,1)S(1)} %get-tuple-element.38.refs_1_.refs_0_, bf16[40,2048]{1,0:T(8,128)(2,1)S(1)} %collective-permute-done.1.refs_2_.refs_1_, bf16[80,2048]{1,0:T(8,128)(2,1)S(1)} %collective-permute-done.2.refs_3_.refs_2_, ...), custom_call_target="tpu_custom_call" | custom-call | flops 1 | bytes 1 | tf_op jit(solution)/shard_map/weight_grads/pallas_call | solution.py:165
  53.3 2.3 %collective-permute-done.13.refs_4_ = bf16[80,1024]{1,0:T(8,128)(2,1)S(1)} collective-permute-done((bf16[80,1024]{1,0:T(8,128)(2,1)S(1)}, bf16[80,1024]{1,0:T(8,128)(2,1)S(1)}, u32[]{:S(2)}, u32[]{:S(2)}) %collective-permute-start.13) | collective-permute-done | bytes 163872 | tf_op jit(solution)/shard_map/ppermute | solution.py:244
  55.6 1.1 %collective-permute-start.14 = (bf16[40,1024]{1,0:T(8,128)(2,1)S(1)}, bf16[40,1024]{1,0:T(8,128)(2,1)S(1)}, u32[]{:S(2)}, u32[]{:S(2)}) collective-permute-start(bf16[40,1024]{1,0:T(8,128)(2,1)S(1)} %slice.26), channel_id=1, source_target_pairs={{0,1},{1,0},{2,3},{3,2},{4,5},{5,4},{6,7},{7,6},{8,9},{9,8},{10,11... | collective-permute-start | bytes 245768 | tf_op jit(solution)/shard_map/ppermute | solution.py:236
  57.2 4.5 %collective-permute-done.15.refs_6_ = bf16[80,1024]{1,0:T(8,128)(2,1)S(1)} collective-permute-done((bf16[80,1024]{1,0:T(8,128)(2,1)S(1)}, bf16[80,1024]{1,0:T(8,128)(2,1)S(1)}, u32[]{:S(2)}, u32[]{:S(2)}) %collective-permute-start.15) | collective-permute-done | bytes 163872 | tf_op jit(solution)/shard_map/ppermute | solution.py:244
  61.7 1.1 %collective-permute-start.16 = (bf16[40,1024]{1,0:T(8,128)(2,1)S(1)}, bf16[40,1024]{1,0:T(8,128)(2,1)S(1)}, u32[]{:S(2)}, u32[]{:S(2)}) collective-permute-start(bf16[40,1024]{1,0:T(8,128)(2,1)S(1)} %slice.31), channel_id=1, source_target_pairs={{0,1},{1,0},{2,3},{3,2},{4,5},{5,4},{6,7},{7,6},{8,9},{9,8},{10,11... | collective-permute-start | bytes 245768 | tf_op jit(solution)/shard_map/ppermute | solution.py:236
  63.8 1.9 %combine.1 = bf16[256,2048]{1,0:T(8,128)(2,1)} custom-call(bf16[256,2048]{1,0:T(8,128)(2,1)S(1)} %collective-permute-done.grad_ref, bf16[88,1024]{1,0:T(8,128)(2,1)S(1)} %collective-permute-done.4.refs_0_, bf16[40,1024]{1,0:T(8,128)(2,1)S(1)} %collective-permute-done.11.refs_1_, bf16[88,1024]{1,0:T(8,128)(2,1)S(1)} %collective-permute-done.10.refs_2_, ...), custom_call_target="tpu_custom_call" | custom-call | flops 1 | bytes 1 | tf_op jit(solution)/shard_map/combine/pallas_call | solution.py:202
  (34 shorter events, 3.9 us)
Async XLA Ops:
  0.6 27.3 %copy-start = (bf16[1,1,2048,384]{3,2,1,0:T(8,128)(2,1)S(1)}, bf16[1,1,2048,384]{3,2,1,0:T(8,128)(2,1)}, u32[]{:S(2)}) copy-start(bf16[1,1,2048,384]{3,2,1,0:T(8,128)(2,1)} %param.15) | copy-start | bytes 4718596
  1.5 1.2 %copy-start.3 = (bf16[1,256,2048]{2,1,0:T(8,128)(2,1)S(1)}, bf16[1,256,2048]{2,1,0:T(8,128)(2,1)}, u32[]{:S(2)}) copy-start(bf16[1,256,2048]{2,1,0:T(8,128)(2,1)} %param.9) | copy-start | bytes 3145732
  2.7 0.7 %copy-start.4 = (f32[1,256,8]{1,2,0:T(8,128)S(1)}, f32[1,256,8]{1,2,0:T(8,128)}, u32[]{:S(2)}) copy-start(f32[1,256,8]{1,2,0:T(8,128)} %param.11) | copy-start | bytes 24580
  5.8 39.1 %collective-permute-start = (bf16[256,2048]{1,0:T(8,128)(2,1)}, bf16[256,2048]{1,0:T(8,128)(2,1)S(1)}, u32[]{:S(2)}, u32[]{:S(2)}) collective-permute-start(bf16[256,2048]{1,0:T(8,128)(2,1)} %bitcast.grad_ref), channel_id=1, source_target_pairs={{8,0},{9,1},{10,2},{11,3},{12,4},{13,5},{14,6},{15,7},{16,8},{17,9... | collective-permute-start | bytes 3145736 | tf_op jit(solution)/shard_map/ppermute | solution.py:244
  8.9 13.2 %collective-permute-start.2 = (bf16[80,2048]{1,0:T(8,128)(2,1)S(1)}, bf16[80,2048]{1,0:T(8,128)(2,1)S(1)}, u32[]{:S(2)}, u32[]{:S(2)}) collective-permute-start(bf16[80,2048]{1,0:T(8,128)(2,1)S(1)} %get-tuple-element.41), channel_id=1, source_target_pairs={{0,2},{1,3},{2,0},{3,1},{4,6},{5,7},{6,4},{7,5},{8,10},{9,11},{10,... | collective-permute-start | bytes 983048 | tf_op jit(solution)/shard_map/ppermute | solution.py:236
  9.1 16.2 %collective-permute-start.5 = (bf16[80,2048]{1,0:T(8,128)(2,1)S(1)}, bf16[80,2048]{1,0:T(8,128)(2,1)S(1)}, u32[]{:S(2)}, u32[]{:S(2)}) collective-permute-start(bf16[80,2048]{1,0:T(8,128)(2,1)S(1)} %get-tuple-element.43), channel_id=1, source_target_pairs={{0,4},{1,5},{2,6},{3,7},{4,0},{5,1},{6,2},{7,3},{8,12},{9,13},{10,... | collective-permute-start | bytes 983048 | tf_op jit(solution)/shard_map/ppermute | solution.py:236
  11.4 15.9 %collective-permute-start.1 = (bf16[40,2048]{1,0:T(8,128)(2,1)S(1)}, bf16[40,2048]{1,0:T(8,128)(2,1)S(1)}, u32[]{:S(2)}, u32[]{:S(2)}) collective-permute-start(bf16[40,2048]{1,0:T(8,128)(2,1)S(1)} %get-tuple-element.40), channel_id=1, source_target_pairs={{0,1},{1,0},{2,3},{3,2},{4,5},{5,4},{6,7},{7,6},{8,9},{9,8},{10,11... | collective-permute-start | bytes 491528 | tf_op jit(solution)/shard_map/ppermute | solution.py:236
  22.1 5.3 %collective-permute-start.3 = (bf16[40,2048]{1,0:T(8,128)(2,1)S(1)}, bf16[40,2048]{1,0:T(8,128)(2,1)S(1)}, u32[]{:S(2)}, u32[]{:S(2)}) collective-permute-start(bf16[40,2048]{1,0:T(8,128)(2,1)S(1)} %slice.28), channel_id=1, source_target_pairs={{0,1},{1,0},{2,3},{3,2},{4,5},{5,4},{6,7},{7,6},{8,9},{9,8},{10,11... | collective-permute-start | bytes 491528 | tf_op jit(solution)/shard_map/ppermute | solution.py:236
  24.0 18.8 %collective-permute-start.8 = (bf16[40,2048]{1,0:T(8,128)(2,1)S(1)}, bf16[40,2048]{1,0:T(8,128)(2,1)S(1)}, u32[]{:S(2)}, u32[]{:S(2)}) collective-permute-start(bf16[40,2048]{1,0:T(8,128)(2,1)S(1)} %get-tuple-element.50), channel_id=1, source_target_pairs={{0,6},{1,7},{2,4},{3,5},{4,2},{5,3},{6,0},{7,1},{8,14},{9,15},{10,... | collective-permute-start | bytes 491528 | tf_op jit(solution)/shard_map/ppermute | solution.py:236
  25.3 19.6 %collective-permute-start.9 = (bf16[40,2048]{1,0:T(8,128)(2,1)S(1)}, bf16[40,2048]{1,0:T(8,128)(2,1)S(1)}, u32[]{:S(2)}, u32[]{:S(2)}) collective-permute-start(bf16[40,2048]{1,0:T(8,128)(2,1)S(1)} %get-tuple-element.51), channel_id=1, source_target_pairs={{0,7},{1,6},{2,5},{3,4},{4,3},{5,2},{6,1},{7,0},{8,15},{9,14},{10,... | collective-permute-start | bytes 491528 | tf_op jit(solution)/shard_map/ppermute | solution.py:236
  27.3 11.4 %collective-permute-start.6 = (bf16[24,2048]{1,0:T(8,128)(2,1)S(1)}, bf16[24,2048]{1,0:T(8,128)(2,1)S(1)}, u32[]{:S(2)}, u32[]{:S(2)}) collective-permute-start(bf16[24,2048]{1,0:T(8,128)(2,1)S(1)} %slice.29), channel_id=1, source_target_pairs={{0,1},{1,0},{2,3},{3,2},{4,5},{5,4},{6,7},{7,6},{8,9},{9,8},{10,11... | collective-permute-start | bytes 294920 | tf_op jit(solution)/shard_map/ppermute | solution.py:236
  27.4 6.0 %collective-permute-start.7 = (bf16[16,2048]{1,0:T(8,128)(2,1)S(1)}, bf16[16,2048]{1,0:T(8,128)(2,1)S(1)}, u32[]{:S(2)}, u32[]{:S(2)}) collective-permute-start(bf16[16,2048]{1,0:T(8,128)(2,1)S(1)} %slice.30), channel_id=1, source_target_pairs={{0,1},{1,0},{2,3},{3,2},{4,5},{5,4},{6,7},{7,6},{8,9},{9,8},{10,11... | collective-permute-start | bytes 196616 | tf_op jit(solution)/shard_map/ppermute | solution.py:236
  27.9 1.4 %copy-start.1 = (bf16[1,1,2048,384]{3,2,1,0:T(8,128)(2,1)S(1)}, bf16[1,1,2048,384]{3,2,1,0:T(8,128)(2,1)}, u32[]{:S(2)}) copy-start(bf16[1,1,2048,384]{3,2,1,0:T(8,128)(2,1)} %param.16) | copy-start | bytes 4718596
  29.3 1.4 %copy-start.2 = (bf16[1,1,384,2048]{3,2,1,0:T(8,128)(2,1)S(1)}, bf16[1,1,384,2048]{3,2,1,0:T(8,128)(2,1)}, u32[]{:S(2)}) copy-start(bf16[1,1,384,2048]{3,2,1,0:T(8,128)(2,1)} %param.17) | copy-start | bytes 4718596
  33.4 15.7 %collective-permute-start.10 = (bf16[88,1024]{1,0:T(8,128)(2,1)S(1)}, bf16[88,1024]{1,0:T(8,128)(2,1)S(1)}, u32[]{:S(2)}, u32[]{:S(2)}) collective-permute-start(bf16[88,1024]{1,0:T(8,128)(2,1)S(1)} %get-tuple-element.57), channel_id=1, source_target_pairs={{8,2},{9,3},{10,0},{11,1},{12,6},{13,7},{14,4},{15,5},{16,10},{17,... | collective-permute-start | bytes 540680 | tf_op jit(solution)/shard_map/ppermute | solution.py:244
  38.7 10.4 %collective-permute-start.4 = (bf16[88,1024]{1,0:T(8,128)(2,1)S(1)}, bf16[88,1024]{1,0:T(8,128)(2,1)S(1)}, u32[]{:S(2)}, u32[]{:S(2)}) collective-permute-start(bf16[88,1024]{1,0:T(8,128)(2,1)S(1)} %get-tuple-element.42), channel_id=1, source_target_pairs={{8,0},{9,1},{10,2},{11,3},{12,4},{13,5},{14,6},{15,7},{16,8},{17,9... | collective-permute-start | bytes 540680 | tf_op jit(solution)/shard_map/ppermute | solution.py:244
  42.9 12.7 %collective-permute-start.13 = (bf16[80,1024]{1,0:T(8,128)(2,1)S(1)}, bf16[80,1024]{1,0:T(8,128)(2,1)S(1)}, u32[]{:S(2)}, u32[]{:S(2)}) collective-permute-start(bf16[80,1024]{1,0:T(8,128)(2,1)S(1)} %get-tuple-element.67), channel_id=1, source_target_pairs={{8,4},{9,5},{10,6},{11,7},{12,0},{13,1},{14,2},{15,3},{16,12},{17,... | collective-permute-start | bytes 491528 | tf_op jit(solution)/shard_map/ppermute | solution.py:244
  47.2 14.5 %collective-permute-start.15 = (bf16[80,1024]{1,0:T(8,128)(2,1)S(1)}, bf16[80,1024]{1,0:T(8,128)(2,1)S(1)}, u32[]{:S(2)}, u32[]{:S(2)}) collective-permute-start(bf16[80,1024]{1,0:T(8,128)(2,1)S(1)} %get-tuple-element.69), channel_id=1, source_target_pairs={{8,6},{9,7},{10,4},{11,5},{12,2},{13,3},{14,0},{15,1},{16,14},{17,... | collective-permute-start | bytes 491528 | tf_op jit(solution)/shard_map/ppermute | solution.py:244
  55.6 7.2 %collective-permute-start.14 = (bf16[40,1024]{1,0:T(8,128)(2,1)S(1)}, bf16[40,1024]{1,0:T(8,128)(2,1)S(1)}, u32[]{:S(2)}, u32[]{:S(2)}) collective-permute-start(bf16[40,1024]{1,0:T(8,128)(2,1)S(1)} %slice.26), channel_id=1, source_target_pairs={{0,1},{1,0},{2,3},{3,2},{4,5},{5,4},{6,7},{7,6},{8,9},{9,8},{10,11... | collective-permute-start | bytes 245768 | tf_op jit(solution)/shard_map/ppermute | solution.py:236
  56.7 6.2 %collective-permute-start.12 = (bf16[40,1024]{1,0:T(8,128)(2,1)S(1)}, bf16[40,1024]{1,0:T(8,128)(2,1)S(1)}, u32[]{:S(2)}, u32[]{:S(2)}) collective-permute-start(bf16[40,1024]{1,0:T(8,128)(2,1)S(1)} %slice.25), channel_id=1, source_target_pairs={{0,1},{1,0},{2,3},{3,2},{4,5},{5,4},{6,7},{7,6},{8,9},{9,8},{10,11... | collective-permute-start | bytes 245768 | tf_op jit(solution)/shard_map/ppermute | solution.py:236
  56.8 6.1 %collective-permute-start.11 = (bf16[40,1024]{1,0:T(8,128)(2,1)S(1)}, bf16[40,1024]{1,0:T(8,128)(2,1)S(1)}, u32[]{:S(2)}, u32[]{:S(2)}) collective-permute-start(bf16[40,1024]{1,0:T(8,128)(2,1)S(1)} %slice.24), channel_id=1, source_target_pairs={{0,1},{1,0},{2,3},{3,2},{4,5},{5,4},{6,7},{7,6},{8,9},{9,8},{10,11... | collective-permute-start | bytes 245768 | tf_op jit(solution)/shard_map/ppermute | solution.py:236
  61.7 2.1 %collective-permute-start.16 = (bf16[40,1024]{1,0:T(8,128)(2,1)S(1)}, bf16[40,1024]{1,0:T(8,128)(2,1)S(1)}, u32[]{:S(2)}, u32[]{:S(2)}) collective-permute-start(bf16[40,1024]{1,0:T(8,128)(2,1)S(1)} %slice.31), channel_id=1, source_target_pairs={{0,1},{1,0},{2,3},{3,2},{4,5},{5,4},{6,7},{7,6},{8,9},{9,8},{10,11... | collective-permute-start | bytes 245768 | tf_op jit(solution)/shard_map/ppermute | solution.py:236

commit v4 on v3

--- a/solution.py
+++ b/solution.py
@@ -29,8 +29,30 @@
     return [keys[k : k + 1, :] == slot for k in range(keys.shape[0])]
 
 
-def gather_kernel(keys_ref, weight_ref, in_ref, grad_ref, *outs):
-    keys = keys_ref[...]
+def gather_kernel(n_expert, ids_hbm, slot_hbm, dropped_hbm, weight_hbm, in_hbm, grad_hbm, keys_ref, *refs):
+    outs, (ids_ref, slot_ref, dropped_ref, weight_ref, in_ref, grad_ref, sem) = refs[:-7], refs[-7:]
+    copies = [
+        pltpu.make_async_copy(src, dst, sem.at[i])
+        for i, (src, dst) in enumerate(
+            (
+                (ids_hbm, ids_ref),
+                (slot_hbm, slot_ref),
+                (dropped_hbm, dropped_ref),
+                (weight_hbm, weight_ref),
+                (in_hbm, in_ref),
+                (grad_hbm, grad_ref),
+            )
+        )
+    ]
+    for copy in copies:
+        copy.start()
+    me = lax.axis_index("expert")
+    for copy in copies[:4]:
+        copy.wait()
+    ids = ids_ref[...]
+    live = (ids < n_expert) & (dropped_ref[...] == 0)
+    keys = jnp.where(live, (ids ^ me) * PAIR + slot_ref[...], -1)
+    keys_ref[...] = keys
     weight = weight_ref[...]
     rows = sum(out.shape[0] for out in outs)
     tokens = keys.shape[1]
@@ -43,7 +65,9 @@
     pick_in = jnp.where(first, own, 0.0).astype(BF16)
     pick_grad = jnp.where(first, 0.0, own).astype(BF16)
     row_weight = jnp.sum(scaled, axis=1, keepdims=True)
+    copies[4].wait()
     got = jnp.dot(pick_in, in_ref[...], preferred_element_type=F32)
+    copies[5].wait()
     got = got + row_weight * jnp.dot(pick_grad, grad_ref[...], preferred_element_type=F32)
     got = got.astype(BF16)
     start = 0
@@ -52,20 +76,48 @@
         start += out.shape[0]
 
 
-def gather(keys, weight, inputs, grads, chips, apart):
-    width = inputs.shape[1]
+def gather(ids, slots, dropped, weight, inputs, grads, chips, apart):
+    tokens, width = inputs.shape
+    ranks = ids.shape[0]
     sizes = [n for c in range(chips) for n in ([PAIR, PAIR] if c in apart else [2 * PAIR])]
     outs = pl.pallas_call(
-        gather_kernel,
-        out_shape=[jax.ShapeDtypeStruct((n, width), BF16) for n in sizes],
-        in_specs=vmem(4),
-        out_specs=vmem(len(sizes)),
+        functools.partial(gather_kernel, 2 * chips),
+        out_shape=[jax.ShapeDtypeStruct((ranks, tokens), jnp.int32)]
+        + [jax.ShapeDtypeStruct((n, width), BF16) for n in sizes],
+        in_specs=[pl.BlockSpec(memory_space=pltpu.HBM)] * 6,
+        out_specs=vmem(1 + len(sizes)),
+        scratch_shapes=[pltpu.VMEM((ranks, tokens), jnp.int32)] * 3
+        + [pltpu.VMEM((ranks, tokens), F32)]
+        + [pltpu.VMEM((tokens, width), BF16)] * 2
+        + [pltpu.SemaphoreType.DMA((6,))],
         name="gather",
         compiler_params=pltpu.CompilerParams(vmem_limit_bytes=16 << 20),
         cost_estimate=SHORT,
-    )(keys, weight, inputs, grads)
-    outs = list(outs)
-    return [[outs.pop(0), outs.pop(0)] if c in apart else outs.pop(0) for c in range(chips)]
+    )(*(pltpu.with_memory_space_constraint(a, pltpu.HBM) for a in (ids, slots, dropped, weight, inputs, grads)))
+    keys, *outs = outs
+    return keys, [[outs.pop(0), outs.pop(0)] if c in apart else outs.pop(0) for c in range(chips)]
+
+
+def load_kernel(count, *refs):
+    sem = refs[-1]
+    copies = [pltpu.make_async_copy(refs[i], refs[count + i], sem.at[i]) for i in range(count)]
+    for copy in copies:
+        copy.start()
+    for copy in copies:
+        copy.wait()
+
+
+def load(*arrays):
+    return pl.pallas_call(
+        functools.partial(load_kernel, len(arrays)),
+        out_shape=[jax.ShapeDtypeStruct(a.shape, a.dtype) for a in arrays],
+        in_specs=[pl.BlockSpec(memory_space=pltpu.HBM)] * len(arrays),
+        out_specs=vmem(len(arrays)),
+        scratch_shapes=[pltpu.SemaphoreType.DMA((len(arrays),))],
+        name="load",
+        compiler_params=pltpu.CompilerParams(vmem_limit_bytes=12 << 20),
+        cost_estimate=SHORT,
+    )(*arrays)
 
 
 def nt(a, b):
@@ -229,7 +281,6 @@
     width, hidden = w_gate.shape
     n_expert = lax.axis_size("expert")
     n_pipe = lax.axis_size("pipe")
-    me = lax.axis_index("expert")
     both_axes = ("pipe", "expert")
 
     def to_partner(value, k):
@@ -243,15 +294,12 @@
         ]
         return lax.ppermute(value, both_axes, pairs)
 
-    live = (expert_ids[0] < n_expert) & (dropped[0] == 0)
-    key = jnp.where(live, (expert_ids[0] ^ me) * PAIR + slot_pos[0], -1)
-    keys = jnp.transpose(key)
-    weight = jnp.transpose(route_weight[0])
     chips = n_expert // 2
     near = list(range(1, chips // 2))
     early = list(range(chips // 2, 3 * chips // 4))
     late = list(range(3 * chips // 4, chips))
-    sent = gather(keys, weight, inputs, grads, chips, [0] + late)
+    by_rank = [jnp.transpose(a[0]) for a in (expert_ids, slot_pos, dropped, route_weight)]
+    keys, sent = gather(*by_rank, inputs, grads, chips, [0] + late)
     mine = (0, PAIR)
 
     def after(values, event):
@@ -285,8 +333,10 @@
     beside = to_partner(sent[0][1], 1)
     next_grads = to_before(after(grads, sent[0][0]), 0)
     pieces = [(sent[0][0], mine), (beside, mine)]
-    for c in near:
-        pieces += forward(arrived[c])
+    w_gate, w_up, w_down = load(*after((w_gate, w_up, w_down), sent[0][0]))
+    here = after([arrived[c] for c in near], w_down)
+    for value in here:
+        pieces += forward(value)
     parts = process([0] + near, pieces, keys=keys)
     pieces = [piece for c in early for piece in forward(arrived[c], PAIR + 24)]
     parts = process(early, gated(pieces, parts))

time: 66 us -> 60.5 us (0.917)
  waiting for transfers between devices: 16.9 us -> 13.6 us
  local copies, waits for them, and re-layouts: 4.79 us -> 2.87 us
  other arithmetic: 0.85 us -> 0 us
    ppermute x12, waiting for transfers between devices: 10.1 us -> 6.9 us  [to_partner(): return lax.ppermute(value, 'expert', [(i, i ^ k) for i in range(n_expert)])]
    unnamed x10 -> x6, local copies, waits for them, and re-layouts: 4.74 us -> 2.82 us
    transpose x1 -> x0, other arithmetic: 0.85 us -> none  [per_device(): keys = jnp.transpose(key)]
    pallas_call x1 -> x2, Pallas kernels: 2.37 us -> 2.98 us  [the longest x1 2.64 us: gather(): pl.pallas_call(functools.partial(gather_kernel, 2 * chips), out_shape=[ja...]
  transfers between devices with their start and end apart: 17 -> 17, of which waited for: 4 -> 4; matrix products, arithmetic and copies ran while one was open for 0% -> 0% of each run, Pallas kernels for 17% -> 19%
where the time goes in v4:
time: 60.5 us; the launch traced here: 60.3 us
  starting transfers between devices  27 us (45%)
  Pallas kernels  16 us (26%)
  waiting for transfers between devices  13.6 us (22%)
  local copies, waits for them, and re-layouts  2.87 us (5%)
  between operations  0.82 us (1%)
    ppermute x5, starting transfers between devices, to_before(): return lax.ppermute(value, both_axes, pairs)  14.4 us
    ppermute x12, starting transfers between devices, to_partner(): return lax.ppermute(value, 'expert', [(i, i ^ k) for i in range(n_expert)])  12.6 us
    pallas_call x3, Pallas kernels, expert_chunk(): pl.pallas_call(functools.partial(expert_kernel, spans, bool(extra)), out_...  6.98 us
    ppermute x12, waiting for transfers between devices, to_partner(): return lax.ppermute(value, 'expert', [(i, i ^ k) for i in range(n_expert)])  6.9 us
    ppermute x5, waiting for transfers between devices, to_before(): return lax.ppermute(value, both_axes, pairs)  6.67 us
    pallas_call x1, Pallas kernels, weight_grads(): pl.pallas_call(functools.partial(weight_kernel, spans, chunks), out_shape...  4.15 us
    unnamed x6, local copies, waits for them, and re-layouts  2.82 us
    pallas_call x1, Pallas kernels, gather(): pl.pallas_call(functools.partial(gather_kernel, 2 * chips), out_shape=[ja...  2.64 us
  transfers between devices with their start and end apart: 17, of which 4 were waited for; matrix products, arithmetic and copies ran while one was open for 0% of the time, Pallas kernels for 19%

profile of v4, /device:TPU:13, one launch (start us, length us, event | category | flops | bytes accessed | tf_op | source)
XLA Modules:
  0.0 60.3 jit_solution(17015637276397180220)
XLA Ops:
  0.6 2.6 %gather.1 = (s32[8,256]{1,0:T(8,128)S(1)}, bf16[40,2048]{1,0:T(8,128)(2,1)S(1)}, bf16[40,2048]{1,0:T(8,128)(2,1)S(1)}, bf16[80,2048]{1,0:T(8,128)(2,1)S(1)}, bf1...) custom-call(s32[8,256]{1,0:T(8,128)} %bitcast.28, s32[8,256]{1,0:T(8,128)} %bitcast.29, ...), custom_call_target="tpu_custom_call" | custom-call | flops 1 | bytes 1 | tf_op jit(solution)/shard_map/gather/pallas_call | solution.py:83
  3.3 3.1 %collective-permute-start = (bf16[256,2048]{1,0:T(8,128)(2,1)}, bf16[256,2048]{1,0:T(8,128)(2,1)S(1)}, u32[]{:S(2)}, u32[]{:S(2)}) collective-permute-start(bf16[256,2048]{1,0:T(8,128)(2,1)} %bitcast.27), channel_id=1, source_target_pairs={{8,0},{9,1},{10,2},{11,3},{12,4},{13,5},{14,6},{15,7},{16,8},{17,9... | collective-permute-start | bytes 3145736 | tf_op jit(solution)/shard_map/ppermute | solution.py:295
  6.6 2.3 %collective-permute-start.5 = (bf16[80,2048]{1,0:T(8,128)(2,1)S(1)}, bf16[80,2048]{1,0:T(8,128)(2,1)S(1)}, u32[]{:S(2)}, u32[]{:S(2)}) collective-permute-start(bf16[80,2048]{1,0:T(8,128)(2,1)S(1)} %get-tuple-element.59), channel_id=1, source_target_pairs={{0,4},{1,5},{2,6},{3,7},{4,0},{5,1},{6,2},{7,3},{8,12},{9,13},{10,... | collective-permute-start | bytes 983048 | tf_op jit(solution)/shard_map/ppermute | solution.py:287
  8.9 1.5 %collective-permute-start.1 = (bf16[40,2048]{1,0:T(8,128)(2,1)S(1)}, bf16[40,2048]{1,0:T(8,128)(2,1)S(1)}, u32[]{:S(2)}, u32[]{:S(2)}) collective-permute-start(bf16[40,2048]{1,0:T(8,128)(2,1)S(1)} %get-tuple-element.49), channel_id=1, source_target_pairs={{0,1},{1,0},{2,3},{3,2},{4,5},{5,4},{6,7},{7,6},{8,9},{9,8},{10,11... | collective-permute-start | bytes 491528 | tf_op jit(solution)/shard_map/ppermute | solution.py:287
  10.4 1.4 %copy-done.1 = bf16[1,1,2048,384]{3,2,1,0:T(8,128)(2,1)S(1)} copy-done((bf16[1,1,2048,384]{3,2,1,0:T(8,128)(2,1)S(1)}, bf16[1,1,2048,384]{3,2,1,0:T(8,128)(2,1)}, u32[]{:S(2)}) %copy-start.1) | copy-done | bytes 1572888
  11.8 1.4 %copy-done.2 = bf16[1,1,384,2048]{3,2,1,0:T(8,128)(2,1)S(1)} copy-done((bf16[1,1,384,2048]{3,2,1,0:T(8,128)(2,1)S(1)}, bf16[1,1,384,2048]{3,2,1,0:T(8,128)(2,1)}, u32[]{:S(2)}) %copy-start.2) | copy-done | bytes 1572888
  13.6 6.0 %collective-permute-done.2.refs_3_.refs_2_ = bf16[80,2048]{1,0:T(8,128)(2,1)S(1)} collective-permute-done((bf16[80,2048]{1,0:T(8,128)(2,1)S(1)}, bf16[80,2048]{1,0:T(8,128)(2,1)S(1)}, u32[]{:S(2)}, u32[]{:S(2)}) %collective-permute-start.2) | collective-permute-done | bytes 327712 | tf_op jit(solution)/shard_map/ppermute | solution.py:287
  19.6 1.9 %collective-permute-start.3 = (bf16[40,2048]{1,0:T(8,128)(2,1)S(1)}, bf16[40,2048]{1,0:T(8,128)(2,1)S(1)}, u32[]{:S(2)}, u32[]{:S(2)}) collective-permute-start(bf16[40,2048]{1,0:T(8,128)(2,1)S(1)} %slice.21), channel_id=1, source_target_pairs={{0,1},{1,0},{2,3},{3,2},{4,5},{5,4},{6,7},{7,6},{8,9},{9,8},{10,11... | collective-permute-start | bytes 491528 | tf_op jit(solution)/shard_map/ppermute | solution.py:287
  21.5 1.3 %collective-permute-start.8 = (bf16[40,2048]{1,0:T(8,128)(2,1)S(1)}, bf16[40,2048]{1,0:T(8,128)(2,1)S(1)}, u32[]{:S(2)}, u32[]{:S(2)}) collective-permute-start(bf16[40,2048]{1,0:T(8,128)(2,1)S(1)} %get-tuple-element.66), channel_id=1, source_target_pairs={{0,6},{1,7},{2,4},{3,5},{4,2},{5,3},{6,0},{7,1},{8,14},{9,15},{10,... | collective-permute-start | bytes 491528 | tf_op jit(solution)/shard_map/ppermute | solution.py:287
  22.8 1.9 %collective-permute-start.9 = (bf16[40,2048]{1,0:T(8,128)(2,1)S(1)}, bf16[40,2048]{1,0:T(8,128)(2,1)S(1)}, u32[]{:S(2)}, u32[]{:S(2)}) collective-permute-start(bf16[40,2048]{1,0:T(8,128)(2,1)S(1)} %get-tuple-element.67), channel_id=1, source_target_pairs={{0,7},{1,6},{2,5},{3,4},{4,3},{5,2},{6,1},{7,0},{8,15},{9,14},{10,... | collective-permute-start | bytes 491528 | tf_op jit(solution)/shard_map/ppermute | solution.py:287
  25.4 2.6 %expert.3 = (bf16[88,1024]{1,0:T(8,128)(2,1)S(1)}, bf16[88,1024]{1,0:T(8,128)(2,1)S(1)}, bf16[160,384]{1,0:T(8,128)(2,1)S(1)}, bf16[160,384]{1,0:T(8,128)(2,1)S(1)}, bf16[160,384]{1,0:T(8,128)(2,1)S(1)}) custom-call(s32[8,256]{1,0:T(8,128)S(1)} %get-tuple-element.48.refs_0_, bf16[40,2048]{1,0:T(8,128)(2,1)S(1)} %get-tuple-element.46.refs_1_.refs_0_, ...), custom_call_target="tpu_custom_call" | custom-call | flops 1 | bytes 1 | tf_op jit(solution)/shard_map/expert/pallas_call | solution.py:185
  28.0 5.3 %collective-permute-start.10 = (bf16[88,1024]{1,0:T(8,128)(2,1)S(1)}, bf16[88,1024]{1,0:T(8,128)(2,1)S(1)}, u32[]{:S(2)}, u32[]{:S(2)}) collective-permute-start(bf16[88,1024]{1,0:T(8,128)(2,1)S(1)} %get-tuple-element.73), channel_id=1, source_target_pairs={{8,2},{9,3},{10,0},{11,1},{12,6},{13,7},{14,4},{15,5},{16,10},{17,... | collective-permute-start | bytes 540680 | tf_op jit(solution)/shard_map/ppermute | solution.py:295
  33.3 1.9 %collective-permute-start.4 = (bf16[88,1024]{1,0:T(8,128)(2,1)S(1)}, bf16[88,1024]{1,0:T(8,128)(2,1)S(1)}, u32[]{:S(2)}, u32[]{:S(2)}) collective-permute-start(bf16[88,1024]{1,0:T(8,128)(2,1)S(1)} %get-tuple-element.58), channel_id=1, source_target_pairs={{8,0},{9,1},{10,2},{11,3},{12,4},{13,5},{14,6},{15,7},{16,8},{17,9... | collective-permute-start | bytes 540680 | tf_op jit(solution)/shard_map/ppermute | solution.py:295
  35.3 2.2 %expert.4 = (bf16[80,1024]{1,0:T(8,128)(2,1)S(1)}, bf16[80,384]{1,0:T(8,128)(2,1)S(1)}, bf16[80,384]{1,0:T(8,128)(2,1)S(1)}, bf16[80,384]{1,0:T(8,128)(2,1)S(1)}) custom-call(bf16[80,2048]{1,0:T(8,128)(2,1)S(1)} %collective-permute-done.5.refs_0_.refs_4_, bf16[24,2048]{1,0:T(8,128)(2,1)S(1)} %collective-permute-done.6.refs_1_.refs_5_, ...), custom_call_target="tpu_custom_call" | custom-call | flops 1 | bytes 1 | tf_op jit(solution)/shard_map/expert/pallas_call | solution.py:185
  37.5 2.0 %collective-permute-start.13 = (bf16[80,1024]{1,0:T(8,128)(2,1)S(1)}, bf16[80,1024]{1,0:T(8,128)(2,1)S(1)}, u32[]{:S(2)}, u32[]{:S(2)}) collective-permute-start(bf16[80,1024]{1,0:T(8,128)(2,1)S(1)} %get-tuple-element.83), channel_id=1, source_target_pairs={{8,4},{9,5},{10,6},{11,7},{12,0},{13,1},{14,2},{15,3},{16,12},{17,... | collective-permute-start | bytes 491528 | tf_op jit(solution)/shard_map/ppermute | solution.py:295
  39.5 2.2 %expert.5 = (bf16[80,1024]{1,0:T(8,128)(2,1)S(1)}, bf16[80,384]{1,0:T(8,128)(2,1)S(1)}, bf16[80,384]{1,0:T(8,128)(2,1)S(1)}, bf16[80,384]{1,0:T(8,128)(2,1)S(1)}) custom-call(bf16[40,2048]{1,0:T(8,128)(2,1)S(1)} %collective-permute-done.8.refs_0_.refs_7_, bf16[40,2048]{1,0:T(8,128)(2,1)S(1)} %collective-permute-done.9.refs_1_.refs_8_, ...), custom_call_target="tpu_custom_call" | custom-call | flops 1 | bytes 1 | tf_op jit(solution)/shard_map/expert/pallas_call | solution.py:185
  41.7 2.2 %collective-permute-start.15 = (bf16[80,1024]{1,0:T(8,128)(2,1)S(1)}, bf16[80,1024]{1,0:T(8,128)(2,1)S(1)}, u32[]{:S(2)}, u32[]{:S(2)}) collective-permute-start(bf16[80,1024]{1,0:T(8,128)(2,1)S(1)} %get-tuple-element.85), channel_id=1, source_target_pairs={{8,6},{9,7},{10,4},{11,5},{12,2},{13,3},{14,0},{15,1},{16,14},{17,... | collective-permute-start | bytes 491528 | tf_op jit(solution)/shard_map/ppermute | solution.py:295
  43.9 4.1 %weight_grads.1 = (bf16[2048,384]{1,0:T(8,128)(2,1)}, bf16[2048,384]{1,0:T(8,128)(2,1)}, bf16[384,2048]{1,0:T(8,128)(2,1)}) custom-call(bf16[40,2048]{1,0:T(8,128)(2,1)S(1)} %get-tuple-element.46.refs_1_.refs_0_, bf16[40,2048]{1,0:T(8,128)(2,1)S(1)} %collective-permute-done.1.refs_2_.refs_1_, bf16[80,2048]{1,0:T(8,128)(2,1)S(1)} %collective-permute-done.2.refs_3_.refs_2_, ...), custom_call_target="tpu_custom_call" | custom-call | flops 1 | bytes 1 | tf_op jit(solution)/shard_map/weight_grads/pallas_call | solution.py:217
  48.0 2.1 %collective-permute-done.13.refs_4_ = bf16[80,1024]{1,0:T(8,128)(2,1)S(1)} collective-permute-done((bf16[80,1024]{1,0:T(8,128)(2,1)S(1)}, bf16[80,1024]{1,0:T(8,128)(2,1)S(1)}, u32[]{:S(2)}, u32[]{:S(2)}) %collective-permute-start.13) | collective-permute-done | bytes 163872 | tf_op jit(solution)/shard_map/ppermute | solution.py:295
  50.1 1.1 %collective-permute-start.14 = (bf16[40,1024]{1,0:T(8,128)(2,1)S(1)}, bf16[40,1024]{1,0:T(8,128)(2,1)S(1)}, u32[]{:S(2)}, u32[]{:S(2)}) collective-permute-start(bf16[40,1024]{1,0:T(8,128)(2,1)S(1)} %slice.26), channel_id=1, source_target_pairs={{0,1},{1,0},{2,3},{3,2},{4,5},{5,4},{6,7},{7,6},{8,9},{9,8},{10,11... | collective-permute-start | bytes 245768 | tf_op jit(solution)/shard_map/ppermute | solution.py:287
  51.8 4.6 %collective-permute-done.15.refs_6_ = bf16[80,1024]{1,0:T(8,128)(2,1)S(1)} collective-permute-done((bf16[80,1024]{1,0:T(8,128)(2,1)S(1)}, bf16[80,1024]{1,0:T(8,128)(2,1)S(1)}, u32[]{:S(2)}, u32[]{:S(2)}) %collective-permute-start.15) | collective-permute-done | bytes 163872 | tf_op jit(solution)/shard_map/ppermute | solution.py:295
  56.3 1.1 %collective-permute-start.16 = (bf16[40,1024]{1,0:T(8,128)(2,1)S(1)}, bf16[40,1024]{1,0:T(8,128)(2,1)S(1)}, u32[]{:S(2)}, u32[]{:S(2)}) collective-permute-start(bf16[40,1024]{1,0:T(8,128)(2,1)S(1)} %slice.30), channel_id=1, source_target_pairs={{0,1},{1,0},{2,3},{3,2},{4,5},{5,4},{6,7},{7,6},{8,9},{9,8},{10,11... | collective-permute-start | bytes 245768 | tf_op jit(solution)/shard_map/ppermute | solution.py:287
  57.5 0.9 %collective-permute-done.16.refs_7_ = bf16[40,1024]{1,0:T(8,128)(2,1)S(1)} collective-permute-done((bf16[40,1024]{1,0:T(8,128)(2,1)S(1)}, bf16[40,1024]{1,0:T(8,128)(2,1)S(1)}, u32[]{:S(2)}, u32[]{:S(2)}) %collective-permute-start.16) | collective-permute-done | bytes 81952 | tf_op jit(solution)/shard_map/ppermute | solution.py:287
  58.4 1.9 %combine.1 = bf16[256,2048]{1,0:T(8,128)(2,1)} custom-call(bf16[256,2048]{1,0:T(8,128)(2,1)S(1)} %collective-permute-done.grad_ref, bf16[88,1024]{1,0:T(8,128)(2,1)S(1)} %collective-permute-done.4.refs_0_, bf16[40,1024]{1,0:T(8,128)(2,1)S(1)} %collective-permute-done.11.refs_1_, bf16[88,1024]{1,0:T(8,128)(2,1)S(1)} %collective-permute-done.10.refs_2_, ...), custom_call_target="tpu_custom_call" | custom-call | flops 1 | bytes 1 | tf_op jit(solution)/shard_map/combine/pallas_call | solution.py:254
  (30 shorter events, 1.8 us)
Async XLA Ops:
  0.6 9.8 %copy-start = (bf16[1,1,2048,384]{3,2,1,0:T(8,128)(2,1)S(1)}, bf16[1,1,2048,384]{3,2,1,0:T(8,128)(2,1)}, u32[]{:S(2)}) copy-start(bf16[1,1,2048,384]{3,2,1,0:T(8,128)(2,1)} %param.15) | copy-start | bytes 4718596
  3.3 36.2 %collective-permute-start = (bf16[256,2048]{1,0:T(8,128)(2,1)}, bf16[256,2048]{1,0:T(8,128)(2,1)S(1)}, u32[]{:S(2)}, u32[]{:S(2)}) collective-permute-start(bf16[256,2048]{1,0:T(8,128)(2,1)} %bitcast.27), channel_id=1, source_target_pairs={{8,0},{9,1},{10,2},{11,3},{12,4},{13,5},{14,6},{15,7},{16,8},{17,9... | collective-permute-start | bytes 3145736 | tf_op jit(solution)/shard_map/ppermute | solution.py:295
  6.4 13.2 %collective-permute-start.2 = (bf16[80,2048]{1,0:T(8,128)(2,1)S(1)}, bf16[80,2048]{1,0:T(8,128)(2,1)S(1)}, u32[]{:S(2)}, u32[]{:S(2)}) collective-permute-start(bf16[80,2048]{1,0:T(8,128)(2,1)S(1)} %get-tuple-element.50), channel_id=1, source_target_pairs={{0,2},{1,3},{2,0},{3,1},{4,6},{5,7},{6,4},{7,5},{8,10},{9,11},{10,... | collective-permute-start | bytes 983048 | tf_op jit(solution)/shard_map/ppermute | solution.py:287
  6.6 16.2 %collective-permute-start.5 = (bf16[80,2048]{1,0:T(8,128)(2,1)S(1)}, bf16[80,2048]{1,0:T(8,128)(2,1)S(1)}, u32[]{:S(2)}, u32[]{:S(2)}) collective-permute-start(bf16[80,2048]{1,0:T(8,128)(2,1)S(1)} %get-tuple-element.59), channel_id=1, source_target_pairs={{0,4},{1,5},{2,6},{3,7},{4,0},{5,1},{6,2},{7,3},{8,12},{9,13},{10,... | collective-permute-start | bytes 983048 | tf_op jit(solution)/shard_map/ppermute | solution.py:287
  8.9 15.8 %collective-permute-start.1 = (bf16[40,2048]{1,0:T(8,128)(2,1)S(1)}, bf16[40,2048]{1,0:T(8,128)(2,1)S(1)}, u32[]{:S(2)}, u32[]{:S(2)}) collective-permute-start(bf16[40,2048]{1,0:T(8,128)(2,1)S(1)} %get-tuple-element.49), channel_id=1, source_target_pairs={{0,1},{1,0},{2,3},{3,2},{4,5},{5,4},{6,7},{7,6},{8,9},{9,8},{10,11... | collective-permute-start | bytes 491528 | tf_op jit(solution)/shard_map/ppermute | solution.py:287
  10.4 1.4 %copy-start.1 = (bf16[1,1,2048,384]{3,2,1,0:T(8,128)(2,1)S(1)}, bf16[1,1,2048,384]{3,2,1,0:T(8,128)(2,1)}, u32[]{:S(2)}) copy-start(bf16[1,1,2048,384]{3,2,1,0:T(8,128)(2,1)} %param.16) | copy-start | bytes 4718596
  11.8 1.4 %copy-start.2 = (bf16[1,1,384,2048]{3,2,1,0:T(8,128)(2,1)S(1)}, bf16[1,1,384,2048]{3,2,1,0:T(8,128)(2,1)}, u32[]{:S(2)}) copy-start(bf16[1,1,384,2048]{3,2,1,0:T(8,128)(2,1)} %param.17) | copy-start | bytes 4718596
  19.6 5.3 %collective-permute-start.3 = (bf16[40,2048]{1,0:T(8,128)(2,1)S(1)}, bf16[40,2048]{1,0:T(8,128)(2,1)S(1)}, u32[]{:S(2)}, u32[]{:S(2)}) collective-permute-start(bf16[40,2048]{1,0:T(8,128)(2,1)S(1)} %slice.21), channel_id=1, source_target_pairs={{0,1},{1,0},{2,3},{3,2},{4,5},{5,4},{6,7},{7,6},{8,9},{9,8},{10,11... | collective-permute-start | bytes 491528 | tf_op jit(solution)/shard_map/ppermute | solution.py:287
  21.5 16.0 %collective-permute-start.8 = (bf16[40,2048]{1,0:T(8,128)(2,1)S(1)}, bf16[40,2048]{1,0:T(8,128)(2,1)S(1)}, u32[]{:S(2)}, u32[]{:S(2)}) collective-permute-start(bf16[40,2048]{1,0:T(8,128)(2,1)S(1)} %get-tuple-element.66), channel_id=1, source_target_pairs={{0,6},{1,7},{2,4},{3,5},{4,2},{5,3},{6,0},{7,1},{8,14},{9,15},{10,... | collective-permute-start | bytes 491528 | tf_op jit(solution)/shard_map/ppermute | solution.py:287
  22.8 16.7 %collective-permute-start.9 = (bf16[40,2048]{1,0:T(8,128)(2,1)S(1)}, bf16[40,2048]{1,0:T(8,128)(2,1)S(1)}, u32[]{:S(2)}, u32[]{:S(2)}) collective-permute-start(bf16[40,2048]{1,0:T(8,128)(2,1)S(1)} %get-tuple-element.67), channel_id=1, source_target_pairs={{0,7},{1,6},{2,5},{3,4},{4,3},{5,2},{6,1},{7,0},{8,15},{9,14},{10,... | collective-permute-start | bytes 491528 | tf_op jit(solution)/shard_map/ppermute | solution.py:287
  24.8 8.6 %collective-permute-start.6 = (bf16[24,2048]{1,0:T(8,128)(2,1)S(1)}, bf16[24,2048]{1,0:T(8,128)(2,1)S(1)}, u32[]{:S(2)}, u32[]{:S(2)}) collective-permute-start(bf16[24,2048]{1,0:T(8,128)(2,1)S(1)} %slice.28), channel_id=1, source_target_pairs={{0,1},{1,0},{2,3},{3,2},{4,5},{5,4},{6,7},{7,6},{8,9},{9,8},{10,11... | collective-permute-start | bytes 294920 | tf_op jit(solution)/shard_map/ppermute | solution.py:287
  24.9 3.1 %collective-permute-start.7 = (bf16[16,2048]{1,0:T(8,128)(2,1)S(1)}, bf16[16,2048]{1,0:T(8,128)(2,1)S(1)}, u32[]{:S(2)}, u32[]{:S(2)}) collective-permute-start(bf16[16,2048]{1,0:T(8,128)(2,1)S(1)} %slice.29), channel_id=1, source_target_pairs={{0,1},{1,0},{2,3},{3,2},{4,5},{5,4},{6,7},{7,6},{8,9},{9,8},{10,11... | collective-permute-start | bytes 196616 | tf_op jit(solution)/shard_map/ppermute | solution.py:287
  28.0 15.9 %collective-permute-start.10 = (bf16[88,1024]{1,0:T(8,128)(2,1)S(1)}, bf16[88,1024]{1,0:T(8,128)(2,1)S(1)}, u32[]{:S(2)}, u32[]{:S(2)}) collective-permute-start(bf16[88,1024]{1,0:T(8,128)(2,1)S(1)} %get-tuple-element.73), channel_id=1, source_target_pairs={{8,2},{9,3},{10,0},{11,1},{12,6},{13,7},{14,4},{15,5},{16,10},{17,... | collective-permute-start | bytes 540680 | tf_op jit(solution)/shard_map/ppermute | solution.py:295
  33.3 10.5 %collective-permute-start.4 = (bf16[88,1024]{1,0:T(8,128)(2,1)S(1)}, bf16[88,1024]{1,0:T(8,128)(2,1)S(1)}, u32[]{:S(2)}, u32[]{:S(2)}) collective-permute-start(bf16[88,1024]{1,0:T(8,128)(2,1)S(1)} %get-tuple-element.58), channel_id=1, source_target_pairs={{8,0},{9,1},{10,2},{11,3},{12,4},{13,5},{14,6},{15,7},{16,8},{17,9... | collective-permute-start | bytes 540680 | tf_op jit(solution)/shard_map/ppermute | solution.py:295
  37.5 12.6 %collective-permute-start.13 = (bf16[80,1024]{1,0:T(8,128)(2,1)S(1)}, bf16[80,1024]{1,0:T(8,128)(2,1)S(1)}, u32[]{:S(2)}, u32[]{:S(2)}) collective-permute-start(bf16[80,1024]{1,0:T(8,128)(2,1)S(1)} %get-tuple-element.83), channel_id=1, source_target_pairs={{8,4},{9,5},{10,6},{11,7},{12,0},{13,1},{14,2},{15,3},{16,12},{17,... | collective-permute-start | bytes 491528 | tf_op jit(solution)/shard_map/ppermute | solution.py:295
  41.7 14.6 %collective-permute-start.15 = (bf16[80,1024]{1,0:T(8,128)(2,1)S(1)}, bf16[80,1024]{1,0:T(8,128)(2,1)S(1)}, u32[]{:S(2)}, u32[]{:S(2)}) collective-permute-start(bf16[80,1024]{1,0:T(8,128)(2,1)S(1)} %get-tuple-element.85), channel_id=1, source_target_pairs={{8,6},{9,7},{10,4},{11,5},{12,2},{13,3},{14,0},{15,1},{16,14},{17,... | collective-permute-start | bytes 491528 | tf_op jit(solution)/shard_map/ppermute | solution.py:295
  50.1 7.3 %collective-permute-start.14 = (bf16[40,1024]{1,0:T(8,128)(2,1)S(1)}, bf16[40,1024]{1,0:T(8,128)(2,1)S(1)}, u32[]{:S(2)}, u32[]{:S(2)}) collective-permute-start(bf16[40,1024]{1,0:T(8,128)(2,1)S(1)} %slice.26), channel_id=1, source_target_pairs={{0,1},{1,0},{2,3},{3,2},{4,5},{5,4},{6,7},{7,6},{8,9},{9,8},{10,11... | collective-permute-start | bytes 245768 | tf_op jit(solution)/shard_map/ppermute | solution.py:287
  51.2 6.2 %collective-permute-start.12 = (bf16[40,1024]{1,0:T(8,128)(2,1)S(1)}, bf16[40,1024]{1,0:T(8,128)(2,1)S(1)}, u32[]{:S(2)}, u32[]{:S(2)}) collective-permute-start(bf16[40,1024]{1,0:T(8,128)(2,1)S(1)} %slice.25), channel_id=1, source_target_pairs={{0,1},{1,0},{2,3},{3,2},{4,5},{5,4},{6,7},{7,6},{8,9},{9,8},{10,11... | collective-permute-start | bytes 245768 | tf_op jit(solution)/shard_map/ppermute | solution.py:287
  51.3 6.1 %collective-permute-start.11 = (bf16[40,1024]{1,0:T(8,128)(2,1)S(1)}, bf16[40,1024]{1,0:T(8,128)(2,1)S(1)}, u32[]{:S(2)}, u32[]{:S(2)}) collective-permute-start(bf16[40,1024]{1,0:T(8,128)(2,1)S(1)} %slice.24), channel_id=1, source_target_pairs={{0,1},{1,0},{2,3},{3,2},{4,5},{5,4},{6,7},{7,6},{8,9},{9,8},{10,11... | collective-permute-start | bytes 245768 | tf_op jit(solution)/shard_map/ppermute | solution.py:287
  56.3 2.0 %collective-permute-start.16 = (bf16[40,1024]{1,0:T(8,128)(2,1)S(1)}, bf16[40,1024]{1,0:T(8,128)(2,1)S(1)}, u32[]{:S(2)}, u32[]{:S(2)}) collective-permute-start(bf16[40,1024]{1,0:T(8,128)(2,1)S(1)} %slice.30), channel_id=1, source_target_pairs={{0,1},{1,0},{2,3},{3,2},{4,5},{5,4},{6,7},{7,6},{8,9},{9,8},{10,11... | collective-permute-start | bytes 245768 | tf_op jit(solution)/shard_map/ppermute | solution.py:287

commit v5 on v4

--- a/solution.py
+++ b/solution.py
@@ -9,6 +9,7 @@
 
 CAP = 20
 PAIR = 2 * CAP
+SHARES = 2
 F32 = jnp.float32
 BF16 = jnp.bfloat16
 SHORT = pl.CostEstimate(flops=1, transcendentals=0, bytes_accessed=1)
@@ -29,8 +30,10 @@
     return [keys[k : k + 1, :] == slot for k in range(keys.shape[0])]
 
 
-def gather_kernel(n_expert, ids_hbm, slot_hbm, dropped_hbm, weight_hbm, in_hbm, grad_hbm, keys_ref, *refs):
-    outs, (ids_ref, slot_ref, dropped_ref, weight_ref, in_ref, grad_ref, sem) = refs[:-7], refs[-7:]
+def gather_kernel(n_expert, shares, ids_hbm, slot_hbm, dropped_hbm, weight_hbm, in_hbm, grad_hbm, keys_ref, *refs):
+    grad_refs, outs = refs[:shares], refs[shares:-6]
+    ids_ref, slot_ref, dropped_ref, weight_ref, in_ref, sem = refs[-6:]
+    share = grad_refs[0].shape[0]
     copies = [
         pltpu.make_async_copy(src, dst, sem.at[i])
         for i, (src, dst) in enumerate(
@@ -40,7 +43,7 @@
                 (dropped_hbm, dropped_ref),
                 (weight_hbm, weight_ref),
                 (in_hbm, in_ref),
-                (grad_hbm, grad_ref),
+                *((grad_hbm.at[pl.ds(i * share, share)], ref) for i, ref in enumerate(grad_refs)),
             )
         )
     ]
@@ -67,8 +70,10 @@
     row_weight = jnp.sum(scaled, axis=1, keepdims=True)
     copies[4].wait()
     got = jnp.dot(pick_in, in_ref[...], preferred_element_type=F32)
-    copies[5].wait()
-    got = got + row_weight * jnp.dot(pick_grad, grad_ref[...], preferred_element_type=F32)
+    for i, ref in enumerate(grad_refs):
+        copies[5 + i].wait()
+        pick = pick_grad[:, i * share : (i + 1) * share]
+        got = got + row_weight * jnp.dot(pick, ref[...], preferred_element_type=F32)
     got = got.astype(BF16)
     start = 0
     for out in outs:
@@ -76,48 +81,61 @@
         start += out.shape[0]
 
 
-def gather(ids, slots, dropped, weight, inputs, grads, chips, apart):
+def gather(ids, slots, dropped, weight, inputs, grads, chips, apart, shares):
     tokens, width = inputs.shape
     ranks = ids.shape[0]
     sizes = [n for c in range(chips) for n in ([PAIR, PAIR] if c in apart else [2 * PAIR])]
     outs = pl.pallas_call(
-        functools.partial(gather_kernel, 2 * chips),
+        functools.partial(gather_kernel, 2 * chips, shares),
         out_shape=[jax.ShapeDtypeStruct((ranks, tokens), jnp.int32)]
+        + [jax.ShapeDtypeStruct((tokens // shares, width), BF16)] * shares
         + [jax.ShapeDtypeStruct((n, width), BF16) for n in sizes],
         in_specs=[pl.BlockSpec(memory_space=pltpu.HBM)] * 6,
-        out_specs=vmem(1 + len(sizes)),
+        out_specs=vmem(1 + shares + len(sizes)),
         scratch_shapes=[pltpu.VMEM((ranks, tokens), jnp.int32)] * 3
         + [pltpu.VMEM((ranks, tokens), F32)]
-        + [pltpu.VMEM((tokens, width), BF16)] * 2
-        + [pltpu.SemaphoreType.DMA((6,))],
+        + [pltpu.VMEM((tokens, width), BF16)]
+        + [pltpu.SemaphoreType.DMA((5 + shares,))],
         name="gather",
         compiler_params=pltpu.CompilerParams(vmem_limit_bytes=16 << 20),
         cost_estimate=SHORT,
-    )(*(pltpu.with_memory_space_constraint(a, pltpu.HBM) for a in (ids, slots, dropped, weight, inputs, grads)))
-    keys, *outs = outs
-    return keys, [[outs.pop(0), outs.pop(0)] if c in apart else outs.pop(0) for c in range(chips)]
-
-
-def load_kernel(count, *refs):
-    sem = refs[-1]
-    copies = [pltpu.make_async_copy(refs[i], refs[count + i], sem.at[i]) for i in range(count)]
+    )(*pinned((ids, slots, dropped, weight, inputs, grads)))
+    keys, held, outs = outs[0], outs[1 : 1 + shares], list(outs[1 + shares :])
+    return keys, held, [[outs.pop(0), outs.pop(0)] if c in apart else outs.pop(0) for c in range(chips)]
+
+
+def load_kernel(gate_hbm, up_hbm, down_hbm, both_ref, down_ref, sem):
+    hidden = gate_hbm.shape[1]
+    copies = [
+        pltpu.make_async_copy(gate_hbm, both_ref.at[:, :hidden], sem.at[0]),
+        pltpu.make_async_copy(up_hbm, both_ref.at[:, hidden:], sem.at[1]),
+        pltpu.make_async_copy(down_hbm, down_ref, sem.at[2]),
+    ]
     for copy in copies:
         copy.start()
     for copy in copies:
         copy.wait()
 
 
-def load(*arrays):
+def pinned(arrays):
+    return [pltpu.with_memory_space_constraint(a, pltpu.HBM) for a in arrays]
+
+
+def load(w_gate, w_up, w_down):
+    width, hidden = w_gate.shape
     return pl.pallas_call(
-        functools.partial(load_kernel, len(arrays)),
-        out_shape=[jax.ShapeDtypeStruct(a.shape, a.dtype) for a in arrays],
-        in_specs=[pl.BlockSpec(memory_space=pltpu.HBM)] * len(arrays),
-        out_specs=vmem(len(arrays)),
-        scratch_shapes=[pltpu.SemaphoreType.DMA((len(arrays),))],
+        load_kernel,
+        out_shape=[
+            jax.ShapeDtypeStruct((width, 2 * hidden), BF16),
+            jax.ShapeDtypeStruct((hidden, width), BF16),
+        ],
+        in_specs=[pl.BlockSpec(memory_space=pltpu.HBM)] * 3,
+        out_specs=vmem(2),
+        scratch_shapes=[pltpu.SemaphoreType.DMA((3,))],
         name="load",
         compiler_params=pltpu.CompilerParams(vmem_limit_bytes=12 << 20),
         cost_estimate=SHORT,
-    )(*arrays)
+    )(*pinned((w_gate, w_up, w_down)))
 
 
 def nt(a, b):
@@ -137,14 +155,15 @@
     if with_keys:
         keys_ref, refs = refs[0], refs[1:]
     payloads = refs[:count]
-    w_gate, w_up, w_down = refs[count : count + 3]
-    returns = refs[count + 3 : -3]
-    gate_out, up_out, hidden_out = refs[-3:]
+    w_both, w_down = refs[count : count + 2]
+    returns = refs[count + 2 : -2]
+    grads_out, hidden_out = refs[-2:]
     rows = sum(hi - lo for lo, hi in spans)
-    half = w_gate.shape[0] // 2
+    width, units = w_down.shape[1], w_down.shape[0]
+    half = width // 2
     both = joined(payloads, spans)
-    gate_pre = jnp.dot(both, w_gate[...], preferred_element_type=F32)
-    up_pre = jnp.dot(both, w_up[...], preferred_element_type=F32)
+    pre = jnp.dot(both, w_both[...], preferred_element_type=F32)
+    gate_pre, up_pre = pre[:, :units], pre[:, units:]
     hidden_grad = pltpu.roll(nt(both, w_down[...]), rows - CAP, 0)
     first = is_first(gate_pre.shape)
     sigma = jax.nn.sigmoid(gate_pre)
@@ -153,17 +172,16 @@
     gate_grad = hidden_grad * up_pre * sigma * (1.0 + gate_pre * (1.0 - sigma))
     gate_grad = jnp.where(first, gate_grad, 0.0)
     up_grad = jnp.where(first, hidden_grad * active, 0.0)
-    gate_out[...] = gate_grad.astype(BF16)
-    up_out[...] = up_grad.astype(BF16)
-    hidden_out[...] = pltpu.roll(hidden, CAP, 0).astype(BF16)
-    gate_two = (gate_grad + pltpu.roll(gate_grad, CAP, 0)).astype(BF16)
-    up_two = (up_grad + pltpu.roll(up_grad, CAP, 0)).astype(BF16)
-    left = nt(gate_two, w_gate[:half, :]) + nt(up_two, w_up[:half, :])
-    right = nt(gate_two, w_gate[half:, :]) + nt(up_two, w_up[half:, :])
+    grads = jnp.concatenate([gate_grad, up_grad], axis=1)
+    grads_two = (grads + pltpu.roll(grads, CAP, 0)).astype(BF16)
+    left = nt(grads_two, w_both[:half, :])
+    right = nt(grads_two, w_both[half:, :])
     row_grad = jnp.where(is_first(left.shape), left, right).astype(BF16)
     step = rows // len(returns)
     for k, out in enumerate(returns):
         out[:step, :] = row_grad[k * step : (k + 1) * step, :]
+    grads_out[...] = grads.astype(BF16)
+    hidden_out[...] = pltpu.roll(hidden, CAP, 0).astype(BF16)
     if with_keys:
         ranks, tokens = keys_ref.shape
         keys = keys_ref[...].astype(F32)
@@ -174,10 +192,10 @@
             out[2 * PAIR :, 2 * tokens :] = jnp.zeros((ranks, half - 2 * tokens), BF16)
 
 
-def expert_chunk(pieces, w_gate, w_up, w_down, keys=None):
+def expert_chunk(pieces, w_both, w_down, keys=None):
     arrays, spans = [p[0] for p in pieces], [p[1] for p in pieces]
     total = sum(hi - lo for lo, hi in spans)
-    width, hidden = w_gate.shape
+    hidden, width = w_down.shape
     extra = [] if keys is None else [keys]
     rows = [2 * PAIR] * (total // (2 * PAIR))
     if extra:
@@ -185,27 +203,28 @@
     out = pl.pallas_call(
         functools.partial(expert_kernel, spans, bool(extra)),
         out_shape=[jax.ShapeDtypeStruct((r, width // 2), BF16) for r in rows]
-        + [jax.ShapeDtypeStruct((total, hidden), BF16)] * 3,
-        in_specs=vmem(len(extra) + len(pieces) + 3),
-        out_specs=vmem(len(rows) + 3),
+        + [jax.ShapeDtypeStruct((total, n * hidden), BF16) for n in (2, 1)],
+        in_specs=vmem(len(extra) + len(pieces) + 2),
+        out_specs=vmem(len(rows) + 2),
         name="expert",
         compiler_params=pltpu.CompilerParams(vmem_limit_bytes=20 << 20),
         cost_estimate=SHORT,
-    )(*extra, *arrays, w_gate, w_up, w_down)
+    )(*extra, *arrays, w_both, w_down)
     return out[: len(rows)], out[len(rows) :]
 
 
 def weight_kernel(spans, chunks, *refs):
     count = len(spans)
     payloads = refs[:count]
-    small = refs[count : count + 3 * chunks]
-    grad_gate, grad_up, grad_down = refs[count + 3 * chunks :]
+    small = refs[count : count + 2 * chunks]
+    grad_gate, grad_up, grad_down = refs[count + 2 * chunks :]
+    units = grad_gate.shape[1]
     both = joined(payloads, spans)
-    gate = jnp.concatenate([r[...] for r in small[0::3]], axis=0)
-    up = jnp.concatenate([r[...] for r in small[1::3]], axis=0)
-    hidden = jnp.concatenate([r[...] for r in small[2::3]], axis=0)
-    grad_gate[...] = tn(both, gate).astype(BF16)
-    grad_up[...] = tn(both, up).astype(BF16)
+    grads = jnp.concatenate([r[...] for r in small[0::2]], axis=0)
+    hidden = jnp.concatenate([r[...] for r in small[1::2]], axis=0)
+    made = tn(both, grads).astype(BF16)
+    grad_gate[...] = made[:, :units]
+    grad_up[...] = made[:, units:]
     grad_down[...] = tn(hidden, both).astype(BF16)
 
 
@@ -221,7 +240,7 @@
             jax.ShapeDtypeStruct((width, hidden), BF16),
             jax.ShapeDtypeStruct((hidden, width), BF16),
         ],
-        in_specs=vmem(count + 3 * chunks),
+        in_specs=vmem(count + 2 * chunks),
         out_specs=vmem(3),
         name="weight_grads",
         compiler_params=pltpu.CompilerParams(vmem_limit_bytes=24 << 20),
@@ -229,37 +248,53 @@
     )(*payloads, *flat)
 
 
-def combine_kernel(spans, ranks, grad_ref, *refs):
-    returned, out = refs[:-1], refs[-1]
+def combine_kernel(spans, start, ranks, bases, keys_ref, *refs):
+    base_refs, returned = refs[:bases], refs[bases : bases + len(spans)]
+    out, *scratch = refs[bases + len(spans) :]
     rows = sum(hi - lo for lo, hi in spans)
-    tokens = grad_ref.shape[0]
-    block = returned[0][2 * PAIR : 2 * PAIR + ranks, :tokens].astype(F32)
-    slot = returned[0][2 * PAIR : 2 * PAIR + ranks, tokens : 2 * tokens].astype(F32)
+    share = base_refs[0].shape[0]
+    tokens, width = out.shape
+    block = keys_ref[2 * PAIR : 2 * PAIR + ranks, :tokens].astype(F32)
+    slot = keys_ref[2 * PAIR : 2 * PAIR + ranks, tokens : 2 * tokens].astype(F32)
     keys = (PAIR * block + slot).astype(jnp.int32)
-    half = grad_ref.shape[1] // 2
     own = jnp.zeros((rows, tokens), F32)
-    for hit in match_rows(keys, 0, rows):
+    for hit in match_rows(keys, start * PAIR, rows):
         own = jnp.where(hit, 1.0, own)
     first = is_first((rows, tokens))
+    picks = [jnp.where(first, own, 0.0).astype(BF16), jnp.where(first, 0.0, own).astype(BF16)]
     back = joined(returned, spans)
-    for side in range(2):
-        pick = jnp.where(first, own, 0.0) if side == 0 else jnp.where(first, 0.0, own)
-        cols = slice(side * half, (side + 1) * half)
-        total = grad_ref[:, cols].astype(F32) + tn(pick.astype(BF16), back)
-        out[:, cols] = total.astype(BF16)
-
-
-def combine(ranks, grads, pieces):
+    quarter = width // 4
+    copies = []
+    for i in range(4):
+        cols = slice(i * quarter, (i + 1) * quarter)
+        side = slice(i % 2 * quarter, (i % 2 + 1) * quarter)
+        added = tn(picks[i // 2], back[:, side])
+        for j, ref in enumerate(base_refs):
+            here = slice(j * share, (j + 1) * share)
+            total = ref[:, cols].astype(F32) + added[here, :]
+            (scratch[0] if scratch else out)[here, cols] = total.astype(out.dtype)
+        if scratch:
+            copy = pltpu.make_async_copy(scratch[0].at[:, cols], out.at[:, cols], scratch[1].at[i])
+            copy.start()
+            copies.append(copy)
+    for copy in copies:
+        copy.wait()
+
+
+def combine(ranks, carrier, bases, start, pieces, last):
     returned, spans = [p[0] for p in pieces], [p[1] for p in pieces]
+    shape = (len(bases) * bases[0].shape[0], bases[0].shape[1])
+    space = pltpu.HBM if last else pltpu.VMEM
     return pl.pallas_call(
-        functools.partial(combine_kernel, spans, ranks),
-        out_shape=jax.ShapeDtypeStruct(grads.shape, BF16),
-        in_specs=vmem(1 + len(returned)),
-        out_specs=pl.BlockSpec(memory_space=pltpu.VMEM),
+        functools.partial(combine_kernel, spans, start, ranks, len(bases)),
+        out_shape=jax.ShapeDtypeStruct(shape, BF16 if last else F32),
+        in_specs=vmem(1 + len(bases) + len(returned)),
+        out_specs=pl.BlockSpec(memory_space=space),
+        scratch_shapes=[pltpu.VMEM(shape, BF16), pltpu.SemaphoreType.DMA((4,))] if last else [],
         name="combine",
         compiler_params=pltpu.CompilerParams(vmem_limit_bytes=16 << 20),
         cost_estimate=SHORT,
-    )(grads, *returned)
+    )(carrier, *bases, *returned)
 
 
 def per_device(
@@ -299,7 +334,7 @@
     early = list(range(chips // 2, 3 * chips // 4))
     late = list(range(3 * chips // 4, chips))
     by_rank = [jnp.transpose(a[0]) for a in (expert_ids, slot_pos, dropped, route_weight)]
-    keys, sent = gather(*by_rank, inputs, grads, chips, [0] + late)
+    keys, held, sent = gather(*by_rank, inputs, grads, chips, [0] + late, SHARES)
     mine = (0, PAIR)
 
     def after(values, event):
@@ -319,7 +354,7 @@
     arrived, order, small, returned = {}, [], [], {}
 
     def process(chunk, pieces, **options):
-        back, parts = expert_chunk(pieces, w_gate, w_up, w_down, **options)
+        back, parts = expert_chunk(pieces, w_both, w_down, **options)
         order.extend(pieces)
         small.append(parts)
         for c, value in zip(chunk, back):
@@ -331,24 +366,25 @@
     for c in late:
         arrived[c] = [(to_partner(v, 2 * c + i), mine) for i, v in enumerate(sent[c])]
     beside = to_partner(sent[0][1], 1)
-    next_grads = to_before(after(grads, sent[0][0]), 0)
+    next_grads = [to_before(share, 0) for share in held]
     pieces = [(sent[0][0], mine), (beside, mine)]
-    w_gate, w_up, w_down = load(*after((w_gate, w_up, w_down), sent[0][0]))
+    w_both, w_down = load(*after((w_gate, w_up, w_down), sent[0][0]))
     here = after([arrived[c] for c in near], w_down)
     for value in here:
         pieces += forward(value)
     parts = process([0] + near, pieces, keys=keys)
     pieces = [piece for c in early for piece in forward(arrived[c], PAIR + 24)]
-    parts = process(early, gated(pieces, parts))
+    parts = process(early, gated(pieces, (parts, next_grads[0])))
     pieces = [piece for c in late for piece in arrived[c]]
     process(late, gated(pieces, (parts, next_grads)))
     small[0] = after(small[0], [returned[c] for c in [0] + near])
     grad_gate, grad_up, grad_down = weight_grads(order, small, width, hidden)
+    carrier = returned[0]
     pieces = []
     for c in range(chips):
         value = after(returned[c], grad_gate) if c not in late else returned[c]
         pieces += forward(value)
-    upstream = combine(keys.shape[0], next_grads, pieces)
+    upstream = combine(keys.shape[0], carrier, next_grads, 0, pieces, True)
     return (upstream[None], grad_gate[None, None], grad_up[None, None], grad_down[None, None])
 
 

time: 60.5 us -> 59.1 us (0.977)
  waiting for transfers between devices: 13.6 us -> 9.52 us
  starting transfers between devices: 27 us -> 30.6 us
  local copies, waits for them, and re-layouts: 2.87 us -> 0.05 us
  Pallas kernels: 16 us -> 17.8 us
    ppermute x5 -> x6, starting transfers between devices: 14.4 us -> 18.3 us  [to_before(): return lax.ppermute(value, both_axes, pairs)]
    unnamed x6 -> x0, local copies, waits for them, and re-layouts: 2.82 us -> none
    ppermute x12, waiting for transfers between devices: 6.9 us -> 4.75 us  [to_partner(): return lax.ppermute(value, 'expert', [(i, i ^ k) for i in range(n_expert)])]
    pallas_call x3, Pallas kernels: 4.88 us -> 6.87 us  [the longest x1 2.82 us: gather(): pl.pallas_call(functools.partial(gather_kernel, 2 * chips, shares), out_s...]
    ppermute x5 -> x6, waiting for transfers between devices: 6.67 us -> 4.77 us  [to_before(): return lax.ppermute(value, both_axes, pairs)]
  transfers between devices with their start and end apart: 17 -> 18, of which waited for: 4 -> 6; matrix products, arithmetic and copies ran while one was open for 0% -> 0% of each run, Pallas kernels for 19% -> 23%
where the time goes in v5:
time: 59.1 us; the launch traced here: 58.7 us
  starting transfers between devices  30.6 us (52%)
  Pallas kernels  17.8 us (30%)
  waiting for transfers between devices  9.52 us (16%)
  between operations  0.78 us (1%)
    ppermute x6, starting transfers between devices, to_before(): return lax.ppermute(value, both_axes, pairs)  18.3 us
    ppermute x12, starting transfers between devices, to_partner(): return lax.ppermute(value, 'expert', [(i, i ^ k) for i in range(n_expert)])  12.3 us
    pallas_call x3, Pallas kernels, expert_chunk(): pl.pallas_call(functools.partial(expert_kernel, spans, bool(extra)), out_...  6.75 us
    ppermute x6, waiting for transfers between devices, to_before(): return lax.ppermute(value, both_axes, pairs)  4.77 us
    ppermute x12, waiting for transfers between devices, to_partner(): return lax.ppermute(value, 'expert', [(i, i ^ k) for i in range(n_expert)])  4.75 us
    pallas_call x1, Pallas kernels, weight_grads(): pl.pallas_call(functools.partial(weight_kernel, spans, chunks), out_shape...  4.13 us
    pallas_call x1, Pallas kernels, gather(): pl.pallas_call(functools.partial(gather_kernel, 2 * chips, shares), out_s...  2.82 us
    pallas_call x1, Pallas kernels, load(): pl.pallas_call(load_kernel, out_shape=[jax.ShapeDtypeStruct((width, 2 * h...  2.38 us
  transfers between devices with their start and end apart: 18, of which 6 were waited for; matrix products, arithmetic and copies ran while one was open for 0% of the time, Pallas kernels for 23%

profile of v5, /device:TPU:13, one launch (start us, length us, event | category | flops | bytes accessed | tf_op | source)
XLA Modules:
  0.0 58.7 jit_solution(10015965989206101149)
XLA Ops:
  0.6 2.8 %gather.1 = (s32[8,256]{1,0:T(8,128)S(1)}, bf16[128,2048]{1,0:T(8,128)(2,1)S(1)}, bf16[128,2048]{1,0:T(8,128)(2,1)S(1)}, bf16[40,2048]{1,0:T(8,128)(2,1)S(1)}, b...) custom-call(s32[8,256]{1,0:T(8,128)} %bitcast.27, ...), custom_call_target="tpu_custom_call" | custom-call | flops 1 | bytes 1 | tf_op jit(solution)/shard_map/gather/pallas_call | solution.py:88
  3.7 2.3 %collective-permute-start.6 = (bf16[80,2048]{1,0:T(8,128)(2,1)S(1)}, bf16[80,2048]{1,0:T(8,128)(2,1)S(1)}, u32[]{:S(2)}, u32[]{:S(2)}) collective-permute-start(bf16[80,2048]{1,0:T(8,128)(2,1)S(1)} %get-tuple-element.55), channel_id=1, source_target_pairs={{0,4},{1,5},{2,6},{3,7},{4,0},{5,1},{6,2},{7,3},{8,12},{9,13},{10,... | collective-permute-start | bytes 983048 | tf_op jit(solution)/shard_map/ppermute | solution.py:322
  6.0 3.0 %collective-permute-start.4 = (bf16[128,2048]{1,0:T(8,128)(2,1)S(1)}, bf16[128,2048]{1,0:T(8,128)(2,1)S(1)}, u32[]{:S(2)}, u32[]{:S(2)}) collective-permute-start(bf16[128,2048]{1,0:T(8,128)(2,1)S(1)} %get-tuple-element.53), channel_id=1, source_target_pairs={{8,0},{9,1},{10,2},{11,3},{12,4},{13,5},{14,6},{15,7},{16,8},{17,9... | collective-permute-start | bytes 1572872 | tf_op jit(solution)/shard_map/ppermute | solution.py:330
  9.1 2.2 %collective-permute-start.5 = (bf16[128,2048]{1,0:T(8,128)(2,1)S(1)}, bf16[128,2048]{1,0:T(8,128)(2,1)S(1)}, u32[]{:S(2)}, u32[]{:S(2)}) collective-permute-start(bf16[128,2048]{1,0:T(8,128)(2,1)S(1)} %get-tuple-element.54), channel_id=1, source_target_pairs={{8,0},{9,1},{10,2},{11,3},{12,4},{13,5},{14,6},{15,7},{16,8},{17,9... | collective-permute-start | bytes 1572872 | tf_op jit(solution)/shard_map/ppermute | solution.py:330
  11.2 1.9 %collective-permute-start = (bf16[40,2048]{1,0:T(8,128)(2,1)S(1)}, bf16[40,2048]{1,0:T(8,128)(2,1)S(1)}, u32[]{:S(2)}, u32[]{:S(2)}) collective-permute-start(bf16[40,2048]{1,0:T(8,128)(2,1)S(1)} %get-tuple-element.44), channel_id=1, source_target_pairs={{0,1},{1,0},{2,3},{3,2},{4,5},{5,4},{6,7},{7,6},{8,9},{9,8},{10,11... | collective-permute-start | bytes 491528 | tf_op jit(solution)/shard_map/ppermute | solution.py:322
  13.1 2.4 %load.1 = (bf16[2048,768]{1,0:T(8,128)(2,1)S(1)}, bf16[384,2048]{1,0:T(8,128)(2,1)S(1)}) custom-call(bf16[2048,384]{1,0:T(8,128)(2,1)} %bitcast.21, bf16[2048,384]{1,0:T(8,128)(2,1)} %bitcast.22, bf16[384,2048]{1,0:T(8,128)(2,1)} %bitcast.23), custom_call_target="tpu_custom_call" | custom-call | flops 1 | bytes 1 | tf_op jit(solution)/shard_map/load/pallas_call | solution.py:126
  15.5 1.5 %collective-permute-done.1.refs_3_.refs_2_ = bf16[80,2048]{1,0:T(8,128)(2,1)S(1)} collective-permute-done((bf16[80,2048]{1,0:T(8,128)(2,1)S(1)}, bf16[80,2048]{1,0:T(8,128)(2,1)S(1)}, u32[]{:S(2)}, u32[]{:S(2)}) %collective-permute-start.1) | collective-permute-done | bytes 327712 | tf_op jit(solution)/shard_map/ppermute | solution.py:322
  17.0 1.6 %collective-permute-start.2 = (bf16[40,2048]{1,0:T(8,128)(2,1)S(1)}, bf16[40,2048]{1,0:T(8,128)(2,1)S(1)}, u32[]{:S(2)}, u32[]{:S(2)}) collective-permute-start(bf16[40,2048]{1,0:T(8,128)(2,1)S(1)} %slice.21), channel_id=1, source_target_pairs={{0,1},{1,0},{2,3},{3,2},{4,5},{5,4},{6,7},{7,6},{8,9},{9,8},{10,11... | collective-permute-start | bytes 491528 | tf_op jit(solution)/shard_map/ppermute | solution.py:322
  18.6 1.6 %collective-permute-done.6.refs_0_.refs_4_ = bf16[80,2048]{1,0:T(8,128)(2,1)S(1)} collective-permute-done((bf16[80,2048]{1,0:T(8,128)(2,1)S(1)}, bf16[80,2048]{1,0:T(8,128)(2,1)S(1)}, u32[]{:S(2)}, u32[]{:S(2)}) %collective-permute-start.6) | collective-permute-done | bytes 327712 | tf_op jit(solution)/shard_map/ppermute | solution.py:322
  20.2 1.6 %collective-permute-start.8 = (bf16[16,2048]{1,0:T(8,128)(2,1)S(1)}, bf16[16,2048]{1,0:T(8,128)(2,1)S(1)}, u32[]{:S(2)}, u32[]{:S(2)}) collective-permute-start(bf16[16,2048]{1,0:T(8,128)(2,1)S(1)} %slice.29), channel_id=1, source_target_pairs={{0,1},{1,0},{2,3},{3,2},{4,5},{5,4},{6,7},{7,6},{8,9},{9,8},{10,11... | collective-permute-start | bytes 196616 | tf_op jit(solution)/shard_map/ppermute | solution.py:322
  23.8 2.4 %expert.3 = (bf16[88,1024]{1,0:T(8,128)(2,1)S(1)}, bf16[88,1024]{1,0:T(8,128)(2,1)S(1)}, bf16[160,768]{1,0:T(8,128)(2,1)S(1)}, bf16[160,384]{1,0:T(8,128)(2,1)S(1)}) custom-call(s32[8,256]{1,0:T(8,128)S(1)} %get-tuple-element.42.refs_0_, bf16[40,2048]{1,0:T(8,128)(2,1)S(1)} %get-tuple-element.43.refs_1_.refs_0_, ...), custom_call_target="tpu_custom_call" | custom-call | flops 1 | bytes 1 | tf_op jit(solution)/shard_map/expert/pallas_call | solution.py:203
  26.1 3.1 %collective-permute-start.3 = (bf16[88,1024]{1,0:T(8,128)(2,1)S(1)}, bf16[88,1024]{1,0:T(8,128)(2,1)S(1)}, u32[]{:S(2)}, u32[]{:S(2)}) collective-permute-start(bf16[88,1024]{1,0:T(8,128)(2,1)S(1)} %get-tuple-element.52), channel_id=1, source_target_pairs={{8,0},{9,1},{10,2},{11,3},{12,4},{13,5},{14,6},{15,7},{16,8},{17,9... | collective-permute-start | bytes 540680 | tf_op jit(solution)/shard_map/ppermute | solution.py:330
  29.2 5.0 %collective-permute-start.11 = (bf16[88,1024]{1,0:T(8,128)(2,1)S(1)}, bf16[88,1024]{1,0:T(8,128)(2,1)S(1)}, u32[]{:S(2)}, u32[]{:S(2)}) collective-permute-start(bf16[88,1024]{1,0:T(8,128)(2,1)S(1)} %get-tuple-element.67), channel_id=1, source_target_pairs={{8,2},{9,3},{10,0},{11,1},{12,6},{13,7},{14,4},{15,5},{16,10},{17,... | collective-permute-start | bytes 540680 | tf_op jit(solution)/shard_map/ppermute | solution.py:330
  34.2 2.2 %expert.4 = (bf16[80,1024]{1,0:T(8,128)(2,1)S(1)}, bf16[80,768]{1,0:T(8,128)(2,1)S(1)}, bf16[80,384]{1,0:T(8,128)(2,1)S(1)}) custom-call(bf16[80,2048]{1,0:T(8,128)(2,1)S(1)} %collective-permute-done.6.refs_0_.refs_4_, bf16[24,2048]{1,0:T(8,128)(2,1)S(1)} %collective-permute-done.7.refs_1_.refs_5_, ...), custom_call_target="tpu_custom_call" | custom-call | flops 1 | bytes 1 | tf_op jit(solution)/shard_map/expert/pallas_call | solution.py:203
  36.4 2.9 %collective-permute-start.14 = (bf16[80,1024]{1,0:T(8,128)(2,1)S(1)}, bf16[80,1024]{1,0:T(8,128)(2,1)S(1)}, u32[]{:S(2)}, u32[]{:S(2)}) collective-permute-start(bf16[80,1024]{1,0:T(8,128)(2,1)S(1)} %get-tuple-element.75), channel_id=1, source_target_pairs={{8,4},{9,5},{10,6},{11,7},{12,0},{13,1},{14,2},{15,3},{16,12},{17,... | collective-permute-start | bytes 491528 | tf_op jit(solution)/shard_map/ppermute | solution.py:330
  39.4 2.2 %expert.5 = (bf16[80,1024]{1,0:T(8,128)(2,1)S(1)}, bf16[80,768]{1,0:T(8,128)(2,1)S(1)}, bf16[80,384]{1,0:T(8,128)(2,1)S(1)}) custom-call(bf16[40,2048]{1,0:T(8,128)(2,1)S(1)} %collective-permute-done.9.refs_0_.refs_7_, bf16[40,2048]{1,0:T(8,128)(2,1)S(1)} %collective-permute-done.10.refs_1_.refs_8_, ...), custom_call_target="tpu_custom_call" | custom-call | flops 1 | bytes 1 | tf_op jit(solution)/shard_map/expert/pallas_call | solution.py:203
  41.6 2.1 %collective-permute-start.16 = (bf16[80,1024]{1,0:T(8,128)(2,1)S(1)}, bf16[80,1024]{1,0:T(8,128)(2,1)S(1)}, u32[]{:S(2)}, u32[]{:S(2)}) collective-permute-start(bf16[80,1024]{1,0:T(8,128)(2,1)S(1)} %get-tuple-element.77), channel_id=1, source_target_pairs={{8,6},{9,7},{10,4},{11,5},{12,2},{13,3},{14,0},{15,1},{16,14},{17,... | collective-permute-start | bytes 491528 | tf_op jit(solution)/shard_map/ppermute | solution.py:330
  43.7 4.1 %weight_grads.1 = (bf16[2048,384]{1,0:T(8,128)(2,1)}, bf16[2048,384]{1,0:T(8,128)(2,1)}, bf16[384,2048]{1,0:T(8,128)(2,1)}) custom-call(bf16[40,2048]{1,0:T(8,128)(2,1)S(1)} %get-tuple-element.43.refs_1_.refs_0_, bf16[40,2048]{1,0:T(8,128)(2,1)S(1)} %collective-permute-done.refs_2_.refs_1_, bf16[80,2048]{1,0:T(8,128)(2,1)S(1)} %collective-permute-done.1.refs_3_.refs_2_, ...), custom_call_target="tpu_custom_call" | custom-call | flops 1 | bytes 1 | tf_op jit(solution)/shard_map/weight_grads/pallas_call | solution.py:236
  48.7 1.3 %collective-permute-done.14.refs_6_ = bf16[80,1024]{1,0:T(8,128)(2,1)S(1)} collective-permute-done((bf16[80,1024]{1,0:T(8,128)(2,1)S(1)}, bf16[80,1024]{1,0:T(8,128)(2,1)S(1)}, u32[]{:S(2)}, u32[]{:S(2)}) %collective-permute-start.14) | collective-permute-done | bytes 163872 | tf_op jit(solution)/shard_map/ppermute | solution.py:330
  50.0 1.2 %collective-permute-start.15 = (bf16[40,1024]{1,0:T(8,128)(2,1)S(1)}, bf16[40,1024]{1,0:T(8,128)(2,1)S(1)}, u32[]{:S(2)}, u32[]{:S(2)}) collective-permute-start(bf16[40,1024]{1,0:T(8,128)(2,1)S(1)} %slice.26), channel_id=1, source_target_pairs={{0,1},{1,0},{2,3},{3,2},{4,5},{5,4},{6,7},{7,6},{8,9},{9,8},{10,11... | collective-permute-start | bytes 245768 | tf_op jit(solution)/shard_map/ppermute | solution.py:322
  51.1 3.4 %collective-permute-done.16.refs_8_ = bf16[80,1024]{1,0:T(8,128)(2,1)S(1)} collective-permute-done((bf16[80,1024]{1,0:T(8,128)(2,1)S(1)}, bf16[80,1024]{1,0:T(8,128)(2,1)S(1)}, u32[]{:S(2)}, u32[]{:S(2)}) %collective-permute-start.16) | collective-permute-done | bytes 163872 | tf_op jit(solution)/shard_map/ppermute | solution.py:330
  54.6 1.5 %collective-permute-start.17 = (bf16[40,1024]{1,0:T(8,128)(2,1)S(1)}, bf16[40,1024]{1,0:T(8,128)(2,1)S(1)}, u32[]{:S(2)}, u32[]{:S(2)}) collective-permute-start(bf16[40,1024]{1,0:T(8,128)(2,1)S(1)} %slice.30), channel_id=1, source_target_pairs={{0,1},{1,0},{2,3},{3,2},{4,5},{5,4},{6,7},{7,6},{8,9},{9,8},{10,11... | collective-permute-start | bytes 245768 | tf_op jit(solution)/shard_map/ppermute | solution.py:322
  56.1 0.9 %collective-permute-done.17.refs_9_ = bf16[40,1024]{1,0:T(8,128)(2,1)S(1)} collective-permute-done((bf16[40,1024]{1,0:T(8,128)(2,1)S(1)}, bf16[40,1024]{1,0:T(8,128)(2,1)S(1)}, u32[]{:S(2)}, u32[]{:S(2)}) %collective-permute-start.17) | collective-permute-done | bytes 81952 | tf_op jit(solution)/shard_map/ppermute | solution.py:322
  57.0 1.7 %combine.1 = bf16[256,2048]{1,0:T(8,128)(2,1)} custom-call(bf16[88,1024]{1,0:T(8,128)(2,1)S(1)} %collective-permute-done.3.keys_ref.refs_2_, bf16[128,2048]{1,0:T(8,128)(2,1)S(1)} %collective-permute-done.4.refs_0_, bf16[128,2048]{1,0:T(8,128)(2,1)S(1)} %collective-permute-done.5.refs_1_, bf16[88,1024]{1,0:T(8,128)(2,1)S(1)} %collective-permute-done.3.keys_ref.refs_2_, ...), custom_call_target="tpu_custom_call" | custom-call | flops 1 | bytes 1 | tf_op jit(solution)/shard_map/combine/pallas_call | solution.py:288
  (26 shorter events, 3.0 us)
Async XLA Ops:
  3.5 13.5 %collective-permute-start.1 = (bf16[80,2048]{1,0:T(8,128)(2,1)S(1)}, bf16[80,2048]{1,0:T(8,128)(2,1)S(1)}, u32[]{:S(2)}, u32[]{:S(2)}) collective-permute-start(bf16[80,2048]{1,0:T(8,128)(2,1)S(1)} %get-tuple-element.45), channel_id=1, source_target_pairs={{0,2},{1,3},{2,0},{3,1},{4,6},{5,7},{6,4},{7,5},{8,10},{9,11},{10,... | collective-permute-start | bytes 983048 | tf_op jit(solution)/shard_map/ppermute | solution.py:322
  3.7 16.5 %collective-permute-start.6 = (bf16[80,2048]{1,0:T(8,128)(2,1)S(1)}, bf16[80,2048]{1,0:T(8,128)(2,1)S(1)}, u32[]{:S(2)}, u32[]{:S(2)}) collective-permute-start(bf16[80,2048]{1,0:T(8,128)(2,1)S(1)} %get-tuple-element.55), channel_id=1, source_target_pairs={{0,4},{1,5},{2,6},{3,7},{4,0},{5,1},{6,2},{7,3},{8,12},{9,13},{10,... | collective-permute-start | bytes 983048 | tf_op jit(solution)/shard_map/ppermute | solution.py:322
  6.0 23.2 %collective-permute-start.4 = (bf16[128,2048]{1,0:T(8,128)(2,1)S(1)}, bf16[128,2048]{1,0:T(8,128)(2,1)S(1)}, u32[]{:S(2)}, u32[]{:S(2)}) collective-permute-start(bf16[128,2048]{1,0:T(8,128)(2,1)S(1)} %get-tuple-element.53), channel_id=1, source_target_pairs={{8,0},{9,1},{10,2},{11,3},{12,4},{13,5},{14,6},{15,7},{16,8},{17,9... | collective-permute-start | bytes 1572872 | tf_op jit(solution)/shard_map/ppermute | solution.py:330
  9.1 30.3 %collective-permute-start.5 = (bf16[128,2048]{1,0:T(8,128)(2,1)S(1)}, bf16[128,2048]{1,0:T(8,128)(2,1)S(1)}, u32[]{:S(2)}, u32[]{:S(2)}) collective-permute-start(bf16[128,2048]{1,0:T(8,128)(2,1)S(1)} %get-tuple-element.54), channel_id=1, source_target_pairs={{8,0},{9,1},{10,2},{11,3},{12,4},{13,5},{14,6},{15,7},{16,8},{17,9... | collective-permute-start | bytes 1572872 | tf_op jit(solution)/shard_map/ppermute | solution.py:330
  11.2 10.6 %collective-permute-start = (bf16[40,2048]{1,0:T(8,128)(2,1)S(1)}, bf16[40,2048]{1,0:T(8,128)(2,1)S(1)}, u32[]{:S(2)}, u32[]{:S(2)}) collective-permute-start(bf16[40,2048]{1,0:T(8,128)(2,1)S(1)} %get-tuple-element.44), channel_id=1, source_target_pairs={{0,1},{1,0},{2,3},{3,2},{4,5},{5,4},{6,7},{7,6},{8,9},{9,8},{10,11... | collective-permute-start | bytes 491528 | tf_op jit(solution)/shard_map/ppermute | solution.py:322
  17.0 6.5 %collective-permute-start.2 = (bf16[40,2048]{1,0:T(8,128)(2,1)S(1)}, bf16[40,2048]{1,0:T(8,128)(2,1)S(1)}, u32[]{:S(2)}, u32[]{:S(2)}) collective-permute-start(bf16[40,2048]{1,0:T(8,128)(2,1)S(1)} %slice.21), channel_id=1, source_target_pairs={{0,1},{1,0},{2,3},{3,2},{4,5},{5,4},{6,7},{7,6},{8,9},{9,8},{10,11... | collective-permute-start | bytes 491528 | tf_op jit(solution)/shard_map/ppermute | solution.py:322
  20.2 2.5 %collective-permute-start.8 = (bf16[16,2048]{1,0:T(8,128)(2,1)S(1)}, bf16[16,2048]{1,0:T(8,128)(2,1)S(1)}, u32[]{:S(2)}, u32[]{:S(2)}) collective-permute-start(bf16[16,2048]{1,0:T(8,128)(2,1)S(1)} %slice.29), channel_id=1, source_target_pairs={{0,1},{1,0},{2,3},{3,2},{4,5},{5,4},{6,7},{7,6},{8,9},{9,8},{10,11... | collective-permute-start | bytes 196616 | tf_op jit(solution)/shard_map/ppermute | solution.py:322
  21.8 14.6 %collective-permute-start.9 = (bf16[40,2048]{1,0:T(8,128)(2,1)S(1)}, bf16[40,2048]{1,0:T(8,128)(2,1)S(1)}, u32[]{:S(2)}, u32[]{:S(2)}) collective-permute-start(bf16[40,2048]{1,0:T(8,128)(2,1)S(1)} %get-tuple-element.61), channel_id=1, source_target_pairs={{0,6},{1,7},{2,4},{3,5},{4,2},{5,3},{6,0},{7,1},{8,14},{9,15},{10,... | collective-permute-start | bytes 491528 | tf_op jit(solution)/shard_map/ppermute | solution.py:322
  22.7 16.6 %collective-permute-start.10 = (bf16[40,2048]{1,0:T(8,128)(2,1)S(1)}, bf16[40,2048]{1,0:T(8,128)(2,1)S(1)}, u32[]{:S(2)}, u32[]{:S(2)}) collective-permute-start(bf16[40,2048]{1,0:T(8,128)(2,1)S(1)} %get-tuple-element.62), channel_id=1, source_target_pairs={{0,7},{1,6},{2,5},{3,4},{4,3},{5,2},{6,1},{7,0},{8,15},{9,14},{10,... | collective-permute-start | bytes 491528 | tf_op jit(solution)/shard_map/ppermute | solution.py:322
  23.5 2.6 %collective-permute-start.7 = (bf16[24,2048]{1,0:T(8,128)(2,1)S(1)}, bf16[24,2048]{1,0:T(8,128)(2,1)S(1)}, u32[]{:S(2)}, u32[]{:S(2)}) collective-permute-start(bf16[24,2048]{1,0:T(8,128)(2,1)S(1)} %slice.28), channel_id=1, source_target_pairs={{0,1},{1,0},{2,3},{3,2},{4,5},{5,4},{6,7},{7,6},{8,9},{9,8},{10,11... | collective-permute-start | bytes 294920 | tf_op jit(solution)/shard_map/ppermute | solution.py:322
  26.1 17.6 %collective-permute-start.3 = (bf16[88,1024]{1,0:T(8,128)(2,1)S(1)}, bf16[88,1024]{1,0:T(8,128)(2,1)S(1)}, u32[]{:S(2)}, u32[]{:S(2)}) collective-permute-start(bf16[88,1024]{1,0:T(8,128)(2,1)S(1)} %get-tuple-element.52), channel_id=1, source_target_pairs={{8,0},{9,1},{10,2},{11,3},{12,4},{13,5},{14,6},{15,7},{16,8},{17,9... | collective-permute-start | bytes 540680 | tf_op jit(solution)/shard_map/ppermute | solution.py:330
  29.2 14.5 %collective-permute-start.11 = (bf16[88,1024]{1,0:T(8,128)(2,1)S(1)}, bf16[88,1024]{1,0:T(8,128)(2,1)S(1)}, u32[]{:S(2)}, u32[]{:S(2)}) collective-permute-start(bf16[88,1024]{1,0:T(8,128)(2,1)S(1)} %get-tuple-element.67), channel_id=1, source_target_pairs={{8,2},{9,3},{10,0},{11,1},{12,6},{13,7},{14,4},{15,5},{16,10},{17,... | collective-permute-start | bytes 540680 | tf_op jit(solution)/shard_map/ppermute | solution.py:330
  36.4 13.6 %collective-permute-start.14 = (bf16[80,1024]{1,0:T(8,128)(2,1)S(1)}, bf16[80,1024]{1,0:T(8,128)(2,1)S(1)}, u32[]{:S(2)}, u32[]{:S(2)}) collective-permute-start(bf16[80,1024]{1,0:T(8,128)(2,1)S(1)} %get-tuple-element.75), channel_id=1, source_target_pairs={{8,4},{9,5},{10,6},{11,7},{12,0},{13,1},{14,2},{15,3},{16,12},{17,... | collective-permute-start | bytes 491528 | tf_op jit(solution)/shard_map/ppermute | solution.py:330
  41.6 13.0 %collective-permute-start.16 = (bf16[80,1024]{1,0:T(8,128)(2,1)S(1)}, bf16[80,1024]{1,0:T(8,128)(2,1)S(1)}, u32[]{:S(2)}, u32[]{:S(2)}) collective-permute-start(bf16[80,1024]{1,0:T(8,128)(2,1)S(1)} %get-tuple-element.77), channel_id=1, source_target_pairs={{8,6},{9,7},{10,4},{11,5},{12,2},{13,3},{14,0},{15,1},{16,14},{17,... | collective-permute-start | bytes 491528 | tf_op jit(solution)/shard_map/ppermute | solution.py:330
  47.9 8.2 %collective-permute-start.12 = (bf16[40,1024]{1,0:T(8,128)(2,1)S(1)}, bf16[40,1024]{1,0:T(8,128)(2,1)S(1)}, u32[]{:S(2)}, u32[]{:S(2)}) collective-permute-start(bf16[40,1024]{1,0:T(8,128)(2,1)S(1)} %slice.24), channel_id=1, source_target_pairs={{0,1},{1,0},{2,3},{3,2},{4,5},{5,4},{6,7},{7,6},{8,9},{9,8},{10,11... | collective-permute-start | bytes 245768 | tf_op jit(solution)/shard_map/ppermute | solution.py:322
  48.6 7.5 %collective-permute-start.13 = (bf16[40,1024]{1,0:T(8,128)(2,1)S(1)}, bf16[40,1024]{1,0:T(8,128)(2,1)S(1)}, u32[]{:S(2)}, u32[]{:S(2)}) collective-permute-start(bf16[40,1024]{1,0:T(8,128)(2,1)S(1)} %slice.25), channel_id=1, source_target_pairs={{0,1},{1,0},{2,3},{3,2},{4,5},{5,4},{6,7},{7,6},{8,9},{9,8},{10,11... | collective-permute-start | bytes 245768 | tf_op jit(solution)/shard_map/ppermute | solution.py:322
  50.0 6.1 %collective-permute-start.15 = (bf16[40,1024]{1,0:T(8,128)(2,1)S(1)}, bf16[40,1024]{1,0:T(8,128)(2,1)S(1)}, u32[]{:S(2)}, u32[]{:S(2)}) collective-permute-start(bf16[40,1024]{1,0:T(8,128)(2,1)S(1)} %slice.26), channel_id=1, source_target_pairs={{0,1},{1,0},{2,3},{3,2},{4,5},{5,4},{6,7},{7,6},{8,9},{9,8},{10,11... | collective-permute-start | bytes 245768 | tf_op jit(solution)/shard_map/ppermute | solution.py:322
  54.6 2.4 %collective-permute-start.17 = (bf16[40,1024]{1,0:T(8,128)(2,1)S(1)}, bf16[40,1024]{1,0:T(8,128)(2,1)S(1)}, u32[]{:S(2)}, u32[]{:S(2)}) collective-permute-start(bf16[40,1024]{1,0:T(8,128)(2,1)S(1)} %slice.30), channel_id=1, source_target_pairs={{0,1},{1,0},{2,3},{3,2},{4,5},{5,4},{6,7},{7,6},{8,9},{9,8},{10,11... | collective-permute-start | bytes 245768 | tf_op jit(solution)/shard_map/ppermute | solution.py:322

commit v6 on v5

--- a/solution.py
+++ b/solution.py
@@ -70,11 +70,12 @@
     row_weight = jnp.sum(scaled, axis=1, keepdims=True)
     copies[4].wait()
     got = jnp.dot(pick_in, in_ref[...], preferred_element_type=F32)
+    scale = jnp.where(is_first(row_weight.shape), 1.0, row_weight)
     for i, ref in enumerate(grad_refs):
         copies[5 + i].wait()
         pick = pick_grad[:, i * share : (i + 1) * share]
-        got = got + row_weight * jnp.dot(pick, ref[...], preferred_element_type=F32)
-    got = got.astype(BF16)
+        got = got + jnp.dot(pick, ref[...], preferred_element_type=F32)
+    got = (scale * got).astype(BF16)
     start = 0
     for out in outs:
         out[...] = got[start : start + out.shape[0], :]

time: 59.1 us -> 59.1 us (level)
  no operation moved by 1% of the time
where the time goes in v6:
time: 59.1 us; the launch traced here: 58.7 us
  starting transfers between devices  30.6 us (52%)
  Pallas kernels  17.7 us (30%)
  waiting for transfers between devices  9.54 us (16%)
  between operations  0.78 us (1%)
    ppermute x6, starting transfers between devices, to_before(): return lax.ppermute(value, both_axes, pairs)  18.3 us
    ppermute x12, starting transfers between devices, to_partner(): return lax.ppermute(value, 'expert', [(i, i ^ k) for i in range(n_expert)])  12.2 us
    pallas_call x3, Pallas kernels, expert_chunk(): pl.pallas_call(functools.partial(expert_kernel, spans, bool(extra)), out_...  6.75 us
    ppermute x6, waiting for transfers between devices, to_before(): return lax.ppermute(value, both_axes, pairs)  4.81 us
    ppermute x12, waiting for transfers between devices, to_partner(): return lax.ppermute(value, 'expert', [(i, i ^ k) for i in range(n_expert)])  4.72 us
    pallas_call x1, Pallas kernels, weight_grads(): pl.pallas_call(functools.partial(weight_kernel, spans, chunks), out_shape...  4.13 us
    pallas_call x1, Pallas kernels, gather(): pl.pallas_call(functools.partial(gather_kernel, 2 * chips, shares), out_s...  2.81 us
    pallas_call x1, Pallas kernels, load(): pl.pallas_call(load_kernel, out_shape=[jax.ShapeDtypeStruct((width, 2 * h...  2.38 us
  transfers between devices with their start and end apart: 18, of which 6 were waited for; matrix products, arithmetic and copies ran while one was open for 0% of the time, Pallas kernels for 23%

profile of v6, /device:TPU:13, one launch (start us, length us, event | category | flops | bytes accessed | tf_op | source)
XLA Modules:
  0.0 58.7 jit_solution(7352777754258008569)
XLA Ops:
  0.6 2.8 %gather.1 = (s32[8,256]{1,0:T(8,128)S(1)}, bf16[128,2048]{1,0:T(8,128)(2,1)S(1)}, bf16[128,2048]{1,0:T(8,128)(2,1)S(1)}, bf16[40,2048]{1,0:T(8,128)(2,1)S(1)}, b...) custom-call(s32[8,256]{1,0:T(8,128)} %bitcast.27, ...), custom_call_target="tpu_custom_call" | custom-call | flops 1 | bytes 1 | tf_op jit(solution)/shard_map/gather/pallas_call | solution.py:89
  3.7 2.3 %collective-permute-start.6 = (bf16[80,2048]{1,0:T(8,128)(2,1)S(1)}, bf16[80,2048]{1,0:T(8,128)(2,1)S(1)}, u32[]{:S(2)}, u32[]{:S(2)}) collective-permute-start(bf16[80,2048]{1,0:T(8,128)(2,1)S(1)} %get-tuple-element.55), channel_id=1, source_target_pairs={{0,4},{1,5},{2,6},{3,7},{4,0},{5,1},{6,2},{7,3},{8,12},{9,13},{10,... | collective-permute-start | bytes 983048 | tf_op jit(solution)/shard_map/ppermute | solution.py:323
  6.0 3.0 %collective-permute-start.4 = (bf16[128,2048]{1,0:T(8,128)(2,1)S(1)}, bf16[128,2048]{1,0:T(8,128)(2,1)S(1)}, u32[]{:S(2)}, u32[]{:S(2)}) collective-permute-start(bf16[128,2048]{1,0:T(8,128)(2,1)S(1)} %get-tuple-element.53), channel_id=1, source_target_pairs={{8,0},{9,1},{10,2},{11,3},{12,4},{13,5},{14,6},{15,7},{16,8},{17,9... | collective-permute-start | bytes 1572872 | tf_op jit(solution)/shard_map/ppermute | solution.py:331
  9.0 2.2 %collective-permute-start.5 = (bf16[128,2048]{1,0:T(8,128)(2,1)S(1)}, bf16[128,2048]{1,0:T(8,128)(2,1)S(1)}, u32[]{:S(2)}, u32[]{:S(2)}) collective-permute-start(bf16[128,2048]{1,0:T(8,128)(2,1)S(1)} %get-tuple-element.54), channel_id=1, source_target_pairs={{8,0},{9,1},{10,2},{11,3},{12,4},{13,5},{14,6},{15,7},{16,8},{17,9... | collective-permute-start | bytes 1572872 | tf_op jit(solution)/shard_map/ppermute | solution.py:331
  11.2 1.9 %collective-permute-start = (bf16[40,2048]{1,0:T(8,128)(2,1)S(1)}, bf16[40,2048]{1,0:T(8,128)(2,1)S(1)}, u32[]{:S(2)}, u32[]{:S(2)}) collective-permute-start(bf16[40,2048]{1,0:T(8,128)(2,1)S(1)} %get-tuple-element.44), channel_id=1, source_target_pairs={{0,1},{1,0},{2,3},{3,2},{4,5},{5,4},{6,7},{7,6},{8,9},{9,8},{10,11... | collective-permute-start | bytes 491528 | tf_op jit(solution)/shard_map/ppermute | solution.py:323
  13.1 2.4 %load.1 = (bf16[2048,768]{1,0:T(8,128)(2,1)S(1)}, bf16[384,2048]{1,0:T(8,128)(2,1)S(1)}) custom-call(bf16[2048,384]{1,0:T(8,128)(2,1)} %bitcast.21, bf16[2048,384]{1,0:T(8,128)(2,1)} %bitcast.22, bf16[384,2048]{1,0:T(8,128)(2,1)} %bitcast.23), custom_call_target="tpu_custom_call" | custom-call | flops 1 | bytes 1 | tf_op jit(solution)/shard_map/load/pallas_call | solution.py:127
  15.5 1.5 %collective-permute-done.1.refs_3_.refs_2_ = bf16[80,2048]{1,0:T(8,128)(2,1)S(1)} collective-permute-done((bf16[80,2048]{1,0:T(8,128)(2,1)S(1)}, bf16[80,2048]{1,0:T(8,128)(2,1)S(1)}, u32[]{:S(2)}, u32[]{:S(2)}) %collective-permute-start.1) | collective-permute-done | bytes 327712 | tf_op jit(solution)/shard_map/ppermute | solution.py:323
  17.0 1.6 %collective-permute-start.2 = (bf16[40,2048]{1,0:T(8,128)(2,1)S(1)}, bf16[40,2048]{1,0:T(8,128)(2,1)S(1)}, u32[]{:S(2)}, u32[]{:S(2)}) collective-permute-start(bf16[40,2048]{1,0:T(8,128)(2,1)S(1)} %slice.21), channel_id=1, source_target_pairs={{0,1},{1,0},{2,3},{3,2},{4,5},{5,4},{6,7},{7,6},{8,9},{9,8},{10,11... | collective-permute-start | bytes 491528 | tf_op jit(solution)/shard_map/ppermute | solution.py:323
  18.6 1.6 %collective-permute-done.6.refs_0_.refs_4_ = bf16[80,2048]{1,0:T(8,128)(2,1)S(1)} collective-permute-done((bf16[80,2048]{1,0:T(8,128)(2,1)S(1)}, bf16[80,2048]{1,0:T(8,128)(2,1)S(1)}, u32[]{:S(2)}, u32[]{:S(2)}) %collective-permute-start.6) | collective-permute-done | bytes 327712 | tf_op jit(solution)/shard_map/ppermute | solution.py:323
  20.2 1.6 %collective-permute-start.8 = (bf16[16,2048]{1,0:T(8,128)(2,1)S(1)}, bf16[16,2048]{1,0:T(8,128)(2,1)S(1)}, u32[]{:S(2)}, u32[]{:S(2)}) collective-permute-start(bf16[16,2048]{1,0:T(8,128)(2,1)S(1)} %slice.29), channel_id=1, source_target_pairs={{0,1},{1,0},{2,3},{3,2},{4,5},{5,4},{6,7},{7,6},{8,9},{9,8},{10,11... | collective-permute-start | bytes 196616 | tf_op jit(solution)/shard_map/ppermute | solution.py:323
  23.7 2.4 %expert.3 = (bf16[88,1024]{1,0:T(8,128)(2,1)S(1)}, bf16[88,1024]{1,0:T(8,128)(2,1)S(1)}, bf16[160,768]{1,0:T(8,128)(2,1)S(1)}, bf16[160,384]{1,0:T(8,128)(2,1)S(1)}) custom-call(s32[8,256]{1,0:T(8,128)S(1)} %get-tuple-element.42.refs_0_, bf16[40,2048]{1,0:T(8,128)(2,1)S(1)} %get-tuple-element.43.refs_1_.refs_0_, ...), custom_call_target="tpu_custom_call" | custom-call | flops 1 | bytes 1 | tf_op jit(solution)/shard_map/expert/pallas_call | solution.py:204
  26.1 3.1 %collective-permute-start.3 = (bf16[88,1024]{1,0:T(8,128)(2,1)S(1)}, bf16[88,1024]{1,0:T(8,128)(2,1)S(1)}, u32[]{:S(2)}, u32[]{:S(2)}) collective-permute-start(bf16[88,1024]{1,0:T(8,128)(2,1)S(1)} %get-tuple-element.52), channel_id=1, source_target_pairs={{8,0},{9,1},{10,2},{11,3},{12,4},{13,5},{14,6},{15,7},{16,8},{17,9... | collective-permute-start | bytes 540680 | tf_op jit(solution)/shard_map/ppermute | solution.py:331
  29.2 5.0 %collective-permute-start.11 = (bf16[88,1024]{1,0:T(8,128)(2,1)S(1)}, bf16[88,1024]{1,0:T(8,128)(2,1)S(1)}, u32[]{:S(2)}, u32[]{:S(2)}) collective-permute-start(bf16[88,1024]{1,0:T(8,128)(2,1)S(1)} %get-tuple-element.67), channel_id=1, source_target_pairs={{8,2},{9,3},{10,0},{11,1},{12,6},{13,7},{14,4},{15,5},{16,10},{17,... | collective-permute-start | bytes 540680 | tf_op jit(solution)/shard_map/ppermute | solution.py:331
  34.2 2.2 %expert.4 = (bf16[80,1024]{1,0:T(8,128)(2,1)S(1)}, bf16[80,768]{1,0:T(8,128)(2,1)S(1)}, bf16[80,384]{1,0:T(8,128)(2,1)S(1)}) custom-call(bf16[80,2048]{1,0:T(8,128)(2,1)S(1)} %collective-permute-done.6.refs_0_.refs_4_, bf16[24,2048]{1,0:T(8,128)(2,1)S(1)} %collective-permute-done.7.refs_1_.refs_5_, ...), custom_call_target="tpu_custom_call" | custom-call | flops 1 | bytes 1 | tf_op jit(solution)/shard_map/expert/pallas_call | solution.py:204
  36.4 2.9 %collective-permute-start.14 = (bf16[80,1024]{1,0:T(8,128)(2,1)S(1)}, bf16[80,1024]{1,0:T(8,128)(2,1)S(1)}, u32[]{:S(2)}, u32[]{:S(2)}) collective-permute-start(bf16[80,1024]{1,0:T(8,128)(2,1)S(1)} %get-tuple-element.75), channel_id=1, source_target_pairs={{8,4},{9,5},{10,6},{11,7},{12,0},{13,1},{14,2},{15,3},{16,12},{17,... | collective-permute-start | bytes 491528 | tf_op jit(solution)/shard_map/ppermute | solution.py:331
  39.4 2.2 %expert.5 = (bf16[80,1024]{1,0:T(8,128)(2,1)S(1)}, bf16[80,768]{1,0:T(8,128)(2,1)S(1)}, bf16[80,384]{1,0:T(8,128)(2,1)S(1)}) custom-call(bf16[40,2048]{1,0:T(8,128)(2,1)S(1)} %collective-permute-done.9.refs_0_.refs_7_, bf16[40,2048]{1,0:T(8,128)(2,1)S(1)} %collective-permute-done.10.refs_1_.refs_8_, ...), custom_call_target="tpu_custom_call" | custom-call | flops 1 | bytes 1 | tf_op jit(solution)/shard_map/expert/pallas_call | solution.py:204
  41.6 2.1 %collective-permute-start.16 = (bf16[80,1024]{1,0:T(8,128)(2,1)S(1)}, bf16[80,1024]{1,0:T(8,128)(2,1)S(1)}, u32[]{:S(2)}, u32[]{:S(2)}) collective-permute-start(bf16[80,1024]{1,0:T(8,128)(2,1)S(1)} %get-tuple-element.77), channel_id=1, source_target_pairs={{8,6},{9,7},{10,4},{11,5},{12,2},{13,3},{14,0},{15,1},{16,14},{17,... | collective-permute-start | bytes 491528 | tf_op jit(solution)/shard_map/ppermute | solution.py:331
  43.7 4.1 %weight_grads.1 = (bf16[2048,384]{1,0:T(8,128)(2,1)}, bf16[2048,384]{1,0:T(8,128)(2,1)}, bf16[384,2048]{1,0:T(8,128)(2,1)}) custom-call(bf16[40,2048]{1,0:T(8,128)(2,1)S(1)} %get-tuple-element.43.refs_1_.refs_0_, bf16[40,2048]{1,0:T(8,128)(2,1)S(1)} %collective-permute-done.refs_2_.refs_1_, bf16[80,2048]{1,0:T(8,128)(2,1)S(1)} %collective-permute-done.1.refs_3_.refs_2_, ...), custom_call_target="tpu_custom_call" | custom-call | flops 1 | bytes 1 | tf_op jit(solution)/shard_map/weight_grads/pallas_call | solution.py:237
  48.6 1.3 %collective-permute-done.14.refs_6_ = bf16[80,1024]{1,0:T(8,128)(2,1)S(1)} collective-permute-done((bf16[80,1024]{1,0:T(8,128)(2,1)S(1)}, bf16[80,1024]{1,0:T(8,128)(2,1)S(1)}, u32[]{:S(2)}, u32[]{:S(2)}) %collective-permute-start.14) | collective-permute-done | bytes 163872 | tf_op jit(solution)/shard_map/ppermute | solution.py:331
  50.0 1.2 %collective-permute-start.15 = (bf16[40,1024]{1,0:T(8,128)(2,1)S(1)}, bf16[40,1024]{1,0:T(8,128)(2,1)S(1)}, u32[]{:S(2)}, u32[]{:S(2)}) collective-permute-start(bf16[40,1024]{1,0:T(8,128)(2,1)S(1)} %slice.26), channel_id=1, source_target_pairs={{0,1},{1,0},{2,3},{3,2},{4,5},{5,4},{6,7},{7,6},{8,9},{9,8},{10,11... | collective-permute-start | bytes 245768 | tf_op jit(solution)/shard_map/ppermute | solution.py:323
  51.1 3.5 %collective-permute-done.16.refs_8_ = bf16[80,1024]{1,0:T(8,128)(2,1)S(1)} collective-permute-done((bf16[80,1024]{1,0:T(8,128)(2,1)S(1)}, bf16[80,1024]{1,0:T(8,128)(2,1)S(1)}, u32[]{:S(2)}, u32[]{:S(2)}) %collective-permute-start.16) | collective-permute-done | bytes 163872 | tf_op jit(solution)/shard_map/ppermute | solution.py:331
  54.6 1.5 %collective-permute-start.17 = (bf16[40,1024]{1,0:T(8,128)(2,1)S(1)}, bf16[40,1024]{1,0:T(8,128)(2,1)S(1)}, u32[]{:S(2)}, u32[]{:S(2)}) collective-permute-start(bf16[40,1024]{1,0:T(8,128)(2,1)S(1)} %slice.30), channel_id=1, source_target_pairs={{0,1},{1,0},{2,3},{3,2},{4,5},{5,4},{6,7},{7,6},{8,9},{9,8},{10,11... | collective-permute-start | bytes 245768 | tf_op jit(solution)/shard_map/ppermute | solution.py:323
  56.1 0.9 %collective-permute-done.17.refs_9_ = bf16[40,1024]{1,0:T(8,128)(2,1)S(1)} collective-permute-done((bf16[40,1024]{1,0:T(8,128)(2,1)S(1)}, bf16[40,1024]{1,0:T(8,128)(2,1)S(1)}, u32[]{:S(2)}, u32[]{:S(2)}) %collective-permute-start.17) | collective-permute-done | bytes 81952 | tf_op jit(solution)/shard_map/ppermute | solution.py:323
  57.0 1.7 %combine.1 = bf16[256,2048]{1,0:T(8,128)(2,1)} custom-call(bf16[88,1024]{1,0:T(8,128)(2,1)S(1)} %collective-permute-done.3.keys_ref.refs_2_, bf16[128,2048]{1,0:T(8,128)(2,1)S(1)} %collective-permute-done.4.refs_0_, bf16[128,2048]{1,0:T(8,128)(2,1)S(1)} %collective-permute-done.5.refs_1_, bf16[88,1024]{1,0:T(8,128)(2,1)S(1)} %collective-permute-done.3.keys_ref.refs_2_, ...), custom_call_target="tpu_custom_call" | custom-call | flops 1 | bytes 1 | tf_op jit(solution)/shard_map/combine/pallas_call | solution.py:289
  (26 shorter events, 3.0 us)
Async XLA Ops:
  3.4 13.5 %collective-permute-start.1 = (bf16[80,2048]{1,0:T(8,128)(2,1)S(1)}, bf16[80,2048]{1,0:T(8,128)(2,1)S(1)}, u32[]{:S(2)}, u32[]{:S(2)}) collective-permute-start(bf16[80,2048]{1,0:T(8,128)(2,1)S(1)} %get-tuple-element.45), channel_id=1, source_target_pairs={{0,2},{1,3},{2,0},{3,1},{4,6},{5,7},{6,4},{7,5},{8,10},{9,11},{10,... | collective-permute-start | bytes 983048 | tf_op jit(solution)/shard_map/ppermute | solution.py:323
  3.7 16.5 %collective-permute-start.6 = (bf16[80,2048]{1,0:T(8,128)(2,1)S(1)}, bf16[80,2048]{1,0:T(8,128)(2,1)S(1)}, u32[]{:S(2)}, u32[]{:S(2)}) collective-permute-start(bf16[80,2048]{1,0:T(8,128)(2,1)S(1)} %get-tuple-element.55), channel_id=1, source_target_pairs={{0,4},{1,5},{2,6},{3,7},{4,0},{5,1},{6,2},{7,3},{8,12},{9,13},{10,... | collective-permute-start | bytes 983048 | tf_op jit(solution)/shard_map/ppermute | solution.py:323
  6.0 23.2 %collective-permute-start.4 = (bf16[128,2048]{1,0:T(8,128)(2,1)S(1)}, bf16[128,2048]{1,0:T(8,128)(2,1)S(1)}, u32[]{:S(2)}, u32[]{:S(2)}) collective-permute-start(bf16[128,2048]{1,0:T(8,128)(2,1)S(1)} %get-tuple-element.53), channel_id=1, source_target_pairs={{8,0},{9,1},{10,2},{11,3},{12,4},{13,5},{14,6},{15,7},{16,8},{17,9... | collective-permute-start | bytes 1572872 | tf_op jit(solution)/shard_map/ppermute | solution.py:331
  9.0 30.3 %collective-permute-start.5 = (bf16[128,2048]{1,0:T(8,128)(2,1)S(1)}, bf16[128,2048]{1,0:T(8,128)(2,1)S(1)}, u32[]{:S(2)}, u32[]{:S(2)}) collective-permute-start(bf16[128,2048]{1,0:T(8,128)(2,1)S(1)} %get-tuple-element.54), channel_id=1, source_target_pairs={{8,0},{9,1},{10,2},{11,3},{12,4},{13,5},{14,6},{15,7},{16,8},{17,9... | collective-permute-start | bytes 1572872 | tf_op jit(solution)/shard_map/ppermute | solution.py:331
  11.2 10.6 %collective-permute-start = (bf16[40,2048]{1,0:T(8,128)(2,1)S(1)}, bf16[40,2048]{1,0:T(8,128)(2,1)S(1)}, u32[]{:S(2)}, u32[]{:S(2)}) collective-permute-start(bf16[40,2048]{1,0:T(8,128)(2,1)S(1)} %get-tuple-element.44), channel_id=1, source_target_pairs={{0,1},{1,0},{2,3},{3,2},{4,5},{5,4},{6,7},{7,6},{8,9},{9,8},{10,11... | collective-permute-start | bytes 491528 | tf_op jit(solution)/shard_map/ppermute | solution.py:323
  17.0 6.5 %collective-permute-start.2 = (bf16[40,2048]{1,0:T(8,128)(2,1)S(1)}, bf16[40,2048]{1,0:T(8,128)(2,1)S(1)}, u32[]{:S(2)}, u32[]{:S(2)}) collective-permute-start(bf16[40,2048]{1,0:T(8,128)(2,1)S(1)} %slice.21), channel_id=1, source_target_pairs={{0,1},{1,0},{2,3},{3,2},{4,5},{5,4},{6,7},{7,6},{8,9},{9,8},{10,11... | collective-permute-start | bytes 491528 | tf_op jit(solution)/shard_map/ppermute | solution.py:323
  20.2 2.5 %collective-permute-start.8 = (bf16[16,2048]{1,0:T(8,128)(2,1)S(1)}, bf16[16,2048]{1,0:T(8,128)(2,1)S(1)}, u32[]{:S(2)}, u32[]{:S(2)}) collective-permute-start(bf16[16,2048]{1,0:T(8,128)(2,1)S(1)} %slice.29), channel_id=1, source_target_pairs={{0,1},{1,0},{2,3},{3,2},{4,5},{5,4},{6,7},{7,6},{8,9},{9,8},{10,11... | collective-permute-start | bytes 196616 | tf_op jit(solution)/shard_map/ppermute | solution.py:323
  21.8 14.6 %collective-permute-start.9 = (bf16[40,2048]{1,0:T(8,128)(2,1)S(1)}, bf16[40,2048]{1,0:T(8,128)(2,1)S(1)}, u32[]{:S(2)}, u32[]{:S(2)}) collective-permute-start(bf16[40,2048]{1,0:T(8,128)(2,1)S(1)} %get-tuple-element.61), channel_id=1, source_target_pairs={{0,6},{1,7},{2,4},{3,5},{4,2},{5,3},{6,0},{7,1},{8,14},{9,15},{10,... | collective-permute-start | bytes 491528 | tf_op jit(solution)/shard_map/ppermute | solution.py:323
  22.7 16.7 %collective-permute-start.10 = (bf16[40,2048]{1,0:T(8,128)(2,1)S(1)}, bf16[40,2048]{1,0:T(8,128)(2,1)S(1)}, u32[]{:S(2)}, u32[]{:S(2)}) collective-permute-start(bf16[40,2048]{1,0:T(8,128)(2,1)S(1)} %get-tuple-element.62), channel_id=1, source_target_pairs={{0,7},{1,6},{2,5},{3,4},{4,3},{5,2},{6,1},{7,0},{8,15},{9,14},{10,... | collective-permute-start | bytes 491528 | tf_op jit(solution)/shard_map/ppermute | solution.py:323
  23.5 2.6 %collective-permute-start.7 = (bf16[24,2048]{1,0:T(8,128)(2,1)S(1)}, bf16[24,2048]{1,0:T(8,128)(2,1)S(1)}, u32[]{:S(2)}, u32[]{:S(2)}) collective-permute-start(bf16[24,2048]{1,0:T(8,128)(2,1)S(1)} %slice.28), channel_id=1, source_target_pairs={{0,1},{1,0},{2,3},{3,2},{4,5},{5,4},{6,7},{7,6},{8,9},{9,8},{10,11... | collective-permute-start | bytes 294920 | tf_op jit(solution)/shard_map/ppermute | solution.py:323
  26.1 17.6 %collective-permute-start.3 = (bf16[88,1024]{1,0:T(8,128)(2,1)S(1)}, bf16[88,1024]{1,0:T(8,128)(2,1)S(1)}, u32[]{:S(2)}, u32[]{:S(2)}) collective-permute-start(bf16[88,1024]{1,0:T(8,128)(2,1)S(1)} %get-tuple-element.52), channel_id=1, source_target_pairs={{8,0},{9,1},{10,2},{11,3},{12,4},{13,5},{14,6},{15,7},{16,8},{17,9... | collective-permute-start | bytes 540680 | tf_op jit(solution)/shard_map/ppermute | solution.py:331
  29.2 14.5 %collective-permute-start.11 = (bf16[88,1024]{1,0:T(8,128)(2,1)S(1)}, bf16[88,1024]{1,0:T(8,128)(2,1)S(1)}, u32[]{:S(2)}, u32[]{:S(2)}) collective-permute-start(bf16[88,1024]{1,0:T(8,128)(2,1)S(1)} %get-tuple-element.67), channel_id=1, source_target_pairs={{8,2},{9,3},{10,0},{11,1},{12,6},{13,7},{14,4},{15,5},{16,10},{17,... | collective-permute-start | bytes 540680 | tf_op jit(solution)/shard_map/ppermute | solution.py:331
  36.4 13.6 %collective-permute-start.14 = (bf16[80,1024]{1,0:T(8,128)(2,1)S(1)}, bf16[80,1024]{1,0:T(8,128)(2,1)S(1)}, u32[]{:S(2)}, u32[]{:S(2)}) collective-permute-start(bf16[80,1024]{1,0:T(8,128)(2,1)S(1)} %get-tuple-element.75), channel_id=1, source_target_pairs={{8,4},{9,5},{10,6},{11,7},{12,0},{13,1},{14,2},{15,3},{16,12},{17,... | collective-permute-start | bytes 491528 | tf_op jit(solution)/shard_map/ppermute | solution.py:331
  41.6 13.0 %collective-permute-start.16 = (bf16[80,1024]{1,0:T(8,128)(2,1)S(1)}, bf16[80,1024]{1,0:T(8,128)(2,1)S(1)}, u32[]{:S(2)}, u32[]{:S(2)}) collective-permute-start(bf16[80,1024]{1,0:T(8,128)(2,1)S(1)} %get-tuple-element.77), channel_id=1, source_target_pairs={{8,6},{9,7},{10,4},{11,5},{12,2},{13,3},{14,0},{15,1},{16,14},{17,... | collective-permute-start | bytes 491528 | tf_op jit(solution)/shard_map/ppermute | solution.py:331
  47.9 8.2 %collective-permute-start.12 = (bf16[40,1024]{1,0:T(8,128)(2,1)S(1)}, bf16[40,1024]{1,0:T(8,128)(2,1)S(1)}, u32[]{:S(2)}, u32[]{:S(2)}) collective-permute-start(bf16[40,1024]{1,0:T(8,128)(2,1)S(1)} %slice.24), channel_id=1, source_target_pairs={{0,1},{1,0},{2,3},{3,2},{4,5},{5,4},{6,7},{7,6},{8,9},{9,8},{10,11... | collective-permute-start | bytes 245768 | tf_op jit(solution)/shard_map/ppermute | solution.py:323
  48.5 7.6 %collective-permute-start.13 = (bf16[40,1024]{1,0:T(8,128)(2,1)S(1)}, bf16[40,1024]{1,0:T(8,128)(2,1)S(1)}, u32[]{:S(2)}, u32[]{:S(2)}) collective-permute-start(bf16[40,1024]{1,0:T(8,128)(2,1)S(1)} %slice.25), channel_id=1, source_target_pairs={{0,1},{1,0},{2,3},{3,2},{4,5},{5,4},{6,7},{7,6},{8,9},{9,8},{10,11... | collective-permute-start | bytes 245768 | tf_op jit(solution)/shard_map/ppermute | solution.py:323
  50.0 6.1 %collective-permute-start.15 = (bf16[40,1024]{1,0:T(8,128)(2,1)S(1)}, bf16[40,1024]{1,0:T(8,128)(2,1)S(1)}, u32[]{:S(2)}, u32[]{:S(2)}) collective-permute-start(bf16[40,1024]{1,0:T(8,128)(2,1)S(1)} %slice.26), channel_id=1, source_target_pairs={{0,1},{1,0},{2,3},{3,2},{4,5},{5,4},{6,7},{7,6},{8,9},{9,8},{10,11... | collective-permute-start | bytes 245768 | tf_op jit(solution)/shard_map/ppermute | solution.py:323
  54.6 2.4 %collective-permute-start.17 = (bf16[40,1024]{1,0:T(8,128)(2,1)S(1)}, bf16[40,1024]{1,0:T(8,128)(2,1)S(1)}, u32[]{:S(2)}, u32[]{:S(2)}) collective-permute-start(bf16[40,1024]{1,0:T(8,128)(2,1)S(1)} %slice.30), channel_id=1, source_target_pairs={{0,1},{1,0},{2,3},{3,2},{4,5},{5,4},{6,7},{7,6},{8,9},{9,8},{10,11... | collective-permute-start | bytes 245768 | tf_op jit(solution)/shard_map/ppermute | solution.py:323

commit v7 on v6

--- a/solution.py
+++ b/solution.py
@@ -9,7 +9,7 @@
 
 CAP = 20
 PAIR = 2 * CAP
-SHARES = 2
+SHARES = 1
 F32 = jnp.float32
 BF16 = jnp.bfloat16
 SHORT = pl.CostEstimate(flops=1, transcendentals=0, bytes_accessed=1)
@@ -105,17 +105,19 @@
     return keys, held, [[outs.pop(0), outs.pop(0)] if c in apart else outs.pop(0) for c in range(chips)]
 
 
-def load_kernel(gate_hbm, up_hbm, down_hbm, both_ref, down_ref, sem):
+def load_kernel(gate_hbm, up_hbm, down_hbm, both_ref, back_ref, down_ref, held_ref, sem):
     hidden = gate_hbm.shape[1]
     copies = [
         pltpu.make_async_copy(gate_hbm, both_ref.at[:, :hidden], sem.at[0]),
         pltpu.make_async_copy(up_hbm, both_ref.at[:, hidden:], sem.at[1]),
-        pltpu.make_async_copy(down_hbm, down_ref, sem.at[2]),
+        pltpu.make_async_copy(down_hbm, held_ref, sem.at[2]),
     ]
     for copy in copies:
         copy.start()
     for copy in copies:
         copy.wait()
+    down_ref[...] = held_ref[...].T
+    back_ref[...] = both_ref[...].T
 
 
 def pinned(arrays):
@@ -128,13 +130,14 @@
         load_kernel,
         out_shape=[
             jax.ShapeDtypeStruct((width, 2 * hidden), BF16),
-            jax.ShapeDtypeStruct((hidden, width), BF16),
+            jax.ShapeDtypeStruct((2 * hidden, width), BF16),
+            jax.ShapeDtypeStruct((width, hidden), BF16),
         ],
         in_specs=[pl.BlockSpec(memory_space=pltpu.HBM)] * 3,
-        out_specs=vmem(2),
-        scratch_shapes=[pltpu.SemaphoreType.DMA((3,))],
+        out_specs=vmem(3),
+        scratch_shapes=[pltpu.VMEM((hidden, width), BF16), pltpu.SemaphoreType.DMA((3,))],
         name="load",
-        compiler_params=pltpu.CompilerParams(vmem_limit_bytes=12 << 20),
+        compiler_params=pltpu.CompilerParams(vmem_limit_bytes=24 << 20),
         cost_estimate=SHORT,
     )(*pinned((w_gate, w_up, w_down)))
 
@@ -156,16 +159,16 @@
     if with_keys:
         keys_ref, refs = refs[0], refs[1:]
     payloads = refs[:count]
-    w_both, w_down = refs[count : count + 2]
-    returns = refs[count + 2 : -2]
+    w_both, w_back, w_down = refs[count : count + 3]
+    returns = refs[count + 3 : -2]
     grads_out, hidden_out = refs[-2:]
     rows = sum(hi - lo for lo, hi in spans)
-    width, units = w_down.shape[1], w_down.shape[0]
+    width, units = w_down.shape
     half = width // 2
     both = joined(payloads, spans)
     pre = jnp.dot(both, w_both[...], preferred_element_type=F32)
     gate_pre, up_pre = pre[:, :units], pre[:, units:]
-    hidden_grad = pltpu.roll(nt(both, w_down[...]), rows - CAP, 0)
+    hidden_grad = pltpu.roll(jnp.dot(both, w_down[...], preferred_element_type=F32), rows - CAP, 0)
     first = is_first(gate_pre.shape)
     sigma = jax.nn.sigmoid(gate_pre)
     active = gate_pre * sigma
@@ -175,8 +178,8 @@
     up_grad = jnp.where(first, hidden_grad * active, 0.0)
     grads = jnp.concatenate([gate_grad, up_grad], axis=1)
     grads_two = (grads + pltpu.roll(grads, CAP, 0)).astype(BF16)
-    left = nt(grads_two, w_both[:half, :])
-    right = nt(grads_two, w_both[half:, :])
+    left = jnp.dot(grads_two, w_back[:, :half], preferred_element_type=F32)
+    right = jnp.dot(grads_two, w_back[:, half:], preferred_element_type=F32)
     row_grad = jnp.where(is_first(left.shape), left, right).astype(BF16)
     step = rows // len(returns)
     for k, out in enumerate(returns):
@@ -193,10 +196,10 @@
             out[2 * PAIR :, 2 * tokens :] = jnp.zeros((ranks, half - 2 * tokens), BF16)
 
 
-def expert_chunk(pieces, w_both, w_down, keys=None):
+def expert_chunk(pieces, weights, keys=None):
     arrays, spans = [p[0] for p in pieces], [p[1] for p in pieces]
     total = sum(hi - lo for lo, hi in spans)
-    hidden, width = w_down.shape
+    width, hidden = weights[2].shape
     extra = [] if keys is None else [keys]
     rows = [2 * PAIR] * (total // (2 * PAIR))
     if extra:
@@ -205,12 +208,12 @@
         functools.partial(expert_kernel, spans, bool(extra)),
         out_shape=[jax.ShapeDtypeStruct((r, width // 2), BF16) for r in rows]
         + [jax.ShapeDtypeStruct((total, n * hidden), BF16) for n in (2, 1)],
-        in_specs=vmem(len(extra) + len(pieces) + 2),
+        in_specs=vmem(len(extra) + len(pieces) + 3),
         out_specs=vmem(len(rows) + 2),
         name="expert",
         compiler_params=pltpu.CompilerParams(vmem_limit_bytes=20 << 20),
         cost_estimate=SHORT,
-    )(*extra, *arrays, w_both, w_down)
+    )(*extra, *arrays, *weights)
     return out[: len(rows)], out[len(rows) :]
 
 
@@ -355,7 +358,7 @@
     arrived, order, small, returned = {}, [], [], {}
 
     def process(chunk, pieces, **options):
-        back, parts = expert_chunk(pieces, w_both, w_down, **options)
+        back, parts = expert_chunk(pieces, turned, **options)
         order.extend(pieces)
         small.append(parts)
         for c, value in zip(chunk, back):
@@ -369,13 +372,13 @@
     beside = to_partner(sent[0][1], 1)
     next_grads = [to_before(share, 0) for share in held]
     pieces = [(sent[0][0], mine), (beside, mine)]
-    w_both, w_down = load(*after((w_gate, w_up, w_down), sent[0][0]))
-    here = after([arrived[c] for c in near], w_down)
+    turned = load(*after((w_gate, w_up, w_down), sent[0][0]))
+    here = after([arrived[c] for c in near], turned)
     for value in here:
         pieces += forward(value)
     parts = process([0] + near, pieces, keys=keys)
     pieces = [piece for c in early for piece in forward(arrived[c], PAIR + 24)]
-    parts = process(early, gated(pieces, (parts, next_grads[0])))
+    parts = process(early, gated(pieces, parts))
     pieces = [piece for c in late for piece in arrived[c]]
     process(late, gated(pieces, (parts, next_grads)))
     small[0] = after(small[0], [returned[c] for c in [0] + near])

time: 59.1 us -> 58.7 us (level)
  waiting for transfers between devices: 9.54 us -> 11.8 us
  starting transfers between devices: 30.6 us -> 28.8 us
  Pallas kernels: 17.7 us -> 17 us
    ppermute x6 -> x5, starting transfers between devices: 18.3 us -> 15.7 us  [to_before(): return lax.ppermute(value, both_axes, pairs)]
    ppermute x12, waiting for transfers between devices: 4.72 us -> 6.79 us  [to_partner(): return lax.ppermute(value, 'expert', [(i, i ^ k) for i in range(n_expert)])]
    pallas_call x3, Pallas kernels: 6.75 us -> 4.91 us  [expert_chunk(): pl.pallas_call(functools.partial(expert_kernel, spans, bool(extra)), out_...]
    pallas_call x1, Pallas kernels: 2.38 us -> 3.72 us  [load(): pl.pallas_call(load_kernel, out_shape=[jax.ShapeDtypeStruct((width, 2 * h...]
    ppermute x12, starting transfers between devices: 12.2 us -> 13.1 us  [to_partner(): return lax.ppermute(value, 'expert', [(i, i ^ k) for i in range(n_expert)])]
    ppermute x6 -> x5, waiting for transfers between devices: 4.81 us -> 5.03 us  [to_before(): return lax.ppermute(value, both_axes, pairs)]
  transfers between devices with their start and end apart: 18 -> 17, of which waited for: 6 -> 5; matrix products, arithmetic and copies ran while one was open for 0% -> 0% of each run, Pallas kernels for 23% -> 22%
where the time goes in v7:
time: 58.7 us; the launch traced here: 58.4 us
  starting transfers between devices  28.8 us (49%)
  Pallas kernels  17 us (29%)
  waiting for transfers between devices  11.8 us (20%)
  between operations  0.79 us (1%)
    ppermute x5, starting transfers between devices, to_before(): return lax.ppermute(value, both_axes, pairs)  15.7 us
    ppermute x12, starting transfers between devices, to_partner(): return lax.ppermute(value, 'expert', [(i, i ^ k) for i in range(n_expert)])  13.1 us
    ppermute x12, waiting for transfers between devices, to_partner(): return lax.ppermute(value, 'expert', [(i, i ^ k) for i in range(n_expert)])  6.79 us
    ppermute x5, waiting for transfers between devices, to_before(): return lax.ppermute(value, both_axes, pairs)  5.03 us
    pallas_call x3, Pallas kernels, expert_chunk(): pl.pallas_call(functools.partial(expert_kernel, spans, bool(extra)), out_...  4.91 us
    pallas_call x1, Pallas kernels, weight_grads(): pl.pallas_call(functools.partial(weight_kernel, spans, chunks), out_shape...  4.14 us
    pallas_call x1, Pallas kernels, load(): pl.pallas_call(load_kernel, out_shape=[jax.ShapeDtypeStruct((width, 2 * h...  3.72 us
    pallas_call x1, Pallas kernels, gather(): pl.pallas_call(functools.partial(gather_kernel, 2 * chips, shares), out_s...  2.51 us
  transfers between devices with their start and end apart: 17, of which 5 were waited for; matrix products, arithmetic and copies ran while one was open for 0% of the time, Pallas kernels for 22%

profile of v7, /device:TPU:13, one launch (start us, length us, event | category | flops | bytes accessed | tf_op | source)
XLA Modules:
  0.0 58.4 jit_solution(16505244266790040317)
XLA Ops:
  0.6 2.5 %gather.1 = (s32[8,256]{1,0:T(8,128)S(1)}, bf16[256,2048]{1,0:T(8,128)(2,1)S(1)}, bf16[40,2048]{1,0:T(8,128)(2,1)S(1)}, bf16[40,2048]{1,0:T(8,128)(2,1)S(1)}, bf...) custom-call(s32[8,256]{1,0:T(8,128)} %bitcast.27, ...), custom_call_target="tpu_custom_call" | custom-call | flops 1 | bytes 1 | tf_op jit(solution)/shard_map/gather/pallas_call | solution.py:89
  3.2 3.1 %collective-permute-start.4 = (bf16[256,2048]{1,0:T(8,128)(2,1)S(1)}, bf16[256,2048]{1,0:T(8,128)(2,1)S(1)}, u32[]{:S(2)}, u32[]{:S(2)}) collective-permute-start(bf16[256,2048]{1,0:T(8,128)(2,1)S(1)} %get-tuple-element.54), channel_id=1, source_target_pairs={{8,0},{9,1},{10,2},{11,3},{12,4},{13,5},{14,6},{15,7},{16,8},{17,9... | collective-permute-start | bytes 3145736 | tf_op jit(solution)/shard_map/ppermute | solution.py:334
  6.5 2.3 %collective-permute-start.5 = (bf16[80,2048]{1,0:T(8,128)(2,1)S(1)}, bf16[80,2048]{1,0:T(8,128)(2,1)S(1)}, u32[]{:S(2)}, u32[]{:S(2)}) collective-permute-start(bf16[80,2048]{1,0:T(8,128)(2,1)S(1)} %get-tuple-element.55), channel_id=1, source_target_pairs={{0,4},{1,5},{2,6},{3,7},{4,0},{5,1},{6,2},{7,3},{8,12},{9,13},{10,... | collective-permute-start | bytes 983048 | tf_op jit(solution)/shard_map/ppermute | solution.py:326
  8.8 1.5 %collective-permute-start = (bf16[40,2048]{1,0:T(8,128)(2,1)S(1)}, bf16[40,2048]{1,0:T(8,128)(2,1)S(1)}, u32[]{:S(2)}, u32[]{:S(2)}) collective-permute-start(bf16[40,2048]{1,0:T(8,128)(2,1)S(1)} %get-tuple-element.44), channel_id=1, source_target_pairs={{0,1},{1,0},{2,3},{3,2},{4,5},{5,4},{6,7},{7,6},{8,9},{9,8},{10,11... | collective-permute-start | bytes 491528 | tf_op jit(solution)/shard_map/ppermute | solution.py:326
  10.3 3.7 %load.1 = (bf16[2048,768]{1,0:T(8,128)(2,1)S(1)}, bf16[768,2048]{1,0:T(8,128)(2,1)S(1)}, bf16[2048,384]{1,0:T(8,128)(2,1)S(1)}) custom-call(bf16[2048,384]{1,0:T(8,128)(2,1)} %bitcast.21, bf16[2048,384]{1,0:T(8,128)(2,1)} %bitcast.22, bf16[384,2048]{1,0:T(8,128)(2,1)} %bitcast.23), custom_call_target="tpu_custom_call" | custom-call | flops 1 | bytes 1 | tf_op jit(solution)/shard_map/load/pallas_call | solution.py:129
  14.0 5.4 %collective-permute-done.1.refs_3_.refs_2_ = bf16[80,2048]{1,0:T(8,128)(2,1)S(1)} collective-permute-done((bf16[80,2048]{1,0:T(8,128)(2,1)S(1)}, bf16[80,2048]{1,0:T(8,128)(2,1)S(1)}, u32[]{:S(2)}, u32[]{:S(2)}) %collective-permute-start.1) | collective-permute-done | bytes 327712 | tf_op jit(solution)/shard_map/ppermute | solution.py:326
  19.4 1.9 %collective-permute-start.2 = (bf16[40,2048]{1,0:T(8,128)(2,1)S(1)}, bf16[40,2048]{1,0:T(8,128)(2,1)S(1)}, u32[]{:S(2)}, u32[]{:S(2)}) collective-permute-start(bf16[40,2048]{1,0:T(8,128)(2,1)S(1)} %slice.21), channel_id=1, source_target_pairs={{0,1},{1,0},{2,3},{3,2},{4,5},{5,4},{6,7},{7,6},{8,9},{9,8},{10,11... | collective-permute-start | bytes 491528 | tf_op jit(solution)/shard_map/ppermute | solution.py:326
  21.4 1.3 %collective-permute-start.8 = (bf16[40,2048]{1,0:T(8,128)(2,1)S(1)}, bf16[40,2048]{1,0:T(8,128)(2,1)S(1)}, u32[]{:S(2)}, u32[]{:S(2)}) collective-permute-start(bf16[40,2048]{1,0:T(8,128)(2,1)S(1)} %get-tuple-element.61), channel_id=1, source_target_pairs={{0,6},{1,7},{2,4},{3,5},{4,2},{5,3},{6,0},{7,1},{8,14},{9,15},{10,... | collective-permute-start | bytes 491528 | tf_op jit(solution)/shard_map/ppermute | solution.py:326
  22.7 1.9 %collective-permute-start.9 = (bf16[40,2048]{1,0:T(8,128)(2,1)S(1)}, bf16[40,2048]{1,0:T(8,128)(2,1)S(1)}, u32[]{:S(2)}, u32[]{:S(2)}) collective-permute-start(bf16[40,2048]{1,0:T(8,128)(2,1)S(1)} %get-tuple-element.62), channel_id=1, source_target_pairs={{0,7},{1,6},{2,5},{3,4},{4,3},{5,2},{6,1},{7,0},{8,15},{9,14},{10,... | collective-permute-start | bytes 491528 | tf_op jit(solution)/shard_map/ppermute | solution.py:326
  24.7 0.5 collective-permute-start.7
  25.3 1.7 %expert.3 = (bf16[88,1024]{1,0:T(8,128)(2,1)S(1)}, bf16[88,1024]{1,0:T(8,128)(2,1)S(1)}, bf16[160,768]{1,0:T(8,128)(2,1)S(1)}, bf16[160,384]{1,0:T(8,128)(2,1)S(1)}) custom-call(s32[8,256]{1,0:T(8,128)S(1)} %get-tuple-element.42.refs_0_, bf16[40,2048]{1,0:T(8,128)(2,1)S(1)} %get-tuple-element.43.refs_1_.refs_0_, ...), custom_call_target="tpu_custom_call" | custom-call | flops 1 | bytes 1 | tf_op jit(solution)/shard_map/expert/pallas_call | solution.py:207
  27.0 2.2 %collective-permute-start.3 = (bf16[88,1024]{1,0:T(8,128)(2,1)S(1)}, bf16[88,1024]{1,0:T(8,128)(2,1)S(1)}, u32[]{:S(2)}, u32[]{:S(2)}) collective-permute-start(bf16[88,1024]{1,0:T(8,128)(2,1)S(1)} %get-tuple-element.53), channel_id=1, source_target_pairs={{8,0},{9,1},{10,2},{11,3},{12,4},{13,5},{14,6},{15,7},{16,8},{17,9... | collective-permute-start | bytes 540680 | tf_op jit(solution)/shard_map/ppermute | solution.py:334
  29.2 5.1 %collective-permute-start.10 = (bf16[88,1024]{1,0:T(8,128)(2,1)S(1)}, bf16[88,1024]{1,0:T(8,128)(2,1)S(1)}, u32[]{:S(2)}, u32[]{:S(2)}) collective-permute-start(bf16[88,1024]{1,0:T(8,128)(2,1)S(1)} %get-tuple-element.67), channel_id=1, source_target_pairs={{8,2},{9,3},{10,0},{11,1},{12,6},{13,7},{14,4},{15,5},{16,10},{17,... | collective-permute-start | bytes 540680 | tf_op jit(solution)/shard_map/ppermute | solution.py:334
  34.3 1.6 %expert.4 = (bf16[80,1024]{1,0:T(8,128)(2,1)S(1)}, bf16[80,768]{1,0:T(8,128)(2,1)S(1)}, bf16[80,384]{1,0:T(8,128)(2,1)S(1)}) custom-call(bf16[80,2048]{1,0:T(8,128)(2,1)S(1)} %collective-permute-done.5.refs_0_.refs_4_, bf16[24,2048]{1,0:T(8,128)(2,1)S(1)} %collective-permute-done.6.refs_1_.refs_5_, ...), custom_call_target="tpu_custom_call" | custom-call | flops 1 | bytes 1 | tf_op jit(solution)/shard_map/expert/pallas_call | solution.py:207
  35.9 2.0 %collective-permute-start.13 = (bf16[80,1024]{1,0:T(8,128)(2,1)S(1)}, bf16[80,1024]{1,0:T(8,128)(2,1)S(1)}, u32[]{:S(2)}, u32[]{:S(2)}) collective-permute-start(bf16[80,1024]{1,0:T(8,128)(2,1)S(1)} %get-tuple-element.75), channel_id=1, source_target_pairs={{8,4},{9,5},{10,6},{11,7},{12,0},{13,1},{14,2},{15,3},{16,12},{17,... | collective-permute-start | bytes 491528 | tf_op jit(solution)/shard_map/ppermute | solution.py:334
  38.3 1.6 %expert.5 = (bf16[80,1024]{1,0:T(8,128)(2,1)S(1)}, bf16[80,768]{1,0:T(8,128)(2,1)S(1)}, bf16[80,384]{1,0:T(8,128)(2,1)S(1)}) custom-call(bf16[40,2048]{1,0:T(8,128)(2,1)S(1)} %collective-permute-done.8.refs_0_.refs_7_, bf16[40,2048]{1,0:T(8,128)(2,1)S(1)} %collective-permute-done.9.refs_1_.refs_8_, ...), custom_call_target="tpu_custom_call" | custom-call | flops 1 | bytes 1 | tf_op jit(solution)/shard_map/expert/pallas_call | solution.py:207
  39.9 3.4 %collective-permute-start.15 = (bf16[80,1024]{1,0:T(8,128)(2,1)S(1)}, bf16[80,1024]{1,0:T(8,128)(2,1)S(1)}, u32[]{:S(2)}, u32[]{:S(2)}) collective-permute-start(bf16[80,1024]{1,0:T(8,128)(2,1)S(1)} %get-tuple-element.77), channel_id=1, source_target_pairs={{8,6},{9,7},{10,4},{11,5},{12,2},{13,3},{14,0},{15,1},{16,14},{17,... | collective-permute-start | bytes 491528 | tf_op jit(solution)/shard_map/ppermute | solution.py:334
  43.4 4.1 %weight_grads.1 = (bf16[2048,384]{1,0:T(8,128)(2,1)}, bf16[2048,384]{1,0:T(8,128)(2,1)}, bf16[384,2048]{1,0:T(8,128)(2,1)}) custom-call(bf16[40,2048]{1,0:T(8,128)(2,1)S(1)} %get-tuple-element.43.refs_1_.refs_0_, bf16[40,2048]{1,0:T(8,128)(2,1)S(1)} %collective-permute-done.refs_2_.refs_1_, bf16[80,2048]{1,0:T(8,128)(2,1)S(1)} %collective-permute-done.1.refs_3_.refs_2_, ...), custom_call_target="tpu_custom_call" | custom-call | flops 1 | bytes 1 | tf_op jit(solution)/shard_map/weight_grads/pallas_call | solution.py:240
  47.5 0.8 %collective-permute-done.13.refs_5_ = bf16[80,1024]{1,0:T(8,128)(2,1)S(1)} collective-permute-done((bf16[80,1024]{1,0:T(8,128)(2,1)S(1)}, bf16[80,1024]{1,0:T(8,128)(2,1)S(1)}, u32[]{:S(2)}, u32[]{:S(2)}) %collective-permute-start.13) | collective-permute-done | bytes 163872 | tf_op jit(solution)/shard_map/ppermute | solution.py:334
  48.3 1.6 %collective-permute-start.14 = (bf16[40,1024]{1,0:T(8,128)(2,1)S(1)}, bf16[40,1024]{1,0:T(8,128)(2,1)S(1)}, u32[]{:S(2)}, u32[]{:S(2)}) collective-permute-start(bf16[40,1024]{1,0:T(8,128)(2,1)S(1)} %slice.26), channel_id=1, source_target_pairs={{0,1},{1,0},{2,3},{3,2},{4,5},{5,4},{6,7},{7,6},{8,9},{9,8},{10,11... | collective-permute-start | bytes 245768 | tf_op jit(solution)/shard_map/ppermute | solution.py:326
  50.5 4.2 %collective-permute-done.15.refs_7_ = bf16[80,1024]{1,0:T(8,128)(2,1)S(1)} collective-permute-done((bf16[80,1024]{1,0:T(8,128)(2,1)S(1)}, bf16[80,1024]{1,0:T(8,128)(2,1)S(1)}, u32[]{:S(2)}, u32[]{:S(2)}) %collective-permute-start.15) | collective-permute-done | bytes 163872 | tf_op jit(solution)/shard_map/ppermute | solution.py:334
  54.7 1.1 %collective-permute-start.16 = (bf16[40,1024]{1,0:T(8,128)(2,1)S(1)}, bf16[40,1024]{1,0:T(8,128)(2,1)S(1)}, u32[]{:S(2)}, u32[]{:S(2)}) collective-permute-start(bf16[40,1024]{1,0:T(8,128)(2,1)S(1)} %slice.30), channel_id=1, source_target_pairs={{0,1},{1,0},{2,3},{3,2},{4,5},{5,4},{6,7},{7,6},{8,9},{9,8},{10,11... | collective-permute-start | bytes 245768 | tf_op jit(solution)/shard_map/ppermute | solution.py:326
  55.8 0.9 %collective-permute-done.16.refs_8_ = bf16[40,1024]{1,0:T(8,128)(2,1)S(1)} collective-permute-done((bf16[40,1024]{1,0:T(8,128)(2,1)S(1)}, bf16[40,1024]{1,0:T(8,128)(2,1)S(1)}, u32[]{:S(2)}, u32[]{:S(2)}) %collective-permute-start.16) | collective-permute-done | bytes 81952 | tf_op jit(solution)/shard_map/ppermute | solution.py:326
  56.8 1.7 %combine.1 = bf16[256,2048]{1,0:T(8,128)(2,1)} custom-call(bf16[88,1024]{1,0:T(8,128)(2,1)S(1)} %collective-permute-done.3.keys_ref.refs_1_, bf16[256,2048]{1,0:T(8,128)(2,1)S(1)} %collective-permute-done.4.refs_0_, bf16[88,1024]{1,0:T(8,128)(2,1)S(1)} %collective-permute-done.3.keys_ref.refs_1_, bf16[40,1024]{1,0:T(8,128)(2,1)S(1)} %collective-permute-done.11.refs_2_, ...), custom_call_target="tpu_custom_call" | custom-call | flops 1 | bytes 1 | tf_op jit(solution)/shard_map/combine/pallas_call | solution.py:292
  (24 shorter events, 1.4 us)
Async XLA Ops:
  3.2 35.2 %collective-permute-start.4 = (bf16[256,2048]{1,0:T(8,128)(2,1)S(1)}, bf16[256,2048]{1,0:T(8,128)(2,1)S(1)}, u32[]{:S(2)}, u32[]{:S(2)}) collective-permute-start(bf16[256,2048]{1,0:T(8,128)(2,1)S(1)} %get-tuple-element.54), channel_id=1, source_target_pairs={{8,0},{9,1},{10,2},{11,3},{12,4},{13,5},{14,6},{15,7},{16,8},{17,9... | collective-permute-start | bytes 3145736 | tf_op jit(solution)/shard_map/ppermute | solution.py:334
  6.2 13.2 %collective-permute-start.1 = (bf16[80,2048]{1,0:T(8,128)(2,1)S(1)}, bf16[80,2048]{1,0:T(8,128)(2,1)S(1)}, u32[]{:S(2)}, u32[]{:S(2)}) collective-permute-start(bf16[80,2048]{1,0:T(8,128)(2,1)S(1)} %get-tuple-element.45), channel_id=1, source_target_pairs={{0,2},{1,3},{2,0},{3,1},{4,6},{5,7},{6,4},{7,5},{8,10},{9,11},{10,... | collective-permute-start | bytes 983048 | tf_op jit(solution)/shard_map/ppermute | solution.py:326
  6.5 16.2 %collective-permute-start.5 = (bf16[80,2048]{1,0:T(8,128)(2,1)S(1)}, bf16[80,2048]{1,0:T(8,128)(2,1)S(1)}, u32[]{:S(2)}, u32[]{:S(2)}) collective-permute-start(bf16[80,2048]{1,0:T(8,128)(2,1)S(1)} %get-tuple-element.55), channel_id=1, source_target_pairs={{0,4},{1,5},{2,6},{3,7},{4,0},{5,1},{6,2},{7,3},{8,12},{9,13},{10,... | collective-permute-start | bytes 983048 | tf_op jit(solution)/shard_map/ppermute | solution.py:326
  8.8 15.8 %collective-permute-start = (bf16[40,2048]{1,0:T(8,128)(2,1)S(1)}, bf16[40,2048]{1,0:T(8,128)(2,1)S(1)}, u32[]{:S(2)}, u32[]{:S(2)}) collective-permute-start(bf16[40,2048]{1,0:T(8,128)(2,1)S(1)} %get-tuple-element.44), channel_id=1, source_target_pairs={{0,1},{1,0},{2,3},{3,2},{4,5},{5,4},{6,7},{7,6},{8,9},{9,8},{10,11... | collective-permute-start | bytes 491528 | tf_op jit(solution)/shard_map/ppermute | solution.py:326
  19.4 5.3 %collective-permute-start.2 = (bf16[40,2048]{1,0:T(8,128)(2,1)S(1)}, bf16[40,2048]{1,0:T(8,128)(2,1)S(1)}, u32[]{:S(2)}, u32[]{:S(2)}) collective-permute-start(bf16[40,2048]{1,0:T(8,128)(2,1)S(1)} %slice.21), channel_id=1, source_target_pairs={{0,1},{1,0},{2,3},{3,2},{4,5},{5,4},{6,7},{7,6},{8,9},{9,8},{10,11... | collective-permute-start | bytes 491528 | tf_op jit(solution)/shard_map/ppermute | solution.py:326
  21.4 14.5 %collective-permute-start.8 = (bf16[40,2048]{1,0:T(8,128)(2,1)S(1)}, bf16[40,2048]{1,0:T(8,128)(2,1)S(1)}, u32[]{:S(2)}, u32[]{:S(2)}) collective-permute-start(bf16[40,2048]{1,0:T(8,128)(2,1)S(1)} %get-tuple-element.61), channel_id=1, source_target_pairs={{0,6},{1,7},{2,4},{3,5},{4,2},{5,3},{6,0},{7,1},{8,14},{9,15},{10,... | collective-permute-start | bytes 491528 | tf_op jit(solution)/shard_map/ppermute | solution.py:326
  22.7 15.6 %collective-permute-start.9 = (bf16[40,2048]{1,0:T(8,128)(2,1)S(1)}, bf16[40,2048]{1,0:T(8,128)(2,1)S(1)}, u32[]{:S(2)}, u32[]{:S(2)}) collective-permute-start(bf16[40,2048]{1,0:T(8,128)(2,1)S(1)} %get-tuple-element.62), channel_id=1, source_target_pairs={{0,7},{1,6},{2,5},{3,4},{4,3},{5,2},{6,1},{7,0},{8,15},{9,14},{10,... | collective-permute-start | bytes 491528 | tf_op jit(solution)/shard_map/ppermute | solution.py:326
  24.6 4.6 %collective-permute-start.6 = (bf16[24,2048]{1,0:T(8,128)(2,1)S(1)}, bf16[24,2048]{1,0:T(8,128)(2,1)S(1)}, u32[]{:S(2)}, u32[]{:S(2)}) collective-permute-start(bf16[24,2048]{1,0:T(8,128)(2,1)S(1)} %slice.28), channel_id=1, source_target_pairs={{0,1},{1,0},{2,3},{3,2},{4,5},{5,4},{6,7},{7,6},{8,9},{9,8},{10,11... | collective-permute-start | bytes 294920 | tf_op jit(solution)/shard_map/ppermute | solution.py:326
  24.7 2.3 %collective-permute-start.7 = (bf16[16,2048]{1,0:T(8,128)(2,1)S(1)}, bf16[16,2048]{1,0:T(8,128)(2,1)S(1)}, u32[]{:S(2)}, u32[]{:S(2)}) collective-permute-start(bf16[16,2048]{1,0:T(8,128)(2,1)S(1)} %slice.29), channel_id=1, source_target_pairs={{0,1},{1,0},{2,3},{3,2},{4,5},{5,4},{6,7},{7,6},{8,9},{9,8},{10,11... | collective-permute-start | bytes 196616 | tf_op jit(solution)/shard_map/ppermute | solution.py:326
  27.0 16.4 %collective-permute-start.3 = (bf16[88,1024]{1,0:T(8,128)(2,1)S(1)}, bf16[88,1024]{1,0:T(8,128)(2,1)S(1)}, u32[]{:S(2)}, u32[]{:S(2)}) collective-permute-start(bf16[88,1024]{1,0:T(8,128)(2,1)S(1)} %get-tuple-element.53), channel_id=1, source_target_pairs={{8,0},{9,1},{10,2},{11,3},{12,4},{13,5},{14,6},{15,7},{16,8},{17,9... | collective-permute-start | bytes 540680 | tf_op jit(solution)/shard_map/ppermute | solution.py:334
  29.2 14.2 %collective-permute-start.10 = (bf16[88,1024]{1,0:T(8,128)(2,1)S(1)}, bf16[88,1024]{1,0:T(8,128)(2,1)S(1)}, u32[]{:S(2)}, u32[]{:S(2)}) collective-permute-start(bf16[88,1024]{1,0:T(8,128)(2,1)S(1)} %get-tuple-element.67), channel_id=1, source_target_pairs={{8,2},{9,3},{10,0},{11,1},{12,6},{13,7},{14,4},{15,5},{16,10},{17,... | collective-permute-start | bytes 540680 | tf_op jit(solution)/shard_map/ppermute | solution.py:334
  35.9 12.4 %collective-permute-start.13 = (bf16[80,1024]{1,0:T(8,128)(2,1)S(1)}, bf16[80,1024]{1,0:T(8,128)(2,1)S(1)}, u32[]{:S(2)}, u32[]{:S(2)}) collective-permute-start(bf16[80,1024]{1,0:T(8,128)(2,1)S(1)} %get-tuple-element.75), channel_id=1, source_target_pairs={{8,4},{9,5},{10,6},{11,7},{12,0},{13,1},{14,2},{15,3},{16,12},{17,... | collective-permute-start | bytes 491528 | tf_op jit(solution)/shard_map/ppermute | solution.py:334
  39.9 14.8 %collective-permute-start.15 = (bf16[80,1024]{1,0:T(8,128)(2,1)S(1)}, bf16[80,1024]{1,0:T(8,128)(2,1)S(1)}, u32[]{:S(2)}, u32[]{:S(2)}) collective-permute-start(bf16[80,1024]{1,0:T(8,128)(2,1)S(1)} %get-tuple-element.77), channel_id=1, source_target_pairs={{8,6},{9,7},{10,4},{11,5},{12,2},{13,3},{14,0},{15,1},{16,14},{17,... | collective-permute-start | bytes 491528 | tf_op jit(solution)/shard_map/ppermute | solution.py:334
  48.3 7.5 %collective-permute-start.14 = (bf16[40,1024]{1,0:T(8,128)(2,1)S(1)}, bf16[40,1024]{1,0:T(8,128)(2,1)S(1)}, u32[]{:S(2)}, u32[]{:S(2)}) collective-permute-start(bf16[40,1024]{1,0:T(8,128)(2,1)S(1)} %slice.26), channel_id=1, source_target_pairs={{0,1},{1,0},{2,3},{3,2},{4,5},{5,4},{6,7},{7,6},{8,9},{9,8},{10,11... | collective-permute-start | bytes 245768 | tf_op jit(solution)/shard_map/ppermute | solution.py:326
  49.9 5.9 %collective-permute-start.12 = (bf16[40,1024]{1,0:T(8,128)(2,1)S(1)}, bf16[40,1024]{1,0:T(8,128)(2,1)S(1)}, u32[]{:S(2)}, u32[]{:S(2)}) collective-permute-start(bf16[40,1024]{1,0:T(8,128)(2,1)S(1)} %slice.25), channel_id=1, source_target_pairs={{0,1},{1,0},{2,3},{3,2},{4,5},{5,4},{6,7},{7,6},{8,9},{9,8},{10,11... | collective-permute-start | bytes 245768 | tf_op jit(solution)/shard_map/ppermute | solution.py:326
  50.0 5.8 %collective-permute-start.11 = (bf16[40,1024]{1,0:T(8,128)(2,1)S(1)}, bf16[40,1024]{1,0:T(8,128)(2,1)S(1)}, u32[]{:S(2)}, u32[]{:S(2)}) collective-permute-start(bf16[40,1024]{1,0:T(8,128)(2,1)S(1)} %slice.24), channel_id=1, source_target_pairs={{0,1},{1,0},{2,3},{3,2},{4,5},{5,4},{6,7},{7,6},{8,9},{9,8},{10,11... | collective-permute-start | bytes 245768 | tf_op jit(solution)/shard_map/ppermute | solution.py:326
  54.7 2.1 %collective-permute-start.16 = (bf16[40,1024]{1,0:T(8,128)(2,1)S(1)}, bf16[40,1024]{1,0:T(8,128)(2,1)S(1)}, u32[]{:S(2)}, u32[]{:S(2)}) collective-permute-start(bf16[40,1024]{1,0:T(8,128)(2,1)S(1)} %slice.30), channel_id=1, source_target_pairs={{0,1},{1,0},{2,3},{3,2},{4,5},{5,4},{6,7},{7,6},{8,9},{9,8},{10,11... | collective-permute-start | bytes 245768 | tf_op jit(solution)/shard_map/ppermute | solution.py:326
